TPU v7x, 32 devices: a whole 2x2x4 slice. The times are simulated.
32 devices in a mesh: depth: 8 (over y, x, core), plan: 4 (over z).
Axes of the slice: x: 2, y: 2, z: 4, core: 2. Of those that a mesh axis runs over, the one named last changes fastest.
Arguments:
- stress: float32 [6, 64, 64, 256], P(None, 'depth', 'plan'), may hold values from -6 to 6
- velocity: float32 [3, 64, 64, 256], P(None, 'depth', 'plan'), may hold values from -3 to 3
- density: float32 [64, 64, 256], P('depth', 'plan'), may hold values from 1 to 4
- branch_flags: int32 [64, 64, 256], P('depth', 'plan'), may hold values from 0 to 2
- pile_velocity: float32 [3, 49152], P(None, 'depth'), may hold values from -3 to 3
- pile_mass: float32 [49152], P('depth'), may hold values from 0.5 to 2
- jack_force: float32 [3, 49152], P(None, 'depth'), may hold values from -6 to 6
- pair_elem: int32 [8, 8192], P('depth', 'plan'), may hold values from 0 to 18431, as said below
- pair_cell: int32 [8, 8192], P('depth', 'plan'), may hold values from -1 to 32767, as said below
Outputs:
- stress_out: float32 [6, 64, 64, 256], P(None, 'depth', 'plan')
- velocity_out: float32 [3, 64, 64, 256], P(None, 'depth', 'plan')
- pile_velocity_out: float32 [3, 49152], P(None, 'depth')
Inputs may be any that keep to these rules, and one draw needn't show every extreme that they name: `pair_elem`: counted from block d - 1 for depth index d, it names an element of the pile: blocks d - 1, d, d + 1 only, never below block 0 or above the last block. `pair_cell`: live pairs (cell >= 0) of one device are its first slots; at most 2048 on one device; all slots live on every device of one depth index, the tip, which lies above the middle depth index and below the last; fewer live on the depth indices before it, none after it.
All inputs are finite; a program needn't handle non-finite values.
Results may differ from a plain program's by a relative error of at most 0.00016.
Values sent between devices are 32-bit elements; how exact they have to be, the bound alone decides.
No kernel may reach another device: no remote copies, remote signals or barrier semaphores. Data moves between devices by JAX's collectives and lax.ppermute only.
A program may use at most 64 MiB of HBM per device.

v0:
```python
import math

import jax
import jax.numpy as jnp
from jax import lax
from jax.sharding import PartitionSpec as P

STEPS = 3


time_step = 0.2
penalty = 1.0
lame_first = 1.0
shear_modulus = 1.0
cone_rate = 1.5


def extended(block, sides, width):
    for axis, dim in sides:
        count = lax.axis_size(axis)
        forward = [(i, i + 1) for i in range(count - 1)]
        backward = [(target, source) for source, target in forward]
        low = lax.ppermute(
            lax.slice_in_dim(block, block.shape[dim] - width, None, axis=dim), axis, forward
        )
        high = lax.ppermute(lax.slice_in_dim(block, 0, width, axis=dim), axis, backward)
        block = jnp.concatenate([low, block, high], axis=dim)
    return block


def slopes_of(padded):
    along_depth = 0.5 * (padded[:, 2:, 1:-1, 1:-1] - padded[:, :-2, 1:-1, 1:-1])
    along_plan = 0.5 * (padded[:, 1:-1, 2:, 1:-1] - padded[:, 1:-1, :-2, 1:-1])
    along_last = 0.5 * (padded[:, 1:-1, 1:-1, 2:] - padded[:, 1:-1, 1:-1, :-2])
    return (along_depth, along_plan, along_last)


def split_divergence(stress):
    depth_part = jnp.stack([stress[0], stress[3], stress[4]])
    plan_part = jnp.stack([stress[3], stress[1], stress[5]])
    last_part = jnp.pad(
        jnp.stack([stress[4], stress[5], stress[2]]), ((0, 0), (0, 0), (0, 0), (1, 1))
    )
    depth_padded = extended(depth_part, (("depth", 1),), 1)
    plan_padded = extended(plan_part, (("plan", 2),), 1)
    along_depth = 0.5 * (depth_padded[:, 2:] - depth_padded[:, :-2])
    along_plan = 0.5 * (plan_padded[:, :, 2:] - plan_padded[:, :, :-2])
    along_last = 0.5 * (last_part[:, :, :, 2:] - last_part[:, :, :, :-2])
    return along_depth + along_plan + along_last


def strain_rate(padded):
    slopes = slopes_of(padded)
    return jnp.stack(
        [
            slopes[0][0],
            slopes[1][1],
            slopes[2][2],
            0.5 * (slopes[1][0] + slopes[0][1]),
            0.5 * (slopes[2][0] + slopes[0][2]),
            0.5 * (slopes[2][1] + slopes[1][2]),
        ]
    )


def return_map(trial_stress, branch_flags):
    pressure = (trial_stress[0] + trial_stress[1] + trial_stress[2]) / 3.0
    deviator = jnp.stack(
        [
            trial_stress[0] - pressure,
            trial_stress[1] - pressure,
            trial_stress[2] - pressure,
            trial_stress[3],
            trial_stress[4],
            trial_stress[5],
        ]
    )
    second = (
        0.5 * (deviator[0] * deviator[0] + deviator[1] * deviator[1] + deviator[2] * deviator[2])
        + deviator[3] * deviator[3]
        + deviator[4] * deviator[4]
        + deviator[5] * deviator[5]
    )
    shrink = 1.0 / (1.0 + cone_rate * jnp.sqrt(second))
    empty_part = jnp.zeros_like(pressure)
    spherical = jnp.stack([pressure, pressure, pressure, empty_part, empty_part, empty_part])
    cone_stress = deviator * shrink + spherical
    return jnp.where(
        branch_flags == 0, trial_stress, jnp.where(branch_flags == 1, cone_stress, spherical)
    )


def stress_update(stress, padded_velocity, branch_flags):
    strain = strain_rate(padded_velocity)
    increment = 2.0 * shear_modulus * strain
    increment = increment.at[:3].add(lame_first * (strain[0] + strain[1] + strain[2]))
    return return_map(stress + time_step * increment, branch_flags)


def pad_last(field):
    return jnp.pad(field, ((0, 0), (0, 0), (0, 0), (1, 1)))


def selectors(indices, row_count, col_count):
    col_table = (
        (indices % col_count)[None, :] == jnp.arange(col_count, dtype=jnp.int32)[:, None]
    ).astype(jnp.float32)
    row_table = (
        (indices // col_count)[None, :] == jnp.arange(row_count, dtype=jnp.int32)[:, None]
    ).astype(jnp.float32)
    return (col_table, row_table)


def pick_values(table, col_table, row_table):
    row_count = row_table.shape[0]
    columns = jnp.dot(
        table, col_table, precision=lax.Precision.HIGHEST, preferred_element_type=jnp.float32
    )
    columns = columns.reshape(3, row_count, columns.shape[1])
    return jnp.sum(columns * row_table[None], axis=1)


def spread_values(values, col_table, row_table):
    row_count = row_table.shape[0]
    spread = (values[:, None, :] * row_table[None]).reshape(3 * row_count, values.shape[1])
    return lax.dot_general(
        spread,
        col_table,
        (((1,), (1,)), ((), ())),
        precision=lax.Precision.HIGHEST,
        preferred_element_type=jnp.float32,
    )


def contact_terms(flat_velocity, window, cell_index, elem_index, weight, cell_cols, pile_cols):
    cell_rows = flat_velocity.shape[1] // cell_cols
    pile_rows = window.shape[1] // pile_cols
    velocity_table = flat_velocity.reshape(3 * cell_rows, cell_cols)
    pile_table = window.reshape(3 * pile_rows, pile_cols)
    total = cell_index.shape[0]
    block = math.gcd(total, 512)
    blocks = total // block
    cell_blocks = cell_index.reshape(blocks, block)
    elem_blocks = elem_index.reshape(blocks, block)
    weight_blocks = weight.reshape(blocks, block)

    def one_block(carry, items):
        cell_sum, pile_sum = carry
        cell_ids, elem_ids, live = items
        cell_cols_table, cell_rows_table = selectors(cell_ids, cell_rows, cell_cols)
        pile_cols_table, pile_rows_table = selectors(elem_ids, pile_rows, pile_cols)
        at_cells = pick_values(velocity_table, cell_cols_table, cell_rows_table)
        at_pile = pick_values(pile_table, pile_cols_table, pile_rows_table)
        pushes = penalty * (at_pile - at_cells) * live[None, :]
        cell_sum = cell_sum + spread_values(pushes, cell_cols_table, cell_rows_table)
        pile_sum = pile_sum + spread_values(pushes, pile_cols_table, pile_rows_table)
        return ((cell_sum, pile_sum), None)

    start = (
        jnp.zeros((3 * cell_rows, cell_cols), jnp.float32),
        jnp.zeros((3 * pile_rows, pile_cols), jnp.float32),
    )
    (cell_sum, pile_sum), unused = lax.scan(
        one_block, start, (cell_blocks, elem_blocks, weight_blocks)
    )
    return (cell_sum.reshape(3, -1), pile_sum.reshape(3, -1))


def shards(
    stress,
    velocity,
    density,
    branch_flags,
    pile_velocity,
    pile_mass,
    jack_force,
    pair_elem,
    pair_cell,
):
    pile_width = pile_velocity.shape[1]
    cell_cols = velocity.shape[3]
    pile_cols = math.gcd(pile_width, 128)
    weight = (pair_cell >= 0).astype(jnp.float32).reshape(-1)
    cell_index = jnp.maximum(pair_cell, 0).reshape(-1)
    elem_index = pair_elem.reshape(-1)
    for step_number in range(STEPS):
        stress_force = split_divergence(stress)
        window = extended(pile_velocity, (("depth", 1),), pile_width)
        flat_velocity = velocity.reshape(3, -1)
        cell_terms, pile_terms = contact_terms(
            flat_velocity, window, cell_index, elem_index, weight, cell_cols, pile_cols
        )
        on_cells = cell_terms.reshape(velocity.shape)
        partial_value = pile_terms.reshape(3, 3, pile_width)
        summed = lax.psum(partial_value, "plan")
        outgoing = jnp.stack([summed[:, 0], summed[:, 2]], axis=1)
        returned = extended(outgoing, (("depth", 1),), 1)
        on_pile = summed[:, 1] + returned[:, 0] + returned[:, 3]
        velocity = velocity + time_step * (stress_force + on_cells) / density
        pile_velocity = pile_velocity + time_step * (jack_force - on_pile) / pile_mass
        velocity_padded = pad_last(extended(velocity, (("depth", 1), ("plan", 2)), 1))
        stress = stress_update(stress, velocity_padded, branch_flags)
    return (stress, velocity, pile_velocity)


def solution(mesh):
    placed = (
        P(None, "depth", "plan", None),
        P(None, "depth", "plan", None),
        P("depth", "plan", None),
        P("depth", "plan", None),
        P(None, "depth"),
        P("depth"),
        P(None, "depth"),
        P("depth", "plan"),
        P("depth", "plan"),
    )
    return jax.shard_map(
        shards,
        mesh=mesh,
        in_specs=placed,
        out_specs=(
            P(None, "depth", "plan", None),
            P(None, "depth", "plan", None),
            P(None, "depth"),
        ),
        check_vma=False,
    )
```

profile of v0, /device:TPU:0, one launch (start us, length us, event | category | flops | bytes accessed | tf_op | source)
XLA Modules:
  0.0 295.5 jit_solution(5458677164543198721)
XLA Ops:
  7.2 1.4 collective-permute-start.5
  8.7 3.0 %collective-permute-start.4 = (f32[3,6144]{1,0:T(4,128)}, f32[3,6144]{1,0:T(4,128)S(1)}, u32[]{:S(2)}, u32[]{:S(2)}) collective-permute-start(f32[3,6144]{1,0:T(4,128)} %param.25), channel_id=1, source_target_pairs={{0,4},{4,8},{8,12},{12,16},{16,20},{20,24},{24,28},{1,5},{5,9},{9,... | collective-permute-start | bytes 221192 | tf_op jit(solution)/shard_map/ppermute | solution.py:23
  13.6 4.9 %collective-permute-start.3 = (f32[3,8,1,256]{3,2,1,0:T(1,128)}, f32[3,8,1,256]{3,2,1,0:T(1,128)S(1)}, u32[]{:S(2)}, u32[]{:S(2)}) collective-permute-start(f32[3,8,1,256]{3,2,1,0:T(1,128)} %get-tuple-element.689), channel_id=1, source_target_pairs={{0,1},{1,2},{2,3},{4,5},{5,6},{6,7},{8,9},{9,10},{10,11},{12,13},{... | collective-permute-start | bytes 73736 | tf_op jit(solution)/shard_map/ppermute | solution.py:23
  18.6 1.4 collective-permute-start.2
  20.7 3.5 %collective-permute-start.1 = (f32[3,1,16,256]{3,2,1,0:T(8,128)}, f32[3,1,16,256]{3,2,1,0:T(8,128)}, u32[]{:S(2)}, u32[]{:S(2)}) collective-permute-start(f32[3,1,16,256]{3,2,1,0:T(8,128)} %get-tuple-element.687), channel_id=1, source_target_pairs={{0,4},{4,8},{8,12},{12,16},{16,20},{20,24},{24,28},{1,5},{5,9},{9,... | collective-permute-start | bytes 147464 | tf_op jit(solution)/shard_map/ppermute | solution.py:23
  27.4 12.3 %while.51 = (s32[]{:T(128)}, f32[384,256]{1,0:T(8,128)S(1)}, f32[432,128]{1,0:T(8,128)S(1)}, s32[4,512]{1,0:T(4,128)S(1)}, f32[432,128]{1,0:T(8,128)S(1)}, /*ind...) while((s32[]{:T(128)}, f32[384,256]{1,0:T(8,128)S(1)}, ...), condition=%wide.region_3.4_spmd.clone, body=%wide.region_0.3_spmd.clone.sunk | while | flops 1889689600 | bytes 10281088 | solution.py:163
  40.3 1.7 fusion.70
  43.3 3.7 %collective-permute-start.7 = (f32[3,1,16,256]{3,2,1,0:T(8,128)S(1)}, f32[3,1,16,256]{3,2,1,0:T(8,128)S(1)}, u32[]{:S(2)}, u32[]{:S(2)}) collective-permute-start(f32[3,1,16,256]{3,2,1,0:T(8,128)S(1)} %get-tuple-element.685), channel_id=1, source_target_pairs={{0,4},{4,8},{8,12},{12,16},{16,20},{20,24},{24,28},{1,5},{5,9},{9,... | collective-permute-start | bytes 147464 | tf_op jit(solution)/shard_map/ppermute | solution.py:23
  47.9 4.3 %collective-permute-start.9 = (f32[3,10,1,256]{3,2,1,0:T(1,128)S(1)}, f32[3,10,1,256]{3,2,1,0:T(1,128)S(1)}, u32[]{:S(2)}, u32[]{:S(2)}) collective-permute-start(f32[3,10,1,256]{3,2,1,0:T(1,128)S(1)} %get-tuple-element.671), channel_id=1, source_target_pairs={{0,1},{1,2},{2,3},{4,5},{5,6},{6,7},{8,9},{9,10},{10,11},{12,13},{... | collective-permute-start | bytes 92168 | tf_op jit(solution)/shard_map/ppermute | solution.py:23
  54.5 3.5 %collective-permute-done.8 = f32[3,10,1,256]{3,2,1,0:T(1,128)S(1)} collective-permute-done((f32[3,10,1,256]{3,2,1,0:T(1,128)S(1)}, f32[3,10,1,256]{3,2,1,0:T(1,128)S(1)}, u32[]{:S(2)}, u32[]{:S(2)}) %collective-permute-start.8) | collective-permute-done | bytes 30752 | tf_op jit(solution)/shard_map/ppermute | solution.py:26
  63.6 4.2 %collective-permute-start.13 = (f32[3,8,1,256]{3,2,1,0:T(1,128)}, f32[3,8,1,256]{3,2,1,0:T(1,128)}, u32[]{:S(2)}, u32[]{:S(2)}) collective-permute-start(f32[3,8,1,256]{3,2,1,0:T(1,128)} %get-tuple-element.683), channel_id=1, source_target_pairs={{0,1},{1,2},{2,3},{4,5},{5,6},{6,7},{8,9},{9,10},{10,11},{12,13},{... | collective-permute-start | bytes 73736 | tf_op jit(solution)/shard_map/ppermute | solution.py:23
  69.2 27.8 %all-reduce.10.cloned.1.call-done = f32[3,3,6144]{2,1,0:T(4,128)} async-done(((f32[3,3,6144]{2,1,0:T(4,128)}), f32[3,3,6144]{2,1,0:T(4,128)}) %all-reduce.10.cloned.1.call-update) | async-done | bytes 221200 | tf_op jit(solution)/shard_map/psum | solution.py:195
  99.5 3.0 %collective-permute-start.14 = (f32[3,1,6144]{2,1,0:T(1,128)S(1)}, f32[3,1,6144]{2,1,0:T(1,128)S(1)}, u32[]{:S(2)}, u32[]{:S(2)}) collective-permute-start(f32[3,1,6144]{2,1,0:T(1,128)S(1)} %get-tuple-element.694), channel_id=1, source_target_pairs={{0,4},{4,8},{8,12},{12,16},{16,20},{20,24},{24,28},{1,5},{5,9},{9,... | collective-permute-start | bytes 221192 | tf_op jit(solution)/shard_map/ppermute | solution.py:23
  103.1 3.6 %collective-permute-start.11 = (f32[3,1,16,256]{3,2,1,0:T(8,128)}, f32[3,1,16,256]{3,2,1,0:T(8,128)}, u32[]{:S(2)}, u32[]{:S(2)}) collective-permute-start(f32[3,1,16,256]{3,2,1,0:T(8,128)} %get-tuple-element.681), channel_id=1, source_target_pairs={{0,4},{4,8},{8,12},{12,16},{16,20},{20,24},{24,28},{1,5},{5,9},{9,... | collective-permute-start | bytes 147464 | tf_op jit(solution)/shard_map/ppermute | solution.py:23
  109.3 3.0 %collective-permute-start.16 = (f32[3,6144]{1,0:T(4,128)S(1)}, f32[3,6144]{1,0:T(4,128)S(1)}, u32[]{:S(2)}, u32[]{:S(2)}) collective-permute-start(f32[3,6144]{1,0:T(4,128)S(1)} %divide_add_fusion.2), channel_id=1, source_target_pairs={{0,4},{4,8},{8,12},{12,16},{16,20},{20,24},{24,28},{1,5},{5,9},{9,... | collective-permute-start | bytes 221192 | tf_op jit(solution)/shard_map/ppermute | solution.py:23
  113.4 1.5 collective-permute-start.10
  115.1 17.8 %while.52 = (s32[]{:T(128)}, f32[384,256]{1,0:T(8,128)S(1)}, f32[432,128]{1,0:T(8,128)S(1)}, s32[4,512]{1,0:T(4,128)}, f32[432,128]{1,0:T(8,128)S(1)}, /*index=5...) while((s32[]{:T(128)}, f32[384,256]{1,0:T(8,128)S(1)}, ...), condition=%wide.region_8.9_spmd.clone, body=%wide.region_5.8_spmd.clone.sunk | while | flops 1889689600 | bytes 10281088 | solution.py:163
  133.0 2.1 fusion.55
  136.4 4.3 %collective-permute-start.19 = (f32[3,1,16,256]{3,2,1,0:T(8,128)S(1)}, f32[3,1,16,256]{3,2,1,0:T(8,128)S(1)}, u32[]{:S(2)}, u32[]{:S(2)}) collective-permute-start(f32[3,1,16,256]{3,2,1,0:T(8,128)S(1)} %get-tuple-element.679), channel_id=1, source_target_pairs={{0,4},{4,8},{8,12},{12,16},{16,20},{20,24},{24,28},{1,5},{5,9},{9,... | collective-permute-start | bytes 147464 | tf_op jit(solution)/shard_map/ppermute | solution.py:23
  142.9 4.5 %collective-permute-start.21 = (f32[3,10,1,256]{3,2,1,0:T(1,128)S(1)}, f32[3,10,1,256]{3,2,1,0:T(1,128)S(1)}, u32[]{:S(2)}, u32[]{:S(2)}) collective-permute-start(f32[3,10,1,256]{3,2,1,0:T(1,128)S(1)} %get-tuple-element.667), channel_id=1, source_target_pairs={{0,1},{1,2},{2,3},{4,5},{5,6},{6,7},{8,9},{9,10},{10,11},{12,13},{... | collective-permute-start | bytes 92168 | tf_op jit(solution)/shard_map/ppermute | solution.py:23
  153.7 4.8 %collective-permute-start.25 = (f32[3,8,1,256]{3,2,1,0:T(1,128)}, f32[3,8,1,256]{3,2,1,0:T(1,128)}, u32[]{:S(2)}, u32[]{:S(2)}) collective-permute-start(f32[3,8,1,256]{3,2,1,0:T(1,128)} %get-tuple-element.677), channel_id=1, source_target_pairs={{0,1},{1,2},{2,3},{4,5},{5,6},{6,7},{8,9},{9,10},{10,11},{12,13},{... | collective-permute-start | bytes 73736 | tf_op jit(solution)/shard_map/ppermute | solution.py:23
  159.8 29.1 %all-reduce.12.cloned.1.call-done = f32[3,3,6144]{2,0,1:T(4,128)} async-done(((f32[3,3,6144]{2,0,1:T(4,128)}), f32[3,3,6144]{2,0,1:T(4,128)}) %all-reduce.12.cloned.1.call-update) | async-done | bytes 221200 | tf_op jit(solution)/shard_map/psum | solution.py:195
  191.2 3.0 %collective-permute-start.26 = (f32[3,1,6144]{2,0,1:T(4,128)S(1)}, f32[3,1,6144]{2,0,1:T(4,128)S(1)}, u32[]{:S(2)}, u32[]{:S(2)}) collective-permute-start(f32[3,1,6144]{2,0,1:T(4,128)S(1)} %get-tuple-element.692), channel_id=1, source_target_pairs={{0,4},{4,8},{8,12},{12,16},{16,20},{20,24},{24,28},{1,5},{5,9},{9,... | collective-permute-start | bytes 221192 | tf_op jit(solution)/shard_map/ppermute | solution.py:23
  194.9 3.0 %collective-permute-start.23 = (f32[3,1,16,256]{3,2,1,0:T(8,128)}, f32[3,1,16,256]{3,2,1,0:T(8,128)S(1)}, u32[]{:S(2)}, u32[]{:S(2)}) collective-permute-start(f32[3,1,16,256]{3,2,1,0:T(8,128)} %get-tuple-element.675), channel_id=1, source_target_pairs={{0,4},{4,8},{8,12},{12,16},{16,20},{20,24},{24,28},{1,5},{5,9},{9,... | collective-permute-start | bytes 147464 | tf_op jit(solution)/shard_map/ppermute | solution.py:23
  200.3 3.0 %collective-permute-start.28 = (f32[3,6144]{1,0:T(4,128)S(1)}, f32[3,6144]{1,0:T(4,128)S(1)}, u32[]{:S(2)}, u32[]{:S(2)}) collective-permute-start(f32[3,6144]{1,0:T(4,128)S(1)} %divide_add_fusion.1), channel_id=1, source_target_pairs={{0,4},{4,8},{8,12},{12,16},{16,20},{20,24},{24,28},{1,5},{5,9},{9,... | collective-permute-start | bytes 221192 | tf_op jit(solution)/shard_map/ppermute | solution.py:23
  205.9 17.8 %while.53 = (s32[]{:T(128)}, f32[384,256]{1,0:T(8,128)S(1)}, f32[432,128]{1,0:T(8,128)S(1)}, s32[4,512]{1,0:T(4,128)}, f32[432,128]{1,0:T(8,128)S(1)}, /*index=5...) while((s32[]{:T(128)}, f32[384,256]{1,0:T(8,128)S(1)}, ...), condition=%wide.region_13.14_spmd.clone, body=%wide.region_10.13_spmd.clone.sunk | while | flops 1889689600 | bytes 10281088 | solution.py:163
  224.4 1.9 fusion.40
  227.7 4.9 %collective-permute-start.31 = (f32[3,1,16,256]{3,2,1,0:T(8,128)S(1)}, f32[3,1,16,256]{3,2,1,0:T(8,128)S(1)}, u32[]{:S(2)}, u32[]{:S(2)}) collective-permute-start(f32[3,1,16,256]{3,2,1,0:T(8,128)S(1)} %get-tuple-element.673), channel_id=1, source_target_pairs={{0,4},{4,8},{8,12},{12,16},{16,20},{20,24},{24,28},{1,5},{5,9},{9,... | collective-permute-start | bytes 147464 | tf_op jit(solution)/shard_map/ppermute | solution.py:23
  234.8 4.8 %collective-permute-start.33 = (f32[3,10,1,256]{3,2,1,0:T(1,128)S(1)}, f32[3,10,1,256]{3,2,1,0:T(1,128)S(1)}, u32[]{:S(2)}, u32[]{:S(2)}) collective-permute-start(f32[3,10,1,256]{3,2,1,0:T(1,128)S(1)} %get-tuple-element.663), channel_id=1, source_target_pairs={{0,1},{1,2},{2,3},{4,5},{5,6},{6,7},{8,9},{9,10},{10,11},{12,13},{... | collective-permute-start | bytes 92168 | tf_op jit(solution)/shard_map/ppermute | solution.py:23
  243.3 37.5 %all-reduce.14.cloned.1.call-done = f32[3,3,6144]{2,0,1:T(4,128)} async-done(((f32[3,3,6144]{2,0,1:T(4,128)}), f32[3,3,6144]{2,0,1:T(4,128)}) %all-reduce.14.cloned.1.call-update) | async-done | bytes 221200 | tf_op jit(solution)/shard_map/psum | solution.py:195
  283.1 3.0 %collective-permute-start.34 = (f32[3,1,6144]{2,0,1:T(4,128)S(1)}, f32[3,1,6144]{2,0,1:T(4,128)S(1)}, u32[]{:S(2)}, u32[]{:S(2)}) collective-permute-start(f32[3,1,6144]{2,0,1:T(4,128)S(1)} %get-tuple-element.690), channel_id=1, source_target_pairs={{0,4},{4,8},{8,12},{12,16},{16,20},{20,24},{24,28},{1,5},{5,9},{9,... | collective-permute-start | bytes 221192 | tf_op jit(solution)/shard_map/ppermute | solution.py:23
  287.4 1.6 divide_add_fusion
  (446 shorter events, 100.6 us)
Async XLA Ops:
  7.2 89.8 %all-reduce.10.cloned.1.call-start = ((), (), s32[]{:S(2)}) async-start(), calls=%async_computation | async-start | bytes 589824 | tf_op jit(solution)/shard_map/psum | solution.py:195
  7.2 18.6 %collective-permute-start.5 = (f32[3,6144]{1,0:T(4,128)}, f32[3,6144]{1,0:T(4,128)S(1)}, u32[]{:S(2)}, u32[]{:S(2)}) collective-permute-start(f32[3,6144]{1,0:T(4,128)} %param.25), channel_id=1, source_target_pairs={{4,0},{8,4},{12,8},{16,12},{20,16},{24,20},{28,24},{5,1},{9,5},{13... | collective-permute-start | bytes 221192 | tf_op jit(solution)/shard_map/ppermute | solution.py:26
  8.7 18.5 %collective-permute-start.4 = (f32[3,6144]{1,0:T(4,128)}, f32[3,6144]{1,0:T(4,128)S(1)}, u32[]{:S(2)}, u32[]{:S(2)}) collective-permute-start(f32[3,6144]{1,0:T(4,128)} %param.25), channel_id=1, source_target_pairs={{0,4},{4,8},{8,12},{12,16},{16,20},{20,24},{24,28},{1,5},{5,9},{9,... | collective-permute-start | bytes 221192 | tf_op jit(solution)/shard_map/ppermute | solution.py:23
  13.6 26.1 %collective-permute-start.3 = (f32[3,8,1,256]{3,2,1,0:T(1,128)}, f32[3,8,1,256]{3,2,1,0:T(1,128)S(1)}, u32[]{:S(2)}, u32[]{:S(2)}) collective-permute-start(f32[3,8,1,256]{3,2,1,0:T(1,128)} %get-tuple-element.689), channel_id=1, source_target_pairs={{0,1},{1,2},{2,3},{4,5},{5,6},{6,7},{8,9},{9,10},{10,11},{12,13},{... | collective-permute-start | bytes 73736 | tf_op jit(solution)/shard_map/ppermute | solution.py:23
  18.6 21.1 %collective-permute-start.2 = (f32[3,8,1,256]{3,2,1,0:T(1,128)}, f32[3,8,1,256]{3,2,1,0:T(1,128)S(1)}, u32[]{:S(2)}, u32[]{:S(2)}) collective-permute-start(f32[3,8,1,256]{3,2,1,0:T(1,128)} %get-tuple-element.688), channel_id=1, source_target_pairs={{1,0},{2,1},{3,2},{5,4},{6,5},{7,6},{9,8},{10,9},{11,10},{13,12},{... | collective-permute-start | bytes 73736 | tf_op jit(solution)/shard_map/ppermute | solution.py:26
  20.7 19.0 %collective-permute-start.1 = (f32[3,1,16,256]{3,2,1,0:T(8,128)}, f32[3,1,16,256]{3,2,1,0:T(8,128)}, u32[]{:S(2)}, u32[]{:S(2)}) collective-permute-start(f32[3,1,16,256]{3,2,1,0:T(8,128)} %get-tuple-element.687), channel_id=1, source_target_pairs={{0,4},{4,8},{8,12},{12,16},{16,20},{20,24},{24,28},{1,5},{5,9},{9,... | collective-permute-start | bytes 147464 | tf_op jit(solution)/shard_map/ppermute | solution.py:23
  25.8 13.9 %collective-permute-start = (f32[3,1,16,256]{3,2,1,0:T(8,128)}, f32[3,1,16,256]{3,2,1,0:T(8,128)}, u32[]{:S(2)}, u32[]{:S(2)}) collective-permute-start(f32[3,1,16,256]{3,2,1,0:T(8,128)} %get-tuple-element.686), channel_id=1, source_target_pairs={{4,0},{8,4},{12,8},{16,12},{20,16},{24,20},{28,24},{5,1},{9,5},{13... | collective-permute-start | bytes 147464 | tf_op jit(solution)/shard_map/ppermute | solution.py:26
  47.9 6.6 %collective-permute-start.9 = (f32[3,10,1,256]{3,2,1,0:T(1,128)S(1)}, f32[3,10,1,256]{3,2,1,0:T(1,128)S(1)}, u32[]{:S(2)}, u32[]{:S(2)}) collective-permute-start(f32[3,10,1,256]{3,2,1,0:T(1,128)S(1)} %get-tuple-element.671), channel_id=1, source_target_pairs={{0,1},{1,2},{2,3},{4,5},{5,6},{6,7},{8,9},{9,10},{10,11},{12,13},{... | collective-permute-start | bytes 92168 | tf_op jit(solution)/shard_map/ppermute | solution.py:23
  52.2 5.8 %collective-permute-start.8 = (f32[3,10,1,256]{3,2,1,0:T(1,128)S(1)}, f32[3,10,1,256]{3,2,1,0:T(1,128)S(1)}, u32[]{:S(2)}, u32[]{:S(2)}) collective-permute-start(f32[3,10,1,256]{3,2,1,0:T(1,128)S(1)} %get-tuple-element.670), channel_id=1, source_target_pairs={{1,0},{2,1},{3,2},{5,4},{6,5},{7,6},{9,8},{10,9},{11,10},{13,12},{... | collective-permute-start | bytes 92168 | tf_op jit(solution)/shard_map/ppermute | solution.py:26
  54.4 134.6 %all-reduce.12.cloned.1.call-start = ((), (), s32[]{:S(2)}) async-start(), calls=%async_computation.1 | async-start | bytes 589824 | tf_op jit(solution)/shard_map/psum | solution.py:195
  63.6 69.4 %collective-permute-start.13 = (f32[3,8,1,256]{3,2,1,0:T(1,128)}, f32[3,8,1,256]{3,2,1,0:T(1,128)}, u32[]{:S(2)}, u32[]{:S(2)}) collective-permute-start(f32[3,8,1,256]{3,2,1,0:T(1,128)} %get-tuple-element.683), channel_id=1, source_target_pairs={{0,1},{1,2},{2,3},{4,5},{5,6},{6,7},{8,9},{9,10},{10,11},{12,13},{... | collective-permute-start | bytes 73736 | tf_op jit(solution)/shard_map/ppermute | solution.py:23
  67.8 65.2 %collective-permute-start.12 = (f32[3,8,1,256]{3,2,1,0:T(1,128)}, f32[3,8,1,256]{3,2,1,0:T(1,128)}, u32[]{:S(2)}, u32[]{:S(2)}) collective-permute-start(f32[3,8,1,256]{3,2,1,0:T(1,128)} %get-tuple-element.682), channel_id=1, source_target_pairs={{1,0},{2,1},{3,2},{5,4},{6,5},{7,6},{9,8},{10,9},{11,10},{13,12},{... | collective-permute-start | bytes 73736 | tf_op jit(solution)/shard_map/ppermute | solution.py:26
  98.2 8.6 %collective-permute-start.15 = (f32[3,1,6144]{2,1,0:T(1,128)S(1)}, f32[3,1,6144]{2,1,0:T(1,128)S(1)}, u32[]{:S(2)}, u32[]{:S(2)}) collective-permute-start(f32[3,1,6144]{2,1,0:T(1,128)S(1)} %get-tuple-element.695), channel_id=1, source_target_pairs={{4,0},{8,4},{12,8},{16,12},{20,16},{24,20},{28,24},{5,1},{9,5},{13... | collective-permute-start | bytes 221192 | tf_op jit(solution)/shard_map/ppermute | solution.py:26
  99.5 7.3 %collective-permute-start.14 = (f32[3,1,6144]{2,1,0:T(1,128)S(1)}, f32[3,1,6144]{2,1,0:T(1,128)S(1)}, u32[]{:S(2)}, u32[]{:S(2)}) collective-permute-start(f32[3,1,6144]{2,1,0:T(1,128)S(1)} %get-tuple-element.694), channel_id=1, source_target_pairs={{0,4},{4,8},{8,12},{12,16},{16,20},{20,24},{24,28},{1,5},{5,9},{9,... | collective-permute-start | bytes 221192 | tf_op jit(solution)/shard_map/ppermute | solution.py:23
  103.1 29.8 %collective-permute-start.11 = (f32[3,1,16,256]{3,2,1,0:T(8,128)}, f32[3,1,16,256]{3,2,1,0:T(8,128)}, u32[]{:S(2)}, u32[]{:S(2)}) collective-permute-start(f32[3,1,16,256]{3,2,1,0:T(8,128)} %get-tuple-element.681), channel_id=1, source_target_pairs={{0,4},{4,8},{8,12},{12,16},{16,20},{20,24},{24,28},{1,5},{5,9},{9,... | collective-permute-start | bytes 147464 | tf_op jit(solution)/shard_map/ppermute | solution.py:23
  109.3 5.6 %collective-permute-start.16 = (f32[3,6144]{1,0:T(4,128)S(1)}, f32[3,6144]{1,0:T(4,128)S(1)}, u32[]{:S(2)}, u32[]{:S(2)}) collective-permute-start(f32[3,6144]{1,0:T(4,128)S(1)} %divide_add_fusion.2), channel_id=1, source_target_pairs={{0,4},{4,8},{8,12},{12,16},{16,20},{20,24},{24,28},{1,5},{5,9},{9,... | collective-permute-start | bytes 221192 | tf_op jit(solution)/shard_map/ppermute | solution.py:23
  113.4 19.6 %collective-permute-start.10 = (f32[3,1,16,256]{3,2,1,0:T(8,128)}, f32[3,1,16,256]{3,2,1,0:T(8,128)}, u32[]{:S(2)}, u32[]{:S(2)}) collective-permute-start(f32[3,1,16,256]{3,2,1,0:T(8,128)} %get-tuple-element.680), channel_id=1, source_target_pairs={{4,0},{8,4},{12,8},{16,12},{20,16},{24,20},{28,24},{5,1},{9,5},{13... | collective-permute-start | bytes 147464 | tf_op jit(solution)/shard_map/ppermute | solution.py:26
  135.1 5.6 %collective-permute-start.18 = (f32[3,1,16,256]{3,2,1,0:T(8,128)S(1)}, f32[3,1,16,256]{3,2,1,0:T(8,128)S(1)}, u32[]{:S(2)}, u32[]{:S(2)}) collective-permute-start(f32[3,1,16,256]{3,2,1,0:T(8,128)S(1)} %get-tuple-element.678), channel_id=1, source_target_pairs={{4,0},{8,4},{12,8},{16,12},{20,16},{24,20},{28,24},{5,1},{9,5},{13... | collective-permute-start | bytes 147464 | tf_op jit(solution)/shard_map/ppermute | solution.py:26
  141.6 6.9 %collective-permute-start.20 = (f32[3,10,1,256]{3,2,1,0:T(1,128)S(1)}, f32[3,10,1,256]{3,2,1,0:T(1,128)S(1)}, u32[]{:S(2)}, u32[]{:S(2)}) collective-permute-start(f32[3,10,1,256]{3,2,1,0:T(1,128)S(1)} %get-tuple-element.666), channel_id=1, source_target_pairs={{1,0},{2,1},{3,2},{5,4},{6,5},{7,6},{9,8},{10,9},{11,10},{13,12},{... | collective-permute-start | bytes 92168 | tf_op jit(solution)/shard_map/ppermute | solution.py:26
  142.9 6.1 %collective-permute-start.21 = (f32[3,10,1,256]{3,2,1,0:T(1,128)S(1)}, f32[3,10,1,256]{3,2,1,0:T(1,128)S(1)}, u32[]{:S(2)}, u32[]{:S(2)}) collective-permute-start(f32[3,10,1,256]{3,2,1,0:T(1,128)S(1)} %get-tuple-element.667), channel_id=1, source_target_pairs={{0,1},{1,2},{2,3},{4,5},{5,6},{6,7},{8,9},{9,10},{10,11},{12,13},{... | collective-permute-start | bytes 92168 | tf_op jit(solution)/shard_map/ppermute | solution.py:23
  148.5 132.4 %all-reduce.14.cloned.1.call-start = ((), (), s32[]{:S(2)}) async-start(), calls=%async_computation.2 | async-start | bytes 589824 | tf_op jit(solution)/shard_map/psum | solution.py:195
  153.7 70.1 %collective-permute-start.25 = (f32[3,8,1,256]{3,2,1,0:T(1,128)}, f32[3,8,1,256]{3,2,1,0:T(1,128)}, u32[]{:S(2)}, u32[]{:S(2)}) collective-permute-start(f32[3,8,1,256]{3,2,1,0:T(1,128)} %get-tuple-element.677), channel_id=1, source_target_pairs={{0,1},{1,2},{2,3},{4,5},{5,6},{6,7},{8,9},{9,10},{10,11},{12,13},{... | collective-permute-start | bytes 73736 | tf_op jit(solution)/shard_map/ppermute | solution.py:23
  158.5 65.3 %collective-permute-start.24 = (f32[3,8,1,256]{3,2,1,0:T(1,128)}, f32[3,8,1,256]{3,2,1,0:T(1,128)}, u32[]{:S(2)}, u32[]{:S(2)}) collective-permute-start(f32[3,8,1,256]{3,2,1,0:T(1,128)} %get-tuple-element.676), channel_id=1, source_target_pairs={{1,0},{2,1},{3,2},{5,4},{6,5},{7,6},{9,8},{10,9},{11,10},{13,12},{... | collective-permute-start | bytes 73736 | tf_op jit(solution)/shard_map/ppermute | solution.py:26
  189.9 8.0 %collective-permute-start.27 = (f32[3,1,6144]{2,0,1:T(4,128)S(1)}, f32[3,1,6144]{2,0,1:T(4,128)S(1)}, u32[]{:S(2)}, u32[]{:S(2)}) collective-permute-start(f32[3,1,6144]{2,0,1:T(4,128)S(1)} %get-tuple-element.693), channel_id=1, source_target_pairs={{4,0},{8,4},{12,8},{16,12},{20,16},{24,20},{28,24},{5,1},{9,5},{13... | collective-permute-start | bytes 221192 | tf_op jit(solution)/shard_map/ppermute | solution.py:26
  191.2 6.7 %collective-permute-start.26 = (f32[3,1,6144]{2,0,1:T(4,128)S(1)}, f32[3,1,6144]{2,0,1:T(4,128)S(1)}, u32[]{:S(2)}, u32[]{:S(2)}) collective-permute-start(f32[3,1,6144]{2,0,1:T(4,128)S(1)} %get-tuple-element.692), channel_id=1, source_target_pairs={{0,4},{4,8},{8,12},{12,16},{16,20},{20,24},{24,28},{1,5},{5,9},{9,... | collective-permute-start | bytes 221192 | tf_op jit(solution)/shard_map/ppermute | solution.py:23
  194.9 28.8 %collective-permute-start.23 = (f32[3,1,16,256]{3,2,1,0:T(8,128)}, f32[3,1,16,256]{3,2,1,0:T(8,128)S(1)}, u32[]{:S(2)}, u32[]{:S(2)}) collective-permute-start(f32[3,1,16,256]{3,2,1,0:T(8,128)} %get-tuple-element.675), channel_id=1, source_target_pairs={{0,4},{4,8},{8,12},{12,16},{16,20},{20,24},{24,28},{1,5},{5,9},{9,... | collective-permute-start | bytes 147464 | tf_op jit(solution)/shard_map/ppermute | solution.py:23
  204.4 19.4 %collective-permute-start.22 = (f32[3,1,16,256]{3,2,1,0:T(8,128)}, f32[3,1,16,256]{3,2,1,0:T(8,128)S(1)}, u32[]{:S(2)}, u32[]{:S(2)}) collective-permute-start(f32[3,1,16,256]{3,2,1,0:T(8,128)} %get-tuple-element.674), channel_id=1, source_target_pairs={{4,0},{8,4},{12,8},{16,12},{20,16},{24,20},{28,24},{5,1},{9,5},{13... | collective-permute-start | bytes 147464 | tf_op jit(solution)/shard_map/ppermute | solution.py:26
  226.4 6.2 %collective-permute-start.30 = (f32[3,1,16,256]{3,2,1,0:T(8,128)S(1)}, f32[3,1,16,256]{3,2,1,0:T(8,128)S(1)}, u32[]{:S(2)}, u32[]{:S(2)}) collective-permute-start(f32[3,1,16,256]{3,2,1,0:T(8,128)S(1)} %get-tuple-element.672), channel_id=1, source_target_pairs={{4,0},{8,4},{12,8},{16,12},{20,16},{24,20},{28,24},{5,1},{9,5},{13... | collective-permute-start | bytes 147464 | tf_op jit(solution)/shard_map/ppermute | solution.py:26
  227.7 5.7 %collective-permute-start.31 = (f32[3,1,16,256]{3,2,1,0:T(8,128)S(1)}, f32[3,1,16,256]{3,2,1,0:T(8,128)S(1)}, u32[]{:S(2)}, u32[]{:S(2)}) collective-permute-start(f32[3,1,16,256]{3,2,1,0:T(8,128)S(1)} %get-tuple-element.673), channel_id=1, source_target_pairs={{0,4},{4,8},{8,12},{12,16},{16,20},{20,24},{24,28},{1,5},{5,9},{9,... | collective-permute-start | bytes 147464 | tf_op jit(solution)/shard_map/ppermute | solution.py:23
  233.5 7.1 %collective-permute-start.32 = (f32[3,10,1,256]{3,2,1,0:T(1,128)S(1)}, f32[3,10,1,256]{3,2,1,0:T(1,128)S(1)}, u32[]{:S(2)}, u32[]{:S(2)}) collective-permute-start(f32[3,10,1,256]{3,2,1,0:T(1,128)S(1)} %get-tuple-element.662), channel_id=1, source_target_pairs={{1,0},{2,1},{3,2},{5,4},{6,5},{7,6},{9,8},{10,9},{11,10},{13,12},{... | collective-permute-start | bytes 92168 | tf_op jit(solution)/shard_map/ppermute | solution.py:26
  234.8 6.1 %collective-permute-start.33 = (f32[3,10,1,256]{3,2,1,0:T(1,128)S(1)}, f32[3,10,1,256]{3,2,1,0:T(1,128)S(1)}, u32[]{:S(2)}, u32[]{:S(2)}) collective-permute-start(f32[3,10,1,256]{3,2,1,0:T(1,128)S(1)} %get-tuple-element.663), channel_id=1, source_target_pairs={{0,1},{1,2},{2,3},{4,5},{5,6},{6,7},{8,9},{9,10},{10,11},{12,13},{... | collective-permute-start | bytes 92168 | tf_op jit(solution)/shard_map/ppermute | solution.py:23
  281.8 5.6 %collective-permute-start.35 = (f32[3,1,6144]{2,0,1:T(4,128)S(1)}, f32[3,1,6144]{2,0,1:T(4,128)S(1)}, u32[]{:S(2)}, u32[]{:S(2)}) collective-permute-start(f32[3,1,6144]{2,0,1:T(4,128)S(1)} %get-tuple-element.691), channel_id=1, source_target_pairs={{4,0},{8,4},{12,8},{16,12},{20,16},{24,20},{28,24},{5,1},{9,5},{13... | collective-permute-start | bytes 221192 | tf_op jit(solution)/shard_map/ppermute | solution.py:26
  (58 other events, 1131.9 us)
Sparse Core Ops, SparseCore 0:
  54.5 42.4 all-reduce.9
  148.6 40.3 all-reduce.11
  240.7 40.1 all-reduce.13
where the time goes:
time: 300 us; the launch traced here: 296 us
  waiting for transfers between devices  101 us (34%)
  starting transfers between devices  92.5 us (31%)
  other arithmetic  35 us (12%)
  matrix products  28.8 us (10%)
  local copies, waits for them, and re-layouts  21.2 us (7%)
  between operations  15.3 us (5%)
    psum x3, waiting for transfers between devices, shards(): summed = lax.psum(partial_value, 'plan')  94.5 us
    ppermute x18, starting transfers between devices, extended(): lax.ppermute(lax.slice_in_dim(block, block.shape[dim] - width, None, axis...  68.7 us
    ppermute x18, starting transfers between devices, extended(): lax.ppermute(lax.slice_in_dim(block, 0, width, axis=dim), axis, backward)  23.7 us
    dot_general x24, matrix products, spread_values(): lax.dot_general(spread, col_table, (((1,), (1,)), ((), ())), precision=la...  16.1 us
    dot_general x24, matrix products, pick_values(): jnp.dot(table, col_table, precision=lax.Precision.HIGHEST, preferred_elem...  12.7 us
    unnamed x118, local copies, waits for them, and re-layouts  7.36 us
    select_n x12, other arithmetic, selectors(): indices // col_count  6.08 us
  transfers between devices with their start and end apart: 39, of which 9 were waited for; matrix products, arithmetic and copies ran while one was open for 24% of the time, Pallas kernels for 0%

commit v1 on v0

v1 whole, which is shorter than its diff:
```python
import functools

import jax
import jax.numpy as jnp
from jax import lax
from jax.experimental import pallas as pl
from jax.experimental.pallas import tpu as pltpu
from jax.sharding import PartitionSpec as P

STEPS = 3
time_step = 0.2
cone_rate = 1.5
F32, BF16, I32 = jnp.float32, jnp.bfloat16, jnp.int32
COLS = 256
DEPTH_PART = (0, 3, 4)
PLAN_PART = (3, 1, 5)
LAST_PART = (4, 5, 2)


class Sizes:
    def __init__(self, stress, pile_velocity, pair_cell):
        self.cz, self.cx, self.cy = stress.shape[1:]
        self.rows = self.cz * self.cx
        self.pile = pile_velocity.shape[1]
        self.pr = self.pile // COLS
        self.wp = -(-3 * self.pr // 16) * 16
        self.pairs = pair_cell.shape[1]
        self.kn = self.pairs // COLS
        self.nd = lax.axis_size("depth")
        self.np = lax.axis_size("plan")


def partner_b(index, count):
    return jnp.where(
        index % 2 == 0, lax.rem(index + count - 1, count), lax.rem(index + 1, count)
    )


def low_high(index, count, ref_a, ref_b, where):
    a, b = ref_a[where], ref_b[where]
    even = index % 2 == 0
    zero = jnp.zeros_like(a)
    low = jnp.where(index > 0, jnp.where(even, b, a), zero)
    high = jnp.where(index < count - 1, jnp.where(even, a, b), zero)
    return low, high


def split(x):
    high = x.astype(BF16)
    return high, (x - high.astype(F32)).astype(BF16)


def hits(ids, count):
    return lax.broadcasted_iota(I32, (count, ids.shape[1]), 0) == ids


def one_hot(ids, count):
    return jnp.where(hits(ids, count), 1.0, 0.0).astype(BF16)


def gather_chunk(table, row_ids, col_ids, parts, rows):
    pick = one_hot(col_ids, COLS)
    got = jnp.dot(table[0][...], pick, preferred_element_type=F32)
    got = got + jnp.dot(table[1][...], pick, preferred_element_type=F32)
    mask = hits(row_ids, rows)
    return [
        jnp.sum(jnp.where(mask, got[c * rows : (c + 1) * rows], 0.0), axis=0, keepdims=True)
        for c in range(parts)
    ]


def scatter_chunk(values, row_ids, col_ids, rows):
    put = one_hot(col_ids, COLS)
    mask = hits(row_ids, rows)
    total = None
    for piece in zip(*[split(v) for v in values]):
        spread = jnp.concatenate(
            [jnp.where(mask, v.astype(F32), 0.0) for v in piece], axis=0
        ).astype(BF16)
        term = lax.dot_general(
            spread, put, (((1,), (1,)), ((), ())), preferred_element_type=F32
        )
        total = term if total is None else total + term
    return total


def row_of(ref, row):
    return ref[pl.ds(row, 1), :]


def shifted_rows(a, low, high):
    count = a.shape[0]
    row = lax.broadcasted_iota(I32, a.shape, 0)
    up = jnp.where(row == count - 1, high, pltpu.roll(a, count - 1, 0))
    down = jnp.where(row == 0, low, pltpu.roll(a, 1, 0))
    return up - down


def shifted_lanes(a):
    count = a.shape[1]
    lane = lax.broadcasted_iota(I32, a.shape, 1)
    up = jnp.where(lane == count - 1, 0.0, pltpu.roll(a, count - 1, 1))
    down = jnp.where(lane == 0, 0.0, pltpu.roll(a, 1, 1))
    return up - down


def send_edges(sz, depth, plan, parts_d, parts_p, plane, refs):
    to_da, to_db, to_pa, to_pb = refs
    even_d, even_p = depth % 2 == 0, plan % 2 == 0
    cx, cz = sz.cx, sz.cz
    for i, c in enumerate(parts_d):
        first, last = plane(c, 0), plane(c, cz - 1)
        to_da[i * cx : (i + 1) * cx, :] = jnp.where(even_d, last, first)
        to_db[i * cx : (i + 1) * cx, :] = jnp.where(even_d, first, last)
    for i, c in enumerate(parts_p):
        for z in range(cz):
            a = plane(c, z)
            first, last = a[0:1], a[cx - 1 : cx]
            to_pa[i * cz + z : i * cz + z + 1, :] = jnp.where(even_p, last, first)
            to_pb[i * cz + z : i * cz + z + 1, :] = jnp.where(even_p, first, last)


def store_split(sz, source, parts, rows, refs):
    for c in range(parts):
        high, low = split(source(c))
        refs[0][c * rows : (c + 1) * rows, :] = high
        refs[1][c * rows : (c + 1) * rows, :] = low


def gather_cells(sz, table, ids, out):
    def body(j, carry):
        got = gather_chunk(table, row_of(ids, j), row_of(ids, sz.kn + j), 3, sz.rows)
        for c in range(3):
            out[pl.ds(c * sz.kn + j, 1), :] = got[c]
        return carry

    lax.fori_loop(0, sz.kn, body, 0)


def scatter_sets(sz, parts, sets, ids, acc):
    acc[...] = jnp.zeros_like(acc)

    def body(t, carry):
        s, j = t // sz.kn, lax.rem(t, sz.kn)
        one, index = sets.at[s], ids.at[s]
        values = [row_of(one, c * sz.kn + j) for c in range(parts)]
        acc[...] += scatter_chunk(values, row_of(index, j), row_of(index, sz.kn + j), sz.wp)
        return carry

    lax.fori_loop(0, sz.np * sz.kn, body, 0)


def sort_sets(sz, plan, own, got, sets, rows, offset):
    a, b, others = got
    index = [plan, lax.rem(plan + 1 - 2 * (plan % 2) + sz.np, sz.np), partner_b(plan, sz.np)]
    sets[index[1]] = a[offset : offset + rows, :]
    sets[index[2]] = b[offset : offset + rows, :]
    for shift, ref in zip(range(2, sz.np - 1), others):
        sets[lax.rem(plan + sz.np - shift, sz.np)] = ref[...]
    sets[index[0]] = own[...]


def send_sums(sz, depth, parts, acc, to_da, to_db, offset):
    even = depth % 2 == 0
    pr = sz.pr
    for c in range(parts):
        first = acc[c * sz.wp : c * sz.wp + pr, :]
        last = acc[c * sz.wp + 2 * pr : c * sz.wp + 3 * pr, :]
        to_da[offset + c * pr : offset + (c + 1) * pr, :] = jnp.where(even, last, first)
        to_db[offset + c * pr : offset + (c + 1) * pr, :] = jnp.where(even, first, last)


def own_sums(sz, parts, acc, out):
    for c in range(parts):
        out[c * sz.pr : (c + 1) * sz.pr, :] = acc[
            c * sz.wp + sz.pr : c * sz.wp + 2 * sz.pr, :
        ]


def total_sum(sz, depth, c, mine, from_da, from_db, offset):
    rows = slice(offset + c * sz.pr, offset + (c + 1) * sz.pr)
    low, high = low_high(depth, sz.nd, from_da, from_db, (rows, slice(None)))
    return low + mine[c * sz.pr : (c + 1) * sz.pr, :] + high


def moved_pile(sz, c, pile, jack, mass, count, summed):
    rows = slice(c * sz.pr, (c + 1) * sz.pr)
    p = pile[rows, :]
    return p + time_step * (jack[rows, :] - (count * p - summed)) / mass[...]


def first_kernel(
    sz, stress, velocity, pile_in, mass_in, jack_in, elem_in, cell_in,
    to_da, to_db, to_pa, to_pb, to_all, cell_ids, elem_ids, pile, mass, jack,
    high, low,
):
    depth, plan = lax.axis_index("depth"), lax.axis_index("plan")
    kn, pr = sz.kn, sz.pr
    for j in range(kn):
        lanes = slice(j * COLS, (j + 1) * COLS)
        cell, elem = cell_in[:, lanes], elem_in[:, lanes]
        cell_ids[j : j + 1, :] = lax.shift_right_arithmetic(cell, 8)
        cell_ids[kn + j : kn + j + 1, :] = lax.bitwise_and(cell, COLS - 1)
        elem_ids[j : j + 1, :] = lax.shift_right_arithmetic(elem, 8)
        elem_ids[kn + j : kn + j + 1, :] = lax.bitwise_and(elem, COLS - 1)
        to_all[3 * kn + j : 3 * kn + j + 1, :] = jnp.where(cell >= 0, 1.0, 0.0)
        to_all[4 * kn + j : 4 * kn + j + 1, :] = elem.astype(F32)
    for r in range(pr):
        lanes = slice(r * COLS, (r + 1) * COLS)
        for c in range(3):
            pile[c * pr + r : c * pr + r + 1, :] = pile_in[c : c + 1, lanes]
            jack[c * pr + r : c * pr + r + 1, :] = jack_in[c : c + 1, lanes]
        mass[r : r + 1, :] = mass_in[:, lanes]
    store_split(sz, lambda c: velocity[c], 3, sz.rows, (high, low))
    gather_cells(sz, (high, low), cell_ids, to_all)
    head = 3 * sz.cx
    to_da[head:, :] = pile[...]
    to_db[head:, :] = pile[...]
    head = 3 * sz.cz
    to_pa[head:, :] = to_all[...]
    to_pb[head:, :] = to_all[...]
    plane = lambda c, z: stress[c, z * sz.cx : (z + 1) * sz.cx, :]
    send_edges(sz, depth, plan, DEPTH_PART, PLAN_PART, plane, (to_da, to_db, to_pa, to_pb))


def velocity_update(
    sz, depth, plan, stress, velocity, density, from_da, from_db, from_pa, from_pb,
    window_of, at_cells, cell_ids, elem_ids, out, high, low, on_cells,
):
    kn, rows, wp, cx, cz = sz.kn, sz.rows, sz.wp, sz.cx, sz.cz
    pile_high, pile_low = high.at[0 : 3 * wp, :], low.at[0 : 3 * wp, :]
    pad = jnp.zeros((wp - 3 * sz.pr, COLS), F32)
    for c in range(3):
        table = jnp.concatenate(list(window_of(c)) + ([pad] if pad.shape[0] else []), axis=0)
        hi, lo = split(table)
        pile_high[c * wp : (c + 1) * wp, :] = hi
        pile_low[c * wp : (c + 1) * wp, :] = lo
    on_cells[...] = jnp.zeros_like(on_cells)

    def body(j, carry):
        at_pile = gather_chunk(
            (pile_high, pile_low), row_of(elem_ids, j), row_of(elem_ids, kn + j), 3, wp
        )
        push = [at_pile[c] - row_of(at_cells, c * kn + j) for c in range(3)]
        on_cells[...] += scatter_chunk(
            push, row_of(cell_ids, j), row_of(cell_ids, kn + j), rows
        )
        return carry

    lax.fori_loop(0, kn, body, 0)
    plane = lambda c, z: stress[c, z * cx : (z + 1) * cx, :]
    d_low, d_high = low_high(
        depth, sz.nd, from_da, from_db, (slice(0, 3 * cx), slice(None))
    )
    p_low, p_high = low_high(plan, sz.np, from_pa, from_pb, (slice(0, 3 * cz), slice(None)))
    for z in range(cz):
        here = slice(z * cx, (z + 1) * cx)
        scale = time_step / density[here, :]
        for i in range(3):
            ahead = plane(DEPTH_PART[i], z + 1) if z + 1 < cz else d_high[i * cx : (i + 1) * cx]
            behind = plane(DEPTH_PART[i], z - 1) if z > 0 else d_low[i * cx : (i + 1) * cx]
            row = slice(i * cz + z, i * cz + z + 1)
            twice = (
                (ahead - behind)
                + shifted_rows(plane(PLAN_PART[i], z), p_low[row], p_high[row])
                + shifted_lanes(plane(LAST_PART[i], z))
            )
            force = 0.5 * twice + on_cells[i * rows + z * cx : i * rows + (z + 1) * cx, :]
            out[i, here, :] = velocity[i, here, :] + scale * force


def stress_update(
    sz, depth, plan, stress, velocity, flags, from_da, from_db, from_pa, from_pb, out
):
    cx, cz = sz.cx, sz.cz
    plane = lambda c, z: velocity[c, z * cx : (z + 1) * cx, :]
    d_low, d_high = low_high(
        depth, sz.nd, from_da, from_db, (slice(0, 3 * cx), slice(None))
    )
    p_low, p_high = low_high(plan, sz.np, from_pa, from_pb, (slice(0, 3 * cz), slice(None)))
    for z in range(cz):
        here = slice(z * cx, (z + 1) * cx)
        v = [plane(c, z) for c in range(3)]
        along_z, along_x = [], []
        for c in range(3):
            ahead = plane(c, z + 1) if z + 1 < cz else d_high[c * cx : (c + 1) * cx]
            behind = plane(c, z - 1) if z > 0 else d_low[c * cx : (c + 1) * cx]
            along_z.append(ahead - behind)
            row = slice(c * cz + z, c * cz + z + 1)
            along_x.append(shifted_rows(v[c], p_low[row], p_high[row]))
        along_y = [shifted_lanes(v[c]) for c in range(3)]
        normal = [along_z[0], along_x[1], along_y[2]]
        shear = [along_x[0] + along_z[1], along_y[0] + along_z[2], along_y[1] + along_x[2]]
        bulk = (0.5 * time_step) * (normal[0] + normal[1] + normal[2])
        trial = [stress[c, here, :] + (time_step * normal[c] + bulk) for c in range(3)]
        sheared = [
            stress[3 + c, here, :] + (0.5 * time_step) * shear[c] for c in range(3)
        ]
        pressure = (trial[0] + trial[1] + trial[2]) * (1.0 / 3.0)
        dev = [t - pressure for t in trial]
        second = 0.5 * (dev[0] * dev[0] + dev[1] * dev[1] + dev[2] * dev[2])
        for t in sheared:
            second = second + t * t
        shrink = 1.0 / (1.0 + cone_rate * jnp.sqrt(second))
        flag = flags[here, :]
        factor = jnp.where(flag == 1, shrink, 0.0)
        elastic = flag == 0
        for c in range(3):
            out[c, here, :] = jnp.where(elastic, trial[c], dev[c] * factor + pressure)
            out[3 + c, here, :] = jnp.where(elastic, sheared[c], sheared[c] * factor)


def window_from(sz, depth, pile, from_da, from_db, offset):
    def of(c):
        rows = slice(offset + c * sz.pr, offset + (c + 1) * sz.pr)
        low, high = low_high(depth, sz.nd, from_da, from_db, (rows, slice(None)))
        return low, pile[c * sz.pr : (c + 1) * sz.pr, :], high

    return of


def velocity_kernel(sz, step, *refs):
    depth, plan = lax.axis_index("depth"), lax.axis_index("plan")
    refs = list(refs)
    take = lambda n: [refs.pop(0) for _ in range(n)]
    stress, velocity, density, cell_ids, elem_ids, at_cells = take(6)
    from_da, from_db, from_pa, from_pb = take(4)
    others = sz.np - 3 if sz.np > 3 else 0
    head_d, head_p, pr3 = 3 * sz.cx, 3 * sz.cz, 3 * sz.pr
    if step == 0:
        from_others = take(others)
        (pile,) = take(1)
        out, to_da, to_db, to_pa, to_pb, to_all, set_ids, mine = take(8)
        high, low, on_cells, sets, acc = take(5)
        window_of = window_from(sz, depth, pile, from_da, from_db, head_d)
    elif step == 1:
        pile, mass, jack, count, mine = take(5)
        out, to_da, to_db, to_pa, to_pb, to_all, new_pile = take(7)
        high, low, on_cells = take(3)
        window_of = window_from(sz, depth, pile, from_da, from_db, head_d)
    else:
        pile, mass, jack, count, mine, pile_da, pile_db = take(7)
        out, to_da, to_db, to_pa, to_pb, pile_out = take(6)
        high, low, on_cells, new_pile = take(4)
        window_of = window_from(sz, depth, pile, pile_da, pile_db, head_d)
    velocity_update(
        sz, depth, plan, stress, velocity, density, from_da, from_db, from_pa, from_pb,
        window_of, at_cells, cell_ids, elem_ids, out, high, low, on_cells,
    )
    if step < 2:
        store_split(sz, lambda c: out[c], 3, sz.rows, (high, low))
        gather_cells(sz, (high, low), cell_ids, to_all)
        to_pa[head_p:, :] = to_all[...]
        to_pb[head_p:, :] = to_all[...]
    if step == 0:
        kn = sz.kn
        sort_sets(sz, plan, at_cells, (from_pa, from_pb, from_others), sets, 5 * kn, head_p)
        for s in range(sz.np):
            elem = sets[s, 4 * kn : 5 * kn, :].astype(I32)
            set_ids[s, 0:kn, :] = lax.shift_right_arithmetic(elem, 8)
            set_ids[s, kn : 2 * kn, :] = lax.bitwise_and(elem, COLS - 1)
        scatter_sets(sz, 4, sets, set_ids, acc)
        send_sums(sz, depth, 4, acc, to_da, to_db, head_d)
        own_sums(sz, 4, acc, mine)
    else:
        offset = head_d + (pr3 if step == 1 else 0)
        for c in range(3):
            summed = total_sum(sz, depth, c, mine, from_da, from_db, offset)
            new_pile[c * sz.pr : (c + 1) * sz.pr, :] = moved_pile(
                sz, c, pile, jack, mass, count[...], summed
            )
        if step == 1:
            to_da[head_d:, :] = new_pile[...]
            to_db[head_d:, :] = new_pile[...]
        else:
            for r in range(sz.pr):
                for c in range(3):
                    pile_out[c : c + 1, r * COLS : (r + 1) * COLS] = new_pile[
                        c * sz.pr + r : c * sz.pr + r + 1, :
                    ]
    plane = lambda c, z: out[c, z * sz.cx : (z + 1) * sz.cx, :]
    send_edges(sz, depth, plan, (0, 1, 2), (0, 1, 2), plane, (to_da, to_db, to_pa, to_pb))


def stress_kernel(sz, step, *refs):
    depth, plan = lax.axis_index("depth"), lax.axis_index("plan")
    refs = list(refs)
    take = lambda n: [refs.pop(0) for _ in range(n)]
    stress, velocity, flags, from_da, from_db, from_pa, from_pb = take(7)
    head_d, head_p, pr3 = 3 * sz.cx, 3 * sz.cz, 3 * sz.pr
    if step == STEPS - 1:
        (out,) = take(1)
        stress_update(
            sz, depth, plan, stress, velocity, flags, from_da, from_db, from_pa, from_pb, out
        )
        return
    from_others = take(max(sz.np - 3, 0))
    own, set_ids = take(2)
    if step == 0:
        pile, mass, jack, mine_before = take(4)
        out, to_da, to_db, to_pa, to_pb, mine, new_pile, count = take(8)
    else:
        out, to_da, to_db, to_pa, to_pb, mine = take(6)
    sets, acc = take(2)
    stress_update(
        sz, depth, plan, stress, velocity, flags, from_da, from_db, from_pa, from_pb, out
    )
    sort_sets(sz, plan, own, (from_pa, from_pb, from_others), sets, 3 * sz.kn, head_p)
    scatter_sets(sz, 3, sets, set_ids, acc)
    own_sums(sz, 3, acc, mine)
    offset = head_d
    if step == 0:
        count[...] = total_sum(sz, depth, 3, mine_before, from_da, from_db, head_d)
        for c in range(3):
            summed = total_sum(sz, depth, c, mine_before, from_da, from_db, head_d)
            new_pile[c * sz.pr : (c + 1) * sz.pr, :] = moved_pile(
                sz, c, pile, jack, mass, count[...], summed
            )
        to_da[offset : offset + pr3, :] = new_pile[...]
        to_db[offset : offset + pr3, :] = new_pile[...]
        offset += pr3
    send_sums(sz, depth, 3, acc, to_da, to_db, offset)
    plane = lambda c, z: out[c, z * sz.cx : (z + 1) * sz.cx, :]
    send_edges(sz, depth, plan, DEPTH_PART, PLAN_PART, plane, (to_da, to_db, to_pa, to_pb))


def call(body, name, ins, outs, scratch=()):
    vmem = pl.BlockSpec(memory_space=pltpu.VMEM)
    return pl.pallas_call(
        body,
        out_shape=[jax.ShapeDtypeStruct(shape, dtype) for shape, dtype in outs],
        in_specs=[vmem] * len(ins),
        out_specs=[vmem] * len(outs),
        scratch_shapes=[pltpu.VMEM(shape, dtype) for shape, dtype in scratch],
        compiler_params=pltpu.CompilerParams(vmem_limit_bytes=48 * 2**20),
        name=name,
    )(*ins)


def matchings(count):
    first = [(i, i ^ 1) for i in range(count)]
    second = [(i, (i - 1) % count if i % 2 == 0 else (i + 1) % count) for i in range(count)]
    return first, second


def shards(
    stress, velocity, density, flags, pile_velocity, pile_mass, jack_force, pair_elem, pair_cell
):
    sz = Sizes(stress, pile_velocity, pair_cell)
    cz, cx, cy, rows, kn, pr = sz.cz, sz.cx, sz.cy, sz.rows, sz.kn, sz.pr
    assert cy == COLS and sz.pile % COLS == 0 and sz.pairs % COLS == 0
    assert sz.nd % 2 == 0 and sz.np % 2 == 0
    d_first, d_second = matchings(sz.nd)
    p_first, p_second = matchings(sz.np)

    def swap(da, db, pa, pb):
        pb = lax.ppermute(pb, "plan", p_second)
        pa = lax.ppermute(pa, "plan", p_first)
        db = lax.ppermute(db, "depth", d_second)
        da = lax.ppermute(da, "depth", d_first)
        return [da, db, pa, pb]

    def to_others(x):
        shifts = range(2, sz.np - 1)
        return [
            lax.ppermute(x, "plan", [(i, (i + s) % sz.np) for i in range(sz.np)]) for s in shifts
        ]

    full_shape = stress.shape, velocity.shape
    stress = stress.reshape(6, rows, cy)
    velocity = velocity.reshape(3, rows, cy)
    density = density.reshape(rows, cy)
    flags = flags.reshape(rows, cy)
    head_d, head_p, pr3, wp = 3 * cx, 3 * cz, 3 * pr, sz.wp
    big = max(3 * rows, 3 * wp)
    tables = [((big, COLS), BF16)] * 2
    cells = [((3 * rows, COLS), F32)]

    def edges(extra_d, extra_p):
        return [((head_d + extra_d, COLS), F32)] * 2 + [((head_p + extra_p, COLS), F32)] * 2

    to = call(
        functools.partial(first_kernel, sz),
        "first",
        [
            stress, velocity, pile_velocity, pile_mass.reshape(1, -1), jack_force, pair_elem,
            pair_cell,
        ],
        edges(pr3, 5 * kn)
        + [
            ((5 * kn, COLS), F32), ((2 * kn, COLS), I32), ((2 * kn, COLS), I32),
            ((pr3, COLS), F32), ((pr, COLS), F32), ((pr3, COLS), F32),
        ],
        tables,
    )
    at_cells, cell_ids, elem_ids, pile, mass, jack = to[4:]
    others = to_others(at_cells)
    got = swap(*to[:4])

    first = call(
        functools.partial(velocity_kernel, sz, 0),
        "velocity_0",
        [stress, velocity, density, cell_ids, elem_ids, at_cells, *got, *others, pile],
        [((3, rows, cy), F32)]
        + edges(4 * pr, 3 * kn)
        + [((3 * kn, COLS), F32), ((sz.np, 2 * kn, COLS), I32), ((4 * pr, COLS), F32)],
        tables
        + cells
        + [((sz.np, 5 * kn, COLS), F32), ((4 * wp, COLS), F32)],
    )
    velocity, (at_cells, set_ids, mine) = first[0], first[5:]
    others = to_others(at_cells)
    got = swap(*first[1:5])
    second = call(
        functools.partial(stress_kernel, sz, 0),
        "stress_0",
        [stress, velocity, flags, *got, *others, at_cells, set_ids, pile, mass, jack, mine],
        [((6, rows, cy), F32)]
        + edges(2 * pr3, 0)
        + [((pr3, COLS), F32), ((pr3, COLS), F32), ((pr, COLS), F32)],
        [((sz.np, 3 * kn, COLS), F32), ((3 * wp, COLS), F32)],
    )
    stress, (mine, pile, count) = second[0], second[5:]
    got = swap(*second[1:5])

    first = call(
        functools.partial(velocity_kernel, sz, 1),
        "velocity_1",
        [
            stress, velocity, density, cell_ids, elem_ids, at_cells, *got, pile, mass, jack,
            count, mine,
        ],
        [((3, rows, cy), F32)]
        + edges(pr3, 3 * kn)
        + [((3 * kn, COLS), F32), ((pr3, COLS), F32)],
        tables + cells,
    )
    velocity, (at_cells, pile) = first[0], first[5:]
    others = to_others(at_cells)
    got = swap(*first[1:5])
    pile_da, pile_db = got[0], got[1]
    second = call(
        functools.partial(stress_kernel, sz, 1),
        "stress_1",
        [stress, velocity, flags, *got, *others, at_cells, set_ids],
        [((6, rows, cy), F32)] + edges(pr3, 0) + [((pr3, COLS), F32)],
        [((sz.np, 3 * kn, COLS), F32), ((3 * wp, COLS), F32)],
    )
    stress, mine = second[0], second[5]
    got = swap(*second[1:5])

    first = call(
        functools.partial(velocity_kernel, sz, 2),
        "velocity_2",
        [
            stress, velocity, density, cell_ids, elem_ids, at_cells, *got, pile, mass, jack,
            count, mine, pile_da, pile_db,
        ],
        [((3, rows, cy), F32)] + edges(0, 0) + [(pile_velocity.shape, F32)],
        tables + cells + [((pr3, COLS), F32)],
    )
    velocity, pile_velocity = first[0], first[5]
    got = swap(*first[1:5])
    (stress,) = call(
        functools.partial(stress_kernel, sz, 2),
        "stress_2",
        [stress, velocity, flags, *got],
        [((6, rows, cy), F32)],
    )
    return stress.reshape(full_shape[0]), velocity.reshape(full_shape[1]), pile_velocity


def solution(mesh):
    cells, field = P("depth", "plan", None), P(None, "depth", "plan", None)
    pile, pairs = P(None, "depth"), P("depth", "plan")
    return jax.shard_map(
        shards,
        mesh=mesh,
        in_specs=(field, field, cells, cells, pile, P("depth"), pile, pairs, pairs),
        out_specs=(field, field, pile),
        check_vma=False,
    )
```

time: 300 us -> 112 us (0.37); the launches traced: 296 us -> 112 us
  waiting for transfers between devices: 101 us -> 23.6 us
  starting transfers between devices: 92.5 us -> 29.4 us
  Pallas kernels: 0 us -> 51.1 us
  other arithmetic: 35 us -> 0 us
  matrix products: 28.8 us -> 0 us
  between operations: 15.3 us -> 0.8 us
  local copies, waits for them, and re-layouts: 21.2 us -> 7.04 us
    psum x3 -> x0, waiting for transfers between devices: 94.5 us -> none  [shards(): summed = lax.psum(partial_value, 'plan')]
    ppermute x36 -> x27, starting transfers between devices: 92.3 us -> 29.4 us  [the longest x6 12.4 us: swap(): pb = lax.ppermute(pb, 'plan', p_second)]
    pallas_call x0 -> x7, Pallas kernels: none -> 51.1 us  [call(): pl.pallas_call(body, out_shape=[jax.ShapeDtypeStruct(shape, dtype) for sh...]
    dot_general x48 -> x0, matrix products: 28.8 us -> none  [the longest x24 16.1 us: spread_values(): lax.dot_general(spread, col_table, (((1,), (1,)), ((), ())), precision=la...]
    ppermute x36 -> x27, waiting for transfers between devices: 6.93 us -> 23.6 us  [the longest x3 12.2 us: to_others(): lax.ppermute(x, 'plan', [(i, (i + s) % sz.np) for i in range(sz.np)])]
    add x13 -> x0, other arithmetic: 10.1 us -> none  [the longest x3 5.66 us: shards(): velocity = velocity + time_step * (stress_force + on_cells) / density]
    select_n x39 -> x0, other arithmetic: 7.99 us -> none  [the longest x12 6.08 us: selectors(): indices // col_count]
    dynamic_slice x12 -> x0, local copies, waits for them, and re-layouts: 5.71 us -> none  [contact_terms(): lax.scan(one_block, start, (cell_blocks, elem_blocks, weight_blocks))]
  transfers between devices with their start and end apart: 39 -> 27, of which waited for: 9 -> 9; matrix products, arithmetic and copies ran while one was open for 24% -> 0% of each run, Pallas kernels for 0% -> 0%
where the time goes in v1:
time: 112 us
  Pallas kernels  51.1 us (46%)
  starting transfers between devices  29.4 us (26%)
  waiting for transfers between devices  23.6 us (21%)
  local copies, waits for them, and re-layouts  7.04 us (6%)
    pallas_call x7, Pallas kernels, call(): pl.pallas_call(body, out_shape=[jax.ShapeDtypeStruct(shape, dtype) for sh...  51.1 us
    ppermute x6, starting transfers between devices, swap(): pb = lax.ppermute(pb, 'plan', p_second)  12.4 us
    ppermute x3, waiting for transfers between devices, to_others(): lax.ppermute(x, 'plan', [(i, (i + s) % sz.np) for i in range(sz.np)])  12.2 us
    ppermute x6, starting transfers between devices, swap(): db = lax.ppermute(db, 'depth', d_second)  10.6 us
    unnamed x20, local copies, waits for them, and re-layouts  7.04 us
    ppermute x6, waiting for transfers between devices, swap(): pb = lax.ppermute(pb, 'plan', p_second)  6.61 us
    ppermute x6, waiting for transfers between devices, swap(): pa = lax.ppermute(pa, 'plan', p_first)  4.76 us
    ppermute x6, starting transfers between devices, swap(): pa = lax.ppermute(pa, 'plan', p_first)  2.88 us
  transfers between devices with their start and end apart: 27, of which 9 were waited for; matrix products, arithmetic and copies ran while one was open for 0% of the time, Pallas kernels for 0%

profile of v1, /device:TPU:0, one launch (start us, length us, event | category | flops | bytes accessed | tf_op | source)
XLA Modules:
  0.0 111.9 jit_solution(8921358396095341065)
XLA Ops:
  0.6 1.1 %copy-done = f32[6,8,16,256]{3,2,1,0:T(8,128)S(1)} copy-done((f32[6,8,16,256]{3,2,1,0:T(8,128)S(1)}, f32[6,8,16,256]{3,2,1,0:T(8,128)}, u32[]{:S(2)}) %copy-start) | copy-done | bytes 786456
  1.8 1.0 copy-done.1
  6.7 2.4 %first.1 = (f32[120,256]{1,0:T(8,128)S(1)}, f32[120,256]{1,0:T(8,128)S(1)}, f32[64,256]{1,0:T(8,128)S(1)}, f32[64,256]{1,0:T(8,128)S(1)}, f32[40,256]{1,0:T(8,12...) custom-call(f32[6,128,256]{2,1,0:T(8,128)S(1)} %bitcast.7, ...), custom_call_target="tpu_custom_call" | custom-call | tf_op jit(solution)/shard_map/first/pallas_call | solution.py:429
  9.7 3.5 %collective-permute-start.1 = (f32[120,256]{1,0:T(8,128)S(1)}, f32[120,256]{1,0:T(8,128)S(1)}, u32[]{:S(2)}, u32[]{:S(2)}) collective-permute-start(f32[120,256]{1,0:T(8,128)S(1)} %get-tuple-element.52), channel_id=1, source_target_pairs={{0,28},{4,8},{8,4},{12,16},{16,12},{20,24},{24,20},{28,0},{1,29},{... | collective-permute-start | bytes 368648 | tf_op jit(solution)/shard_map/ppermute | solution.py:459
  13.2 1.6 %collective-permute-start.2 = (f32[64,256]{1,0:T(8,128)S(1)}, f32[64,256]{1,0:T(8,128)S(1)}, u32[]{:S(2)}, u32[]{:S(2)}) collective-permute-start(f32[64,256]{1,0:T(8,128)S(1)} %get-tuple-element.53), channel_id=1, source_target_pairs={{0,1},{1,0},{2,3},{3,2},{4,5},{5,4},{6,7},{7,6},{8,9},{9,8},{10,11... | collective-permute-start | bytes 196616 | tf_op jit(solution)/shard_map/ppermute | solution.py:458
  14.8 2.5 %collective-permute-start.3 = (f32[64,256]{1,0:T(8,128)S(1)}, f32[64,256]{1,0:T(8,128)S(1)}, u32[]{:S(2)}, u32[]{:S(2)}) collective-permute-start(f32[64,256]{1,0:T(8,128)S(1)} %get-tuple-element.54), channel_id=1, source_target_pairs={{0,3},{1,2},{2,1},{3,0},{4,7},{5,6},{6,5},{7,4},{8,11},{9,10},{10,... | collective-permute-start | bytes 196616 | tf_op jit(solution)/shard_map/ppermute | solution.py:457
  17.4 5.2 %collective-permute-done.4.refs_10_ = f32[40,256]{1,0:T(8,128)S(1)} collective-permute-done((f32[40,256]{1,0:T(8,128)S(1)}, f32[40,256]{1,0:T(8,128)S(1)}, u32[]{:S(2)}, u32[]{:S(2)}) %collective-permute-start.4) | collective-permute-done | bytes 40992 | tf_op jit(solution)/shard_map/ppermute | solution.py:466
  22.6 16.3 %velocity_0.1 = (f32[3,128,256]{2,1,0:T(8,128)S(1)}, f32[144,256]{1,0:T(8,128)S(1)}, f32[144,256]{1,0:T(8,128)S(1)}, f32[48,256]{1,0:T(8,128)S(1)}, f32[48,256]{...) custom-call(f32[6,128,256]{2,1,0:T(8,128)S(1)} %bitcast.8, ...), custom_call_target="tpu_custom_call" | custom-call | tf_op jit(solution)/shard_map/velocity_0/pallas_call | solution.py:429
  39.9 2.5 %collective-permute-start.8 = (f32[48,256]{1,0:T(8,128)S(1)}, f32[48,256]{1,0:T(8,128)S(1)}, u32[]{:S(2)}, u32[]{:S(2)}) collective-permute-start(f32[48,256]{1,0:T(8,128)S(1)} %get-tuple-element.60), channel_id=1, source_target_pairs={{0,3},{1,2},{2,1},{3,0},{4,7},{5,6},{6,5},{7,4},{8,11},{9,10},{10,... | collective-permute-start | bytes 147464 | tf_op jit(solution)/shard_map/ppermute | solution.py:457
  43.3 3.8 %collective-permute-done.9.refs_7_ = f32[24,256]{1,0:T(8,128)S(1)} collective-permute-done((f32[24,256]{1,0:T(8,128)S(1)}, f32[24,256]{1,0:T(8,128)S(1)}, u32[]{:S(2)}, u32[]{:S(2)}) %collective-permute-start.9) | collective-permute-done | bytes 24608 | tf_op jit(solution)/shard_map/ppermute | solution.py:466
  47.2 9.3 %stress_0.1 = (f32[6,128,256]{2,1,0:T(8,128)S(1)}, f32[192,256]{1,0:T(8,128)S(1)}, f32[192,256]{1,0:T(8,128)S(1)}, f32[24,256]{1,0:T(8,128)S(1)}, f32[24,256]{1,...) custom-call(f32[6,128,256]{2,1,0:T(8,128)S(1)} %bitcast.9, ...), custom_call_target="tpu_custom_call" | custom-call | tf_op jit(solution)/shard_map/stress_0/pallas_call | solution.py:429
  56.5 1.7 %collective-permute-start.11 = (f32[192,256]{1,0:T(8,128)S(1)}, f32[192,256]{1,0:T(8,128)S(1)}, u32[]{:S(2)}, u32[]{:S(2)}) collective-permute-start(f32[192,256]{1,0:T(8,128)S(1)} %get-tuple-element.68), channel_id=1, source_target_pairs={{0,28},{4,8},{8,4},{12,16},{16,12},{20,24},{24,20},{28,0},{1,29},{... | collective-permute-start | bytes 589832 | tf_op jit(solution)/shard_map/ppermute | solution.py:459
  58.3 0.9 collective-permute-start.12
  59.2 1.6 %collective-permute-start.13 = (f32[24,256]{1,0:T(8,128)S(1)}, f32[24,256]{1,0:T(8,128)S(1)}, u32[]{:S(2)}, u32[]{:S(2)}) collective-permute-start(f32[24,256]{1,0:T(8,128)S(1)} %get-tuple-element.70), channel_id=1, source_target_pairs={{0,3},{1,2},{2,1},{3,0},{4,7},{5,6},{6,5},{7,4},{8,11},{9,10},{10,... | collective-permute-start | bytes 73736 | tf_op jit(solution)/shard_map/ppermute | solution.py:457
  60.8 1.3 %collective-permute-done.12.refs_8_ = f32[24,256]{1,0:T(8,128)S(1)} collective-permute-done((f32[24,256]{1,0:T(8,128)S(1)}, f32[24,256]{1,0:T(8,128)S(1)}, u32[]{:S(2)}, u32[]{:S(2)}) %collective-permute-start.12) | collective-permute-done | bytes 24608 | tf_op jit(solution)/shard_map/ppermute | solution.py:458
  62.1 2.7 %collective-permute-done.13.refs_9_ = f32[24,256]{1,0:T(8,128)S(1)} collective-permute-done((f32[24,256]{1,0:T(8,128)S(1)}, f32[24,256]{1,0:T(8,128)S(1)}, u32[]{:S(2)}, u32[]{:S(2)}) %collective-permute-start.13) | collective-permute-done | bytes 24608 | tf_op jit(solution)/shard_map/ppermute | solution.py:457
  64.9 7.0 %velocity_1.1 = (f32[3,128,256]{2,1,0:T(8,128)S(1)}, f32[120,256]{1,0:T(8,128)S(1)}, f32[120,256]{1,0:T(8,128)S(1)}, f32[48,256]{1,0:T(8,128)S(1)}, f32[48,256]{...) custom-call(f32[6,128,256]{2,1,0:T(8,128)S(1)} %get-tuple-element.66.refs_0_, ...), custom_call_target="tpu_custom_call" | custom-call | tf_op jit(solution)/shard_map/velocity_1/pallas_call | solution.py:429
  72.0 1.5 %collective-permute-start.15 = (f32[120,256]{1,0:T(8,128)S(1)}, f32[120,256]{1,0:T(8,128)S(1)}, u32[]{:S(2)}, u32[]{:S(2)}) collective-permute-start(f32[120,256]{1,0:T(8,128)S(1)} %get-tuple-element.76), channel_id=1, source_target_pairs={{0,28},{4,8},{8,4},{12,16},{16,12},{20,24},{24,20},{28,0},{1,29},{... | collective-permute-start | bytes 368648 | tf_op jit(solution)/shard_map/ppermute | solution.py:459
  73.4 1.9 %collective-permute-start.17 = (f32[48,256]{1,0:T(8,128)S(1)}, f32[48,256]{1,0:T(8,128)S(1)}, u32[]{:S(2)}, u32[]{:S(2)}) collective-permute-start(f32[48,256]{1,0:T(8,128)S(1)} %get-tuple-element.78), channel_id=1, source_target_pairs={{0,3},{1,2},{2,1},{3,0},{4,7},{5,6},{6,5},{7,4},{8,11},{9,10},{10,... | collective-permute-start | bytes 147464 | tf_op jit(solution)/shard_map/ppermute | solution.py:457
  75.3 1.6 %collective-permute-start.18 = (f32[24,256]{1,0:T(8,128)S(1)}, f32[24,256]{1,0:T(8,128)S(1)}, u32[]{:S(2)}, u32[]{:S(2)}) collective-permute-start(f32[24,256]{1,0:T(8,128)S(1)} %get-tuple-element.79.refs_8_.refs_5_), channel_id=1, source_target_pairs={{0,2},{1,3},{2,0},{3,1},{4,6},{5,7},{6,4},{7,5},{8,10},{9,11},{10,... | collective-permute-start | bytes 73736 | tf_op jit(solution)/shard_map/ppermute | solution.py:466
  76.9 3.1 %collective-permute-done.18.refs_7_ = f32[24,256]{1,0:T(8,128)S(1)} collective-permute-done((f32[24,256]{1,0:T(8,128)S(1)}, f32[24,256]{1,0:T(8,128)S(1)}, u32[]{:S(2)}, u32[]{:S(2)}) %collective-permute-start.18) | collective-permute-done | bytes 24608 | tf_op jit(solution)/shard_map/ppermute | solution.py:466
  80.1 9.2 %stress_1.1 = (f32[6,128,256]{2,1,0:T(8,128)S(1)}, f32[120,256]{1,0:T(8,128)S(1)}, f32[120,256]{1,0:T(8,128)S(1)}, f32[24,256]{1,0:T(8,128)S(1)}, f32[24,256]{1,0:T(8,128)S(1)}, /*index=5*/f32[72,256]{1,0:T(8,128)S(1)}) custom-call(f32[6,128,256]{2,1,0:T(8,128)S(1)} %get-tuple-element.66.refs_0_, f32[3,128,256]{2,1,0:T(8,128)S(1)} %get-tuple-element.74.refs_1_, ...), custom_call_target="tpu_custom_call" | custom-call | tf_op jit(solution)/shard_map/stress_1/pallas_call | solution.py:429
  89.4 2.2 %collective-permute-start.20 = (f32[120,256]{1,0:T(8,128)S(1)}, f32[120,256]{1,0:T(8,128)S(1)}, u32[]{:S(2)}, u32[]{:S(2)}) collective-permute-start(f32[120,256]{1,0:T(8,128)S(1)} %get-tuple-element.82), channel_id=1, source_target_pairs={{0,28},{4,8},{8,4},{12,16},{16,12},{20,24},{24,20},{28,0},{1,29},{... | collective-permute-start | bytes 368648 | tf_op jit(solution)/shard_map/ppermute | solution.py:459
  91.9 1.9 %collective-permute-start.22 = (f32[24,256]{1,0:T(8,128)S(1)}, f32[24,256]{1,0:T(8,128)S(1)}, u32[]{:S(2)}, u32[]{:S(2)}) collective-permute-start(f32[24,256]{1,0:T(8,128)S(1)} %get-tuple-element.84), channel_id=1, source_target_pairs={{0,3},{1,2},{2,1},{3,0},{4,7},{5,6},{6,5},{7,4},{8,11},{9,10},{10,... | collective-permute-start | bytes 73736 | tf_op jit(solution)/shard_map/ppermute | solution.py:457
  93.8 1.7 %collective-permute-done.21.refs_8_ = f32[24,256]{1,0:T(8,128)S(1)} collective-permute-done((f32[24,256]{1,0:T(8,128)S(1)}, f32[24,256]{1,0:T(8,128)S(1)}, u32[]{:S(2)}, u32[]{:S(2)}) %collective-permute-start.21) | collective-permute-done | bytes 24608 | tf_op jit(solution)/shard_map/ppermute | solution.py:458
  95.4 2.1 %collective-permute-done.22.refs_9_ = f32[24,256]{1,0:T(8,128)S(1)} collective-permute-done((f32[24,256]{1,0:T(8,128)S(1)}, f32[24,256]{1,0:T(8,128)S(1)}, u32[]{:S(2)}, u32[]{:S(2)}) %collective-permute-start.22) | collective-permute-done | bytes 24608 | tf_op jit(solution)/shard_map/ppermute | solution.py:457
  97.5 5.5 %velocity_2.1 = (f32[3,128,256]{2,1,0:T(8,128)}, f32[48,256]{1,0:T(8,128)S(1)}, f32[48,256]{1,0:T(8,128)S(1)}, f32[24,256]{1,0:T(8,128)S(1)}, f32[24,256]{1,0:T(8,128)S(1)}, /*index=5*/f32[3,6144]{1,0:T(4,128)}) custom-call(f32[6,128,256]{2,1,0:T(8,128)S(1)} %get-tuple-element.80.refs_0_, f32[3,128,256]{2,1,0:T(8,128)S(1)} %get-tuple-element.74.refs_1_, ...), custom_call_target="tpu_custom_call" | custom-call | tf_op jit(solution)/shard_map/velocity_2/pallas_call | solution.py:429
  103.9 2.1 %collective-permute-start.26 = (f32[24,256]{1,0:T(8,128)S(1)}, f32[24,256]{1,0:T(8,128)S(1)}, u32[]{:S(2)}, u32[]{:S(2)}) collective-permute-start(f32[24,256]{1,0:T(8,128)S(1)} %get-tuple-element.91), channel_id=1, source_target_pairs={{0,3},{1,2},{2,1},{3,0},{4,7},{5,6},{6,5},{7,4},{8,11},{9,10},{10,... | collective-permute-start | bytes 73736 | tf_op jit(solution)/shard_map/ppermute | solution.py:457
  105.9 1.8 %collective-permute-done.25.refs_5_ = f32[24,256]{1,0:T(8,128)S(1)} collective-permute-done((f32[24,256]{1,0:T(8,128)S(1)}, f32[24,256]{1,0:T(8,128)S(1)}, u32[]{:S(2)}, u32[]{:S(2)}) %collective-permute-start.25) | collective-permute-done | bytes 24608 | tf_op jit(solution)/shard_map/ppermute | solution.py:458
  107.7 1.8 %collective-permute-done.26.refs_6_ = f32[24,256]{1,0:T(8,128)S(1)} collective-permute-done((f32[24,256]{1,0:T(8,128)S(1)}, f32[24,256]{1,0:T(8,128)S(1)}, u32[]{:S(2)}, u32[]{:S(2)}) %collective-permute-start.26) | collective-permute-done | bytes 24608 | tf_op jit(solution)/shard_map/ppermute | solution.py:457
  109.5 1.0 copy-done.4
  110.5 1.4 %stress_2.1 = f32[6,128,256]{2,1,0:T(8,128)} custom-call(f32[6,128,256]{2,1,0:T(8,128)S(1)} %get-tuple-element.80.refs_0_, f32[3,128,256]{2,1,0:T(8,128)S(1)} %copy-done.4, s32[128,256]{1,0:T(8,128)S(1)} %bitcast.17, f32[48,256]{1,0:T(8,128)S(1)} %collective-permute-done.23.refs_3_, f32[48,256]{1,0:T(8,128)S(1)} %collective-permute-done.24.refs_4_, ...), custom_call_target="tpu_custom_call" | custom-call | tf_op jit(solution)/shard_map/stress_2/pallas_call | solution.py:429
  (49 shorter events, 7.9 us)
Async XLA Ops:
  0.6 1.1 %copy-start = (f32[6,8,16,256]{3,2,1,0:T(8,128)S(1)}, f32[6,8,16,256]{3,2,1,0:T(8,128)}, u32[]{:S(2)}) copy-start(f32[6,8,16,256]{3,2,1,0:T(8,128)} %param.9) | copy-start | bytes 2359300
  1.8 1.0 copy-start.1
  6.7 15.9 %copy-start.2 = (f32[8,16,256]{2,1,0:T(8,128)S(1)}, f32[8,16,256]{2,1,0:T(8,128)}, u32[]{:S(2)}) copy-start(f32[8,16,256]{2,1,0:T(8,128)} %param.11) | copy-start | bytes 393220
  9.1 13.5 %collective-permute-start = (f32[120,256]{1,0:T(8,128)S(1)}, f32[120,256]{1,0:T(8,128)S(1)}, u32[]{:S(2)}, u32[]{:S(2)}) collective-permute-start(f32[120,256]{1,0:T(8,128)S(1)} %get-tuple-element.51), channel_id=1, source_target_pairs={{0,4},{4,0},{8,12},{12,8},{16,20},{20,16},{24,28},{28,24},{1,5},{5... | collective-permute-start | bytes 368648 | tf_op jit(solution)/shard_map/ppermute | solution.py:460
  9.7 13.0 %collective-permute-start.1 = (f32[120,256]{1,0:T(8,128)S(1)}, f32[120,256]{1,0:T(8,128)S(1)}, u32[]{:S(2)}, u32[]{:S(2)}) collective-permute-start(f32[120,256]{1,0:T(8,128)S(1)} %get-tuple-element.52), channel_id=1, source_target_pairs={{0,28},{4,8},{8,4},{12,16},{16,12},{20,24},{24,20},{28,0},{1,29},{... | collective-permute-start | bytes 368648 | tf_op jit(solution)/shard_map/ppermute | solution.py:459
  13.2 9.4 %collective-permute-start.2 = (f32[64,256]{1,0:T(8,128)S(1)}, f32[64,256]{1,0:T(8,128)S(1)}, u32[]{:S(2)}, u32[]{:S(2)}) collective-permute-start(f32[64,256]{1,0:T(8,128)S(1)} %get-tuple-element.53), channel_id=1, source_target_pairs={{0,1},{1,0},{2,3},{3,2},{4,5},{5,4},{6,7},{7,6},{8,9},{9,8},{10,11... | collective-permute-start | bytes 196616 | tf_op jit(solution)/shard_map/ppermute | solution.py:458
  14.8 7.8 %collective-permute-start.3 = (f32[64,256]{1,0:T(8,128)S(1)}, f32[64,256]{1,0:T(8,128)S(1)}, u32[]{:S(2)}, u32[]{:S(2)}) collective-permute-start(f32[64,256]{1,0:T(8,128)S(1)} %get-tuple-element.54), channel_id=1, source_target_pairs={{0,3},{1,2},{2,1},{3,0},{4,7},{5,6},{6,5},{7,4},{8,11},{9,10},{10,... | collective-permute-start | bytes 196616 | tf_op jit(solution)/shard_map/ppermute | solution.py:457
  17.3 5.3 %collective-permute-start.4 = (f32[40,256]{1,0:T(8,128)S(1)}, f32[40,256]{1,0:T(8,128)S(1)}, u32[]{:S(2)}, u32[]{:S(2)}) collective-permute-start(f32[40,256]{1,0:T(8,128)S(1)} %get-tuple-element.50.refs_5_), channel_id=1, source_target_pairs={{0,2},{1,3},{2,0},{3,1},{4,6},{5,7},{6,4},{7,5},{8,10},{9,11},{10,... | collective-permute-start | bytes 122888 | tf_op jit(solution)/shard_map/ppermute | solution.py:466
  22.6 24.5 %copy-start.3 = (s32[8,16,256]{2,1,0:T(8,128)S(1)}, s32[8,16,256]{2,1,0:T(8,128)}, u32[]{:S(2)}) copy-start(s32[8,16,256]{2,1,0:T(8,128)} %param.12) | copy-start | bytes 393220
  38.9 8.2 %collective-permute-start.5 = (f32[144,256]{1,0:T(8,128)S(1)}, f32[144,256]{1,0:T(8,128)S(1)}, u32[]{:S(2)}, u32[]{:S(2)}) collective-permute-start(f32[144,256]{1,0:T(8,128)S(1)} %get-tuple-element.57), channel_id=1, source_target_pairs={{0,4},{4,0},{8,12},{12,8},{16,20},{20,16},{24,28},{28,24},{1,5},{5... | collective-permute-start | bytes 442376 | tf_op jit(solution)/shard_map/ppermute | solution.py:460
  39.0 8.2 %collective-permute-start.6 = (f32[144,256]{1,0:T(8,128)S(1)}, f32[144,256]{1,0:T(8,128)S(1)}, u32[]{:S(2)}, u32[]{:S(2)}) collective-permute-start(f32[144,256]{1,0:T(8,128)S(1)} %get-tuple-element.58), channel_id=1, source_target_pairs={{0,28},{4,8},{8,4},{12,16},{16,12},{20,24},{24,20},{28,0},{1,29},{... | collective-permute-start | bytes 442376 | tf_op jit(solution)/shard_map/ppermute | solution.py:459
  39.8 7.3 %collective-permute-start.7 = (f32[48,256]{1,0:T(8,128)S(1)}, f32[48,256]{1,0:T(8,128)S(1)}, u32[]{:S(2)}, u32[]{:S(2)}) collective-permute-start(f32[48,256]{1,0:T(8,128)S(1)} %get-tuple-element.59), channel_id=1, source_target_pairs={{0,1},{1,0},{2,3},{3,2},{4,5},{5,4},{6,7},{7,6},{8,9},{9,8},{10,11... | collective-permute-start | bytes 147464 | tf_op jit(solution)/shard_map/ppermute | solution.py:458
  39.9 7.3 %collective-permute-start.8 = (f32[48,256]{1,0:T(8,128)S(1)}, f32[48,256]{1,0:T(8,128)S(1)}, u32[]{:S(2)}, u32[]{:S(2)}) collective-permute-start(f32[48,256]{1,0:T(8,128)S(1)} %get-tuple-element.60), channel_id=1, source_target_pairs={{0,3},{1,2},{2,1},{3,0},{4,7},{5,6},{6,5},{7,4},{8,11},{9,10},{10,... | collective-permute-start | bytes 147464 | tf_op jit(solution)/shard_map/ppermute | solution.py:457
  42.4 4.7 %collective-permute-start.9 = (f32[24,256]{1,0:T(8,128)S(1)}, f32[24,256]{1,0:T(8,128)S(1)}, u32[]{:S(2)}, u32[]{:S(2)}) collective-permute-start(f32[24,256]{1,0:T(8,128)S(1)} %get-tuple-element.61.refs_8_.refs_5_), channel_id=1, source_target_pairs={{0,2},{1,3},{2,0},{3,1},{4,6},{5,7},{6,4},{7,5},{8,10},{9,11},{10,... | collective-permute-start | bytes 73736 | tf_op jit(solution)/shard_map/ppermute | solution.py:466
  56.5 8.4 %collective-permute-start.10 = (f32[192,256]{1,0:T(8,128)S(1)}, f32[192,256]{1,0:T(8,128)S(1)}, u32[]{:S(2)}, u32[]{:S(2)}) collective-permute-start(f32[192,256]{1,0:T(8,128)S(1)} %get-tuple-element.67), channel_id=1, source_target_pairs={{0,4},{4,0},{8,12},{12,8},{16,20},{20,16},{24,28},{28,24},{1,5},{5... | collective-permute-start | bytes 589832 | tf_op jit(solution)/shard_map/ppermute | solution.py:460
  56.5 8.3 %collective-permute-start.11 = (f32[192,256]{1,0:T(8,128)S(1)}, f32[192,256]{1,0:T(8,128)S(1)}, u32[]{:S(2)}, u32[]{:S(2)}) collective-permute-start(f32[192,256]{1,0:T(8,128)S(1)} %get-tuple-element.68), channel_id=1, source_target_pairs={{0,28},{4,8},{8,4},{12,16},{16,12},{20,24},{24,20},{28,0},{1,29},{... | collective-permute-start | bytes 589832 | tf_op jit(solution)/shard_map/ppermute | solution.py:459
  58.3 3.8 %collective-permute-start.12 = (f32[24,256]{1,0:T(8,128)S(1)}, f32[24,256]{1,0:T(8,128)S(1)}, u32[]{:S(2)}, u32[]{:S(2)}) collective-permute-start(f32[24,256]{1,0:T(8,128)S(1)} %get-tuple-element.69), channel_id=1, source_target_pairs={{0,1},{1,0},{2,3},{3,2},{4,5},{5,4},{6,7},{7,6},{8,9},{9,8},{10,11... | collective-permute-start | bytes 73736 | tf_op jit(solution)/shard_map/ppermute | solution.py:458
  59.2 5.6 %collective-permute-start.13 = (f32[24,256]{1,0:T(8,128)S(1)}, f32[24,256]{1,0:T(8,128)S(1)}, u32[]{:S(2)}, u32[]{:S(2)}) collective-permute-start(f32[24,256]{1,0:T(8,128)S(1)} %get-tuple-element.70), channel_id=1, source_target_pairs={{0,3},{1,2},{2,1},{3,0},{4,7},{5,6},{6,5},{7,4},{8,11},{9,10},{10,... | collective-permute-start | bytes 73736 | tf_op jit(solution)/shard_map/ppermute | solution.py:457
  71.9 8.2 %collective-permute-start.14 = (f32[120,256]{1,0:T(8,128)S(1)}, f32[120,256]{1,0:T(8,128)S(1)}, u32[]{:S(2)}, u32[]{:S(2)}) collective-permute-start(f32[120,256]{1,0:T(8,128)S(1)} %get-tuple-element.75), channel_id=1, source_target_pairs={{0,4},{4,0},{8,12},{12,8},{16,20},{20,16},{24,28},{28,24},{1,5},{5... | collective-permute-start | bytes 368648 | tf_op jit(solution)/shard_map/ppermute | solution.py:460
  72.0 8.1 %collective-permute-start.15 = (f32[120,256]{1,0:T(8,128)S(1)}, f32[120,256]{1,0:T(8,128)S(1)}, u32[]{:S(2)}, u32[]{:S(2)}) collective-permute-start(f32[120,256]{1,0:T(8,128)S(1)} %get-tuple-element.76), channel_id=1, source_target_pairs={{0,28},{4,8},{8,4},{12,16},{16,12},{20,24},{24,20},{28,0},{1,29},{... | collective-permute-start | bytes 368648 | tf_op jit(solution)/shard_map/ppermute | solution.py:459
  73.4 6.6 %collective-permute-start.16 = (f32[48,256]{1,0:T(8,128)S(1)}, f32[48,256]{1,0:T(8,128)S(1)}, u32[]{:S(2)}, u32[]{:S(2)}) collective-permute-start(f32[48,256]{1,0:T(8,128)S(1)} %get-tuple-element.77), channel_id=1, source_target_pairs={{0,1},{1,0},{2,3},{3,2},{4,5},{5,4},{6,7},{7,6},{8,9},{9,8},{10,11... | collective-permute-start | bytes 147464 | tf_op jit(solution)/shard_map/ppermute | solution.py:458
  73.4 6.6 %collective-permute-start.17 = (f32[48,256]{1,0:T(8,128)S(1)}, f32[48,256]{1,0:T(8,128)S(1)}, u32[]{:S(2)}, u32[]{:S(2)}) collective-permute-start(f32[48,256]{1,0:T(8,128)S(1)} %get-tuple-element.78), channel_id=1, source_target_pairs={{0,3},{1,2},{2,1},{3,0},{4,7},{5,6},{6,5},{7,4},{8,11},{9,10},{10,... | collective-permute-start | bytes 147464 | tf_op jit(solution)/shard_map/ppermute | solution.py:457
  75.3 4.7 %collective-permute-start.18 = (f32[24,256]{1,0:T(8,128)S(1)}, f32[24,256]{1,0:T(8,128)S(1)}, u32[]{:S(2)}, u32[]{:S(2)}) collective-permute-start(f32[24,256]{1,0:T(8,128)S(1)} %get-tuple-element.79.refs_8_.refs_5_), channel_id=1, source_target_pairs={{0,2},{1,3},{2,0},{3,1},{4,6},{5,7},{6,4},{7,5},{8,10},{9,11},{10,... | collective-permute-start | bytes 73736 | tf_op jit(solution)/shard_map/ppermute | solution.py:466
  89.3 8.2 %collective-permute-start.19 = (f32[120,256]{1,0:T(8,128)S(1)}, f32[120,256]{1,0:T(8,128)S(1)}, u32[]{:S(2)}, u32[]{:S(2)}) collective-permute-start(f32[120,256]{1,0:T(8,128)S(1)} %get-tuple-element.81), channel_id=1, source_target_pairs={{0,4},{4,0},{8,12},{12,8},{16,20},{20,16},{24,28},{28,24},{1,5},{5... | collective-permute-start | bytes 368648 | tf_op jit(solution)/shard_map/ppermute | solution.py:460
  89.4 8.1 %collective-permute-start.20 = (f32[120,256]{1,0:T(8,128)S(1)}, f32[120,256]{1,0:T(8,128)S(1)}, u32[]{:S(2)}, u32[]{:S(2)}) collective-permute-start(f32[120,256]{1,0:T(8,128)S(1)} %get-tuple-element.82), channel_id=1, source_target_pairs={{0,28},{4,8},{8,4},{12,16},{16,12},{20,24},{24,20},{28,0},{1,29},{... | collective-permute-start | bytes 368648 | tf_op jit(solution)/shard_map/ppermute | solution.py:459
  91.6 3.8 %collective-permute-start.21 = (f32[24,256]{1,0:T(8,128)S(1)}, f32[24,256]{1,0:T(8,128)S(1)}, u32[]{:S(2)}, u32[]{:S(2)}) collective-permute-start(f32[24,256]{1,0:T(8,128)S(1)} %get-tuple-element.83), channel_id=1, source_target_pairs={{0,1},{1,0},{2,3},{3,2},{4,5},{5,4},{6,7},{7,6},{8,9},{9,8},{10,11... | collective-permute-start | bytes 73736 | tf_op jit(solution)/shard_map/ppermute | solution.py:458
  91.9 5.6 %collective-permute-start.22 = (f32[24,256]{1,0:T(8,128)S(1)}, f32[24,256]{1,0:T(8,128)S(1)}, u32[]{:S(2)}, u32[]{:S(2)}) collective-permute-start(f32[24,256]{1,0:T(8,128)S(1)} %get-tuple-element.84), channel_id=1, source_target_pairs={{0,3},{1,2},{2,1},{3,0},{4,7},{5,6},{6,5},{7,4},{8,11},{9,10},{10,... | collective-permute-start | bytes 73736 | tf_op jit(solution)/shard_map/ppermute | solution.py:457
  103.0 6.5 %collective-permute-start.23 = (f32[48,256]{1,0:T(8,128)S(1)}, f32[48,256]{1,0:T(8,128)S(1)}, u32[]{:S(2)}, u32[]{:S(2)}) collective-permute-start(f32[48,256]{1,0:T(8,128)S(1)} %get-tuple-element.88), channel_id=1, source_target_pairs={{0,4},{4,0},{8,12},{12,8},{16,20},{20,16},{24,28},{28,24},{1,5},{5... | collective-permute-start | bytes 147464 | tf_op jit(solution)/shard_map/ppermute | solution.py:460
  103.0 6.5 %collective-permute-start.24 = (f32[48,256]{1,0:T(8,128)S(1)}, f32[48,256]{1,0:T(8,128)S(1)}, u32[]{:S(2)}, u32[]{:S(2)}) collective-permute-start(f32[48,256]{1,0:T(8,128)S(1)} %get-tuple-element.89), channel_id=1, source_target_pairs={{0,28},{4,8},{8,4},{12,16},{16,12},{20,24},{24,20},{28,0},{1,29},{... | collective-permute-start | bytes 147464 | tf_op jit(solution)/shard_map/ppermute | solution.py:459
  103.9 3.8 %collective-permute-start.25 = (f32[24,256]{1,0:T(8,128)S(1)}, f32[24,256]{1,0:T(8,128)S(1)}, u32[]{:S(2)}, u32[]{:S(2)}) collective-permute-start(f32[24,256]{1,0:T(8,128)S(1)} %get-tuple-element.90), channel_id=1, source_target_pairs={{0,1},{1,0},{2,3},{3,2},{4,5},{5,4},{6,7},{7,6},{8,9},{9,8},{10,11... | collective-permute-start | bytes 73736 | tf_op jit(solution)/shard_map/ppermute | solution.py:458
  103.9 5.6 %collective-permute-start.26 = (f32[24,256]{1,0:T(8,128)S(1)}, f32[24,256]{1,0:T(8,128)S(1)}, u32[]{:S(2)}, u32[]{:S(2)}) collective-permute-start(f32[24,256]{1,0:T(8,128)S(1)} %get-tuple-element.91), channel_id=1, source_target_pairs={{0,3},{1,2},{2,1},{3,0},{4,7},{5,6},{6,5},{7,4},{8,11},{9,10},{10,... | collective-permute-start | bytes 73736 | tf_op jit(solution)/shard_map/ppermute | solution.py:457
  109.5 1.0 copy-start.4
  (5 other events, 3.9 us)

commit v2 on v1

--- a/solution.py
+++ b/solution.py
@@ -1,4 +1,5 @@
 import functools
+import math
 
 import jax
 import jax.numpy as jnp
@@ -23,7 +24,7 @@
         self.rows = self.cz * self.cx
         self.pile = pile_velocity.shape[1]
         self.pr = self.pile // COLS
-        self.wp = -(-3 * self.pr // 16) * 16
+        self.wp = 3 * self.pr
         self.pairs = pair_cell.shape[1]
         self.kn = self.pairs // COLS
         self.nd = lax.axis_size("depth")
@@ -85,7 +86,7 @@
 
 
 def row_of(ref, row):
-    return ref[pl.ds(row, 1), :]
+    return ref[row : row + 1, :]
 
 
 def shifted_rows(a, low, high):
@@ -128,26 +129,33 @@
 
 
 def gather_cells(sz, table, ids, out):
-    def body(j, carry):
+    for j in range(sz.kn):
         got = gather_chunk(table, row_of(ids, j), row_of(ids, sz.kn + j), 3, sz.rows)
         for c in range(3):
-            out[pl.ds(c * sz.kn + j, 1), :] = got[c]
+            out[c * sz.kn + j : c * sz.kn + j + 1, :] = got[c]
+
+
+def scatter_sets(sz, parts, sets, ids, acc):
+    group = math.gcd(sz.np, 4)
+    acc[...] = jnp.zeros_like(acc)
+
+    def body(t, carry):
+        total = None
+        for s in range(group):
+            one, index = sets.at[t * group + s], ids.at[t * group + s]
+            for j in range(sz.kn):
+                values = [row_of(one, c * sz.kn + j) for c in range(parts)]
+                term = scatter_chunk(
+                    values, row_of(index, j), row_of(index, sz.kn + j), sz.wp
+                )
+                total = term if total is None else total + term
+        acc[...] += total
         return carry
 
-    lax.fori_loop(0, sz.kn, body, 0)
-
-
-def scatter_sets(sz, parts, sets, ids, acc):
-    acc[...] = jnp.zeros_like(acc)
-
-    def body(t, carry):
-        s, j = t // sz.kn, lax.rem(t, sz.kn)
-        one, index = sets.at[s], ids.at[s]
-        values = [row_of(one, c * sz.kn + j) for c in range(parts)]
-        acc[...] += scatter_chunk(values, row_of(index, j), row_of(index, sz.kn + j), sz.wp)
-        return carry
-
-    lax.fori_loop(0, sz.np * sz.kn, body, 0)
+    if group == sz.np:
+        body(0, 0)
+    else:
+        lax.fori_loop(0, sz.np // group, body, 0)
 
 
 def sort_sets(sz, plan, own, got, sets, rows, offset):
@@ -189,13 +197,25 @@
     return p + time_step * (jack[rows, :] - (count * p - summed)) / mass[...]
 
 
-def first_kernel(
-    sz, stress, velocity, pile_in, mass_in, jack_in, elem_in, cell_in,
-    to_da, to_db, to_pa, to_pb, to_all, cell_ids, elem_ids, pile, mass, jack,
-    high, low,
-):
+def first_kernel(sz, *refs):
+    refs = list(refs)
+    take = lambda n: [refs.pop(0) for _ in range(n)]
+    sources = take(9)
+    to_da, to_db, to_pa, to_pb, to_all, cell_ids, elem_ids, pile, mass, jack = take(10)
+    stress, velocity, density, flags = take(4)
+    high, low, pile_in, mass_in, jack_in, elem_in, cell_in, sems = take(8)
+    targets = (
+        cell_in, velocity, elem_in, pile_in, mass_in, jack_in, stress, density, flags,
+    )
+    copies = [
+        pltpu.make_async_copy(a, b, sems.at[i]) for i, (a, b) in enumerate(zip(sources, targets))
+    ]
+    for copy in copies:
+        copy.start()
     depth, plan = lax.axis_index("depth"), lax.axis_index("plan")
     kn, pr = sz.kn, sz.pr
+    for copy in copies[:3]:
+        copy.wait()
     for j in range(kn):
         lanes = slice(j * COLS, (j + 1) * COLS)
         cell, elem = cell_in[:, lanes], elem_in[:, lanes]
@@ -205,14 +225,16 @@
         elem_ids[kn + j : kn + j + 1, :] = lax.bitwise_and(elem, COLS - 1)
         to_all[3 * kn + j : 3 * kn + j + 1, :] = jnp.where(cell >= 0, 1.0, 0.0)
         to_all[4 * kn + j : 4 * kn + j + 1, :] = elem.astype(F32)
+    store_split(sz, lambda c: velocity[c], 3, sz.rows, (high, low))
+    gather_cells(sz, (high, low), cell_ids, to_all)
+    for copy in copies[3:]:
+        copy.wait()
     for r in range(pr):
         lanes = slice(r * COLS, (r + 1) * COLS)
         for c in range(3):
             pile[c * pr + r : c * pr + r + 1, :] = pile_in[c : c + 1, lanes]
             jack[c * pr + r : c * pr + r + 1, :] = jack_in[c : c + 1, lanes]
         mass[r : r + 1, :] = mass_in[:, lanes]
-    store_split(sz, lambda c: velocity[c], 3, sz.rows, (high, low))
-    gather_cells(sz, (high, low), cell_ids, to_all)
     head = 3 * sz.cx
     to_da[head:, :] = pile[...]
     to_db[head:, :] = pile[...]
@@ -235,19 +257,15 @@
         hi, lo = split(table)
         pile_high[c * wp : (c + 1) * wp, :] = hi
         pile_low[c * wp : (c + 1) * wp, :] = lo
-    on_cells[...] = jnp.zeros_like(on_cells)
-
-    def body(j, carry):
+    total = None
+    for j in range(kn):
         at_pile = gather_chunk(
             (pile_high, pile_low), row_of(elem_ids, j), row_of(elem_ids, kn + j), 3, wp
         )
         push = [at_pile[c] - row_of(at_cells, c * kn + j) for c in range(3)]
-        on_cells[...] += scatter_chunk(
-            push, row_of(cell_ids, j), row_of(cell_ids, kn + j), rows
-        )
-        return carry
-
-    lax.fori_loop(0, kn, body, 0)
+        term = scatter_chunk(push, row_of(cell_ids, j), row_of(cell_ids, kn + j), rows)
+        total = term if total is None else total + term
+    on_cells[...] = total
     plane = lambda c, z: stress[c, z * cx : (z + 1) * cx, :]
     d_low, d_high = low_high(
         depth, sz.nd, from_da, from_db, (slice(0, 3 * cx), slice(None))
@@ -424,14 +442,15 @@
     send_edges(sz, depth, plan, DEPTH_PART, PLAN_PART, plane, (to_da, to_db, to_pa, to_pb))
 
 
-def call(body, name, ins, outs, scratch=()):
+def call(body, name, ins, outs, scratch=(), copies=0):
     vmem = pl.BlockSpec(memory_space=pltpu.VMEM)
+    sems = [pltpu.SemaphoreType.DMA((copies,))] if copies else []
     return pl.pallas_call(
         body,
         out_shape=[jax.ShapeDtypeStruct(shape, dtype) for shape, dtype in outs],
-        in_specs=[vmem] * len(ins),
+        in_specs=[pl.BlockSpec(memory_space=pl.ANY) if copies else vmem] * len(ins),
         out_specs=[vmem] * len(outs),
-        scratch_shapes=[pltpu.VMEM(shape, dtype) for shape, dtype in scratch],
+        scratch_shapes=[pltpu.VMEM(shape, dtype) for shape, dtype in scratch] + sems,
         compiler_params=pltpu.CompilerParams(vmem_limit_bytes=48 * 2**20),
         name=name,
     )(*ins)
@@ -483,17 +502,22 @@
         functools.partial(first_kernel, sz),
         "first",
         [
-            stress, velocity, pile_velocity, pile_mass.reshape(1, -1), jack_force, pair_elem,
-            pair_cell,
+            pair_cell, velocity, pair_elem, pile_velocity, pile_mass.reshape(1, -1), jack_force,
+            stress, density, flags,
         ],
         edges(pr3, 5 * kn)
         + [
             ((5 * kn, COLS), F32), ((2 * kn, COLS), I32), ((2 * kn, COLS), I32),
             ((pr3, COLS), F32), ((pr, COLS), F32), ((pr3, COLS), F32),
+            (stress.shape, F32), (velocity.shape, F32), (density.shape, F32), (flags.shape, I32),
         ],
-        tables,
-    )
-    at_cells, cell_ids, elem_ids, pile, mass, jack = to[4:]
+        tables
+        + [(pile_velocity.shape, F32), ((1, sz.pile), F32), (jack_force.shape, F32)]
+        + [(pair_elem.shape, I32), (pair_cell.shape, I32)],
+        copies=9,
+    )
+    at_cells, cell_ids, elem_ids, pile, mass, jack = to[4:10]
+    stress, velocity, density, flags = to[10:]
     others = to_others(at_cells)
     got = swap(*to[:4])
 

time: 112 us -> 90 us (0.80)
  Pallas kernels: 51.1 us -> 26.9 us
  local copies, waits for them, and re-layouts: 7.04 us -> 8.84 us
    pallas_call x7, Pallas kernels: 51.1 us -> 26.9 us  [call(): pl.pallas_call(body, out_shape=[jax.ShapeDtypeStruct(shape, dtype) for sh...]
    unnamed x20, local copies, waits for them, and re-layouts: 7.04 us -> 8.84 us
where the time goes in v2:
time: 90 us; the launch traced here: 89.5 us
  starting transfers between devices  29.5 us (33%)
  Pallas kernels  26.9 us (30%)
  waiting for transfers between devices  23.5 us (26%)
  local copies, waits for them, and re-layouts  8.84 us (10%)
    pallas_call x7, Pallas kernels, call(): pl.pallas_call(body, out_shape=[jax.ShapeDtypeStruct(shape, dtype) for sh...  26.9 us
    ppermute x6, starting transfers between devices, swap(): pb = lax.ppermute(pb, 'plan', p_second)  12.5 us
    ppermute x3, waiting for transfers between devices, to_others(): lax.ppermute(x, 'plan', [(i, (i + s) % sz.np) for i in range(sz.np)])  12.2 us
    ppermute x6, starting transfers between devices, swap(): db = lax.ppermute(db, 'depth', d_second)  10.5 us
    unnamed x20, local copies, waits for them, and re-layouts  8.84 us
    ppermute x6, waiting for transfers between devices, swap(): pb = lax.ppermute(pb, 'plan', p_second)  6.6 us
    ppermute x6, waiting for transfers between devices, swap(): pa = lax.ppermute(pa, 'plan', p_first)  4.66 us
    ppermute x6, starting transfers between devices, swap(): pa = lax.ppermute(pa, 'plan', p_first)  2.84 us
  transfers between devices with their start and end apart: 27, of which 9 were waited for; matrix products, arithmetic and copies ran while one was open for 0% of the time, Pallas kernels for 0%

profile of v2, /device:TPU:0, one launch (start us, length us, event | category | flops | bytes accessed | tf_op | source)
XLA Modules:
  0.0 89.5 jit_solution(2189786890613091696)
XLA Ops:
  1.3 1.1 %copy-done = f32[6,8,16,256]{3,2,1,0:T(8,128)S(1)} copy-done((f32[6,8,16,256]{3,2,1,0:T(8,128)S(1)}, f32[6,8,16,256]{3,2,1,0:T(8,128)}, u32[]{:S(2)}) %copy-start) | copy-done | bytes 786456
  2.5 1.0 %copy-done.1 = f32[3,8,16,256]{3,2,1,0:T(8,128)S(1)} copy-done((f32[3,8,16,256]{3,2,1,0:T(8,128)S(1)}, f32[3,8,16,256]{3,2,1,0:T(8,128)}, u32[]{:S(2)}) %copy-start.1) | copy-done | bytes 393240
  8.5 2.5 %first.1 = (f32[120,256]{1,0:T(8,128)S(1)}, f32[120,256]{1,0:T(8,128)S(1)}, f32[64,256]{1,0:T(8,128)S(1)}, f32[64,256]{1,0:T(8,128)S(1)}, f32[40,256]{1,0:T(8,12...) custom-call(s32[1,2048]{1,0:T(1,128)S(1)} %copy-done.8, ...), custom_call_target="tpu_custom_call" | custom-call | tf_op jit(solution)/shard_map/first/pallas_call | solution.py:448
  11.5 3.5 %collective-permute-start.1 = (f32[120,256]{1,0:T(8,128)S(1)}, f32[120,256]{1,0:T(8,128)S(1)}, u32[]{:S(2)}, u32[]{:S(2)}) collective-permute-start(f32[120,256]{1,0:T(8,128)S(1)} %get-tuple-element.59), channel_id=1, source_target_pairs={{0,28},{4,8},{8,4},{12,16},{16,12},{20,24},{24,20},{28,0},{1,29},{... | collective-permute-start | bytes 368648 | tf_op jit(solution)/shard_map/ppermute | solution.py:478
  15.1 1.6 %collective-permute-start.2 = (f32[64,256]{1,0:T(8,128)S(1)}, f32[64,256]{1,0:T(8,128)S(1)}, u32[]{:S(2)}, u32[]{:S(2)}) collective-permute-start(f32[64,256]{1,0:T(8,128)S(1)} %get-tuple-element.60), channel_id=1, source_target_pairs={{0,1},{1,0},{2,3},{3,2},{4,5},{5,4},{6,7},{7,6},{8,9},{9,8},{10,11... | collective-permute-start | bytes 196616 | tf_op jit(solution)/shard_map/ppermute | solution.py:477
  16.6 2.5 %collective-permute-start.3 = (f32[64,256]{1,0:T(8,128)S(1)}, f32[64,256]{1,0:T(8,128)S(1)}, u32[]{:S(2)}, u32[]{:S(2)}) collective-permute-start(f32[64,256]{1,0:T(8,128)S(1)} %get-tuple-element.61), channel_id=1, source_target_pairs={{0,3},{1,2},{2,1},{3,0},{4,7},{5,6},{6,5},{7,4},{8,11},{9,10},{10,... | collective-permute-start | bytes 196616 | tf_op jit(solution)/shard_map/ppermute | solution.py:476
  19.2 5.2 %collective-permute-done.4.refs_10_ = f32[40,256]{1,0:T(8,128)S(1)} collective-permute-done((f32[40,256]{1,0:T(8,128)S(1)}, f32[40,256]{1,0:T(8,128)S(1)}, u32[]{:S(2)}, u32[]{:S(2)}) %collective-permute-start.4) | collective-permute-done | bytes 40992 | tf_op jit(solution)/shard_map/ppermute | solution.py:485
  24.5 8.6 %velocity_0.1 = (f32[3,128,256]{2,1,0:T(8,128)S(1)}, f32[144,256]{1,0:T(8,128)S(1)}, f32[144,256]{1,0:T(8,128)S(1)}, f32[48,256]{1,0:T(8,128)S(1)}, f32[48,256]{...) custom-call(f32[6,128,256]{2,1,0:T(8,128)S(1)} %get-tuple-element.52.refs_0_, ...), custom_call_target="tpu_custom_call" | custom-call | tf_op jit(solution)/shard_map/velocity_0/pallas_call | solution.py:448
  34.0 2.5 %collective-permute-start.8 = (f32[48,256]{1,0:T(8,128)S(1)}, f32[48,256]{1,0:T(8,128)S(1)}, u32[]{:S(2)}, u32[]{:S(2)}) collective-permute-start(f32[48,256]{1,0:T(8,128)S(1)} %get-tuple-element.68), channel_id=1, source_target_pairs={{0,3},{1,2},{2,1},{3,0},{4,7},{5,6},{6,5},{7,4},{8,11},{9,10},{10,... | collective-permute-start | bytes 147464 | tf_op jit(solution)/shard_map/ppermute | solution.py:476
  37.5 3.8 %collective-permute-done.9.refs_7_ = f32[24,256]{1,0:T(8,128)S(1)} collective-permute-done((f32[24,256]{1,0:T(8,128)S(1)}, f32[24,256]{1,0:T(8,128)S(1)}, u32[]{:S(2)}, u32[]{:S(2)}) %collective-permute-start.9) | collective-permute-done | bytes 24608 | tf_op jit(solution)/shard_map/ppermute | solution.py:485
  41.3 3.6 %stress_0.1 = (f32[6,128,256]{2,1,0:T(8,128)S(1)}, f32[192,256]{1,0:T(8,128)S(1)}, f32[192,256]{1,0:T(8,128)S(1)}, f32[24,256]{1,0:T(8,128)S(1)}, f32[24,256]{1,...) custom-call(f32[6,128,256]{2,1,0:T(8,128)S(1)} %get-tuple-element.52.refs_0_, ...), custom_call_target="tpu_custom_call" | custom-call | tf_op jit(solution)/shard_map/stress_0/pallas_call | solution.py:448
  45.2 1.8 %collective-permute-start.11 = (f32[192,256]{1,0:T(8,128)S(1)}, f32[192,256]{1,0:T(8,128)S(1)}, u32[]{:S(2)}, u32[]{:S(2)}) collective-permute-start(f32[192,256]{1,0:T(8,128)S(1)} %get-tuple-element.76), channel_id=1, source_target_pairs={{0,28},{4,8},{8,4},{12,16},{16,12},{20,24},{24,20},{28,0},{1,29},{... | collective-permute-start | bytes 589832 | tf_op jit(solution)/shard_map/ppermute | solution.py:478
  47.0 0.9 %collective-permute-start.12 = (f32[24,256]{1,0:T(8,128)S(1)}, f32[24,256]{1,0:T(8,128)S(1)}, u32[]{:S(2)}, u32[]{:S(2)}) collective-permute-start(f32[24,256]{1,0:T(8,128)S(1)} %get-tuple-element.77), channel_id=1, source_target_pairs={{0,1},{1,0},{2,3},{3,2},{4,5},{5,4},{6,7},{7,6},{8,9},{9,8},{10,11... | collective-permute-start | bytes 73736 | tf_op jit(solution)/shard_map/ppermute | solution.py:477
  47.9 1.6 %collective-permute-start.13 = (f32[24,256]{1,0:T(8,128)S(1)}, f32[24,256]{1,0:T(8,128)S(1)}, u32[]{:S(2)}, u32[]{:S(2)}) collective-permute-start(f32[24,256]{1,0:T(8,128)S(1)} %get-tuple-element.78), channel_id=1, source_target_pairs={{0,3},{1,2},{2,1},{3,0},{4,7},{5,6},{6,5},{7,4},{8,11},{9,10},{10,... | collective-permute-start | bytes 73736 | tf_op jit(solution)/shard_map/ppermute | solution.py:476
  49.4 1.3 %collective-permute-done.12.refs_8_ = f32[24,256]{1,0:T(8,128)S(1)} collective-permute-done((f32[24,256]{1,0:T(8,128)S(1)}, f32[24,256]{1,0:T(8,128)S(1)}, u32[]{:S(2)}, u32[]{:S(2)}) %collective-permute-start.12) | collective-permute-done | bytes 24608 | tf_op jit(solution)/shard_map/ppermute | solution.py:477
  50.8 2.7 %collective-permute-done.13.refs_9_ = f32[24,256]{1,0:T(8,128)S(1)} collective-permute-done((f32[24,256]{1,0:T(8,128)S(1)}, f32[24,256]{1,0:T(8,128)S(1)}, u32[]{:S(2)}, u32[]{:S(2)}) %collective-permute-start.13) | collective-permute-done | bytes 24608 | tf_op jit(solution)/shard_map/ppermute | solution.py:476
  53.5 3.8 %velocity_1.1 = (f32[3,128,256]{2,1,0:T(8,128)S(1)}, f32[120,256]{1,0:T(8,128)S(1)}, f32[120,256]{1,0:T(8,128)S(1)}, f32[48,256]{1,0:T(8,128)S(1)}, f32[48,256]{...) custom-call(f32[6,128,256]{2,1,0:T(8,128)S(1)} %get-tuple-element.74.refs_0_, ...), custom_call_target="tpu_custom_call" | custom-call | tf_op jit(solution)/shard_map/velocity_1/pallas_call | solution.py:448
  57.4 1.4 %collective-permute-start.15 = (f32[120,256]{1,0:T(8,128)S(1)}, f32[120,256]{1,0:T(8,128)S(1)}, u32[]{:S(2)}, u32[]{:S(2)}) collective-permute-start(f32[120,256]{1,0:T(8,128)S(1)} %get-tuple-element.84), channel_id=1, source_target_pairs={{0,28},{4,8},{8,4},{12,16},{16,12},{20,24},{24,20},{28,0},{1,29},{... | collective-permute-start | bytes 368648 | tf_op jit(solution)/shard_map/ppermute | solution.py:478
  58.8 1.9 %collective-permute-start.17 = (f32[48,256]{1,0:T(8,128)S(1)}, f32[48,256]{1,0:T(8,128)S(1)}, u32[]{:S(2)}, u32[]{:S(2)}) collective-permute-start(f32[48,256]{1,0:T(8,128)S(1)} %get-tuple-element.86), channel_id=1, source_target_pairs={{0,3},{1,2},{2,1},{3,0},{4,7},{5,6},{6,5},{7,4},{8,11},{9,10},{10,... | collective-permute-start | bytes 147464 | tf_op jit(solution)/shard_map/ppermute | solution.py:476
  60.8 1.6 %collective-permute-start.18 = (f32[24,256]{1,0:T(8,128)S(1)}, f32[24,256]{1,0:T(8,128)S(1)}, u32[]{:S(2)}, u32[]{:S(2)}) collective-permute-start(f32[24,256]{1,0:T(8,128)S(1)} %get-tuple-element.87.refs_8_.refs_5_), channel_id=1, source_target_pairs={{0,2},{1,3},{2,0},{3,1},{4,6},{5,7},{6,4},{7,5},{8,10},{9,11},{10,... | collective-permute-start | bytes 73736 | tf_op jit(solution)/shard_map/ppermute | solution.py:485
  62.3 3.2 %collective-permute-done.18.refs_7_ = f32[24,256]{1,0:T(8,128)S(1)} collective-permute-done((f32[24,256]{1,0:T(8,128)S(1)}, f32[24,256]{1,0:T(8,128)S(1)}, u32[]{:S(2)}, u32[]{:S(2)}) %collective-permute-start.18) | collective-permute-done | bytes 24608 | tf_op jit(solution)/shard_map/ppermute | solution.py:485
  65.5 3.6 %stress_1.1 = (f32[6,128,256]{2,1,0:T(8,128)S(1)}, f32[120,256]{1,0:T(8,128)S(1)}, f32[120,256]{1,0:T(8,128)S(1)}, f32[24,256]{1,0:T(8,128)S(1)}, f32[24,256]{1,0:T(8,128)S(1)}, /*index=5*/f32[72,256]{1,0:T(8,128)S(1)}) custom-call(f32[6,128,256]{2,1,0:T(8,128)S(1)} %get-tuple-element.74.refs_0_, f32[3,128,256]{2,1,0:T(8,128)S(1)} %get-tuple-element.82.refs_1_, ...), custom_call_target="tpu_custom_call" | custom-call | tf_op jit(solution)/shard_map/stress_1/pallas_call | solution.py:448
  69.2 2.2 %collective-permute-start.20 = (f32[120,256]{1,0:T(8,128)S(1)}, f32[120,256]{1,0:T(8,128)S(1)}, u32[]{:S(2)}, u32[]{:S(2)}) collective-permute-start(f32[120,256]{1,0:T(8,128)S(1)} %get-tuple-element.90), channel_id=1, source_target_pairs={{0,28},{4,8},{8,4},{12,16},{16,12},{20,24},{24,20},{28,0},{1,29},{... | collective-permute-start | bytes 368648 | tf_op jit(solution)/shard_map/ppermute | solution.py:478
  71.7 1.9 %collective-permute-start.22 = (f32[24,256]{1,0:T(8,128)S(1)}, f32[24,256]{1,0:T(8,128)S(1)}, u32[]{:S(2)}, u32[]{:S(2)}) collective-permute-start(f32[24,256]{1,0:T(8,128)S(1)} %get-tuple-element.92), channel_id=1, source_target_pairs={{0,3},{1,2},{2,1},{3,0},{4,7},{5,6},{6,5},{7,4},{8,11},{9,10},{10,... | collective-permute-start | bytes 73736 | tf_op jit(solution)/shard_map/ppermute | solution.py:476
  73.6 1.7 %collective-permute-done.21.refs_8_ = f32[24,256]{1,0:T(8,128)S(1)} collective-permute-done((f32[24,256]{1,0:T(8,128)S(1)}, f32[24,256]{1,0:T(8,128)S(1)}, u32[]{:S(2)}, u32[]{:S(2)}) %collective-permute-start.21) | collective-permute-done | bytes 24608 | tf_op jit(solution)/shard_map/ppermute | solution.py:477
  75.3 2.1 %collective-permute-done.22.refs_9_ = f32[24,256]{1,0:T(8,128)S(1)} collective-permute-done((f32[24,256]{1,0:T(8,128)S(1)}, f32[24,256]{1,0:T(8,128)S(1)}, u32[]{:S(2)}, u32[]{:S(2)}) %collective-permute-start.22) | collective-permute-done | bytes 24608 | tf_op jit(solution)/shard_map/ppermute | solution.py:476
  77.4 3.3 %velocity_2.1 = (f32[3,128,256]{2,1,0:T(8,128)}, f32[48,256]{1,0:T(8,128)S(1)}, f32[48,256]{1,0:T(8,128)S(1)}, f32[24,256]{1,0:T(8,128)S(1)}, f32[24,256]{1,0:T(8,128)S(1)}, /*index=5*/f32[3,6144]{1,0:T(4,128)}) custom-call(f32[6,128,256]{2,1,0:T(8,128)S(1)} %get-tuple-element.88.refs_0_, f32[3,128,256]{2,1,0:T(8,128)S(1)} %get-tuple-element.82.refs_1_, ...), custom_call_target="tpu_custom_call" | custom-call | tf_op jit(solution)/shard_map/velocity_2/pallas_call | solution.py:448
  81.5 2.2 %collective-permute-start.26 = (f32[24,256]{1,0:T(8,128)S(1)}, f32[24,256]{1,0:T(8,128)S(1)}, u32[]{:S(2)}, u32[]{:S(2)}) collective-permute-start(f32[24,256]{1,0:T(8,128)S(1)} %get-tuple-element.99), channel_id=1, source_target_pairs={{0,3},{1,2},{2,1},{3,0},{4,7},{5,6},{6,5},{7,4},{8,11},{9,10},{10,... | collective-permute-start | bytes 73736 | tf_op jit(solution)/shard_map/ppermute | solution.py:476
  83.6 1.7 %collective-permute-done.25.refs_5_ = f32[24,256]{1,0:T(8,128)S(1)} collective-permute-done((f32[24,256]{1,0:T(8,128)S(1)}, f32[24,256]{1,0:T(8,128)S(1)}, u32[]{:S(2)}, u32[]{:S(2)}) %collective-permute-start.25) | collective-permute-done | bytes 24608 | tf_op jit(solution)/shard_map/ppermute | solution.py:477
  85.3 1.8 %collective-permute-done.26.refs_6_ = f32[24,256]{1,0:T(8,128)S(1)} collective-permute-done((f32[24,256]{1,0:T(8,128)S(1)}, f32[24,256]{1,0:T(8,128)S(1)}, u32[]{:S(2)}, u32[]{:S(2)}) %collective-permute-start.26) | collective-permute-done | bytes 24608 | tf_op jit(solution)/shard_map/ppermute | solution.py:476
  87.1 1.0 %copy-done.2 = f32[3,128,256]{2,1,0:T(8,128)S(1)} copy-done((f32[3,128,256]{2,1,0:T(8,128)S(1)}, f32[3,128,256]{2,1,0:T(8,128)}, u32[]{:S(2)}) %copy-start.2) | copy-done | bytes 393240
  88.1 1.4 %stress_2.1 = f32[6,128,256]{2,1,0:T(8,128)} custom-call(f32[6,128,256]{2,1,0:T(8,128)S(1)} %get-tuple-element.88.refs_0_, f32[3,128,256]{2,1,0:T(8,128)S(1)} %copy-done.2, s32[128,256]{1,0:T(8,128)S(1)} %get-tuple-element.64.refs_2_, f32[48,256]{1,0:T(8,128)S(1)} %collective-permute-done.23.refs_3_, f32[48,256]{1,0:T(8,128)S(1)} %collective-permute-done.24.refs_4_, ...), custom_call_target="tpu_custom_call" | custom-call | tf_op jit(solution)/shard_map/stress_2/pallas_call | solution.py:448
  (49 shorter events, 9.7 us)
Async XLA Ops:
  1.3 1.1 %copy-start = (f32[6,8,16,256]{3,2,1,0:T(8,128)S(1)}, f32[6,8,16,256]{3,2,1,0:T(8,128)}, u32[]{:S(2)}) copy-start(f32[6,8,16,256]{3,2,1,0:T(8,128)} %param.9) | copy-start | bytes 2359300
  2.5 1.0 %copy-start.1 = (f32[3,8,16,256]{3,2,1,0:T(8,128)S(1)}, f32[3,8,16,256]{3,2,1,0:T(8,128)}, u32[]{:S(2)}) copy-start(f32[3,8,16,256]{3,2,1,0:T(8,128)} %param.10) | copy-start | bytes 1179652
  3.5 0.9 %copy-start.3 = (f32[8,16,256]{2,1,0:T(8,128)S(1)}, f32[8,16,256]{2,1,0:T(8,128)}, u32[]{:S(2)}) copy-start(f32[8,16,256]{2,1,0:T(8,128)} %param.11) | copy-start | bytes 393220
  4.4 0.9 %copy-start.4 = (s32[8,16,256]{2,1,0:T(8,128)S(1)}, s32[8,16,256]{2,1,0:T(8,128)}, u32[]{:S(2)}) copy-start(s32[8,16,256]{2,1,0:T(8,128)} %param.12) | copy-start | bytes 393220
  11.0 13.5 %collective-permute-start = (f32[120,256]{1,0:T(8,128)S(1)}, f32[120,256]{1,0:T(8,128)S(1)}, u32[]{:S(2)}, u32[]{:S(2)}) collective-permute-start(f32[120,256]{1,0:T(8,128)S(1)} %get-tuple-element.58), channel_id=1, source_target_pairs={{0,4},{4,0},{8,12},{12,8},{16,20},{20,16},{24,28},{28,24},{1,5},{5... | collective-permute-start | bytes 368648 | tf_op jit(solution)/shard_map/ppermute | solution.py:479
  11.5 13.0 %collective-permute-start.1 = (f32[120,256]{1,0:T(8,128)S(1)}, f32[120,256]{1,0:T(8,128)S(1)}, u32[]{:S(2)}, u32[]{:S(2)}) collective-permute-start(f32[120,256]{1,0:T(8,128)S(1)} %get-tuple-element.59), channel_id=1, source_target_pairs={{0,28},{4,8},{8,4},{12,16},{16,12},{20,24},{24,20},{28,0},{1,29},{... | collective-permute-start | bytes 368648 | tf_op jit(solution)/shard_map/ppermute | solution.py:478
  15.1 9.4 %collective-permute-start.2 = (f32[64,256]{1,0:T(8,128)S(1)}, f32[64,256]{1,0:T(8,128)S(1)}, u32[]{:S(2)}, u32[]{:S(2)}) collective-permute-start(f32[64,256]{1,0:T(8,128)S(1)} %get-tuple-element.60), channel_id=1, source_target_pairs={{0,1},{1,0},{2,3},{3,2},{4,5},{5,4},{6,7},{7,6},{8,9},{9,8},{10,11... | collective-permute-start | bytes 196616 | tf_op jit(solution)/shard_map/ppermute | solution.py:477
  16.6 7.8 %collective-permute-start.3 = (f32[64,256]{1,0:T(8,128)S(1)}, f32[64,256]{1,0:T(8,128)S(1)}, u32[]{:S(2)}, u32[]{:S(2)}) collective-permute-start(f32[64,256]{1,0:T(8,128)S(1)} %get-tuple-element.61), channel_id=1, source_target_pairs={{0,3},{1,2},{2,1},{3,0},{4,7},{5,6},{6,5},{7,4},{8,11},{9,10},{10,... | collective-permute-start | bytes 196616 | tf_op jit(solution)/shard_map/ppermute | solution.py:476
  19.1 5.3 %collective-permute-start.4 = (f32[40,256]{1,0:T(8,128)S(1)}, f32[40,256]{1,0:T(8,128)S(1)}, u32[]{:S(2)}, u32[]{:S(2)}) collective-permute-start(f32[40,256]{1,0:T(8,128)S(1)} %get-tuple-element.57.refs_5_), channel_id=1, source_target_pairs={{0,2},{1,3},{2,0},{3,1},{4,6},{5,7},{6,4},{7,5},{8,10},{9,11},{10,... | collective-permute-start | bytes 122888 | tf_op jit(solution)/shard_map/ppermute | solution.py:485
  33.1 8.2 %collective-permute-start.5 = (f32[144,256]{1,0:T(8,128)S(1)}, f32[144,256]{1,0:T(8,128)S(1)}, u32[]{:S(2)}, u32[]{:S(2)}) collective-permute-start(f32[144,256]{1,0:T(8,128)S(1)} %get-tuple-element.65), channel_id=1, source_target_pairs={{0,4},{4,0},{8,12},{12,8},{16,20},{20,16},{24,28},{28,24},{1,5},{5... | collective-permute-start | bytes 442376 | tf_op jit(solution)/shard_map/ppermute | solution.py:479
  33.2 8.1 %collective-permute-start.6 = (f32[144,256]{1,0:T(8,128)S(1)}, f32[144,256]{1,0:T(8,128)S(1)}, u32[]{:S(2)}, u32[]{:S(2)}) collective-permute-start(f32[144,256]{1,0:T(8,128)S(1)} %get-tuple-element.66), channel_id=1, source_target_pairs={{0,28},{4,8},{8,4},{12,16},{16,12},{20,24},{24,20},{28,0},{1,29},{... | collective-permute-start | bytes 442376 | tf_op jit(solution)/shard_map/ppermute | solution.py:478
  34.0 7.3 %collective-permute-start.7 = (f32[48,256]{1,0:T(8,128)S(1)}, f32[48,256]{1,0:T(8,128)S(1)}, u32[]{:S(2)}, u32[]{:S(2)}) collective-permute-start(f32[48,256]{1,0:T(8,128)S(1)} %get-tuple-element.67), channel_id=1, source_target_pairs={{0,1},{1,0},{2,3},{3,2},{4,5},{5,4},{6,7},{7,6},{8,9},{9,8},{10,11... | collective-permute-start | bytes 147464 | tf_op jit(solution)/shard_map/ppermute | solution.py:477
  34.0 7.3 %collective-permute-start.8 = (f32[48,256]{1,0:T(8,128)S(1)}, f32[48,256]{1,0:T(8,128)S(1)}, u32[]{:S(2)}, u32[]{:S(2)}) collective-permute-start(f32[48,256]{1,0:T(8,128)S(1)} %get-tuple-element.68), channel_id=1, source_target_pairs={{0,3},{1,2},{2,1},{3,0},{4,7},{5,6},{6,5},{7,4},{8,11},{9,10},{10,... | collective-permute-start | bytes 147464 | tf_op jit(solution)/shard_map/ppermute | solution.py:476
  36.6 4.7 %collective-permute-start.9 = (f32[24,256]{1,0:T(8,128)S(1)}, f32[24,256]{1,0:T(8,128)S(1)}, u32[]{:S(2)}, u32[]{:S(2)}) collective-permute-start(f32[24,256]{1,0:T(8,128)S(1)} %get-tuple-element.69.refs_8_.refs_5_), channel_id=1, source_target_pairs={{0,2},{1,3},{2,0},{3,1},{4,6},{5,7},{6,4},{7,5},{8,10},{9,11},{10,... | collective-permute-start | bytes 73736 | tf_op jit(solution)/shard_map/ppermute | solution.py:485
  44.9 8.6 %collective-permute-start.10 = (f32[192,256]{1,0:T(8,128)S(1)}, f32[192,256]{1,0:T(8,128)S(1)}, u32[]{:S(2)}, u32[]{:S(2)}) collective-permute-start(f32[192,256]{1,0:T(8,128)S(1)} %get-tuple-element.75), channel_id=1, source_target_pairs={{0,4},{4,0},{8,12},{12,8},{16,20},{20,16},{24,28},{28,24},{1,5},{5... | collective-permute-start | bytes 589832 | tf_op jit(solution)/shard_map/ppermute | solution.py:479
  45.2 8.3 %collective-permute-start.11 = (f32[192,256]{1,0:T(8,128)S(1)}, f32[192,256]{1,0:T(8,128)S(1)}, u32[]{:S(2)}, u32[]{:S(2)}) collective-permute-start(f32[192,256]{1,0:T(8,128)S(1)} %get-tuple-element.76), channel_id=1, source_target_pairs={{0,28},{4,8},{8,4},{12,16},{16,12},{20,24},{24,20},{28,0},{1,29},{... | collective-permute-start | bytes 589832 | tf_op jit(solution)/shard_map/ppermute | solution.py:478
  47.0 3.8 %collective-permute-start.12 = (f32[24,256]{1,0:T(8,128)S(1)}, f32[24,256]{1,0:T(8,128)S(1)}, u32[]{:S(2)}, u32[]{:S(2)}) collective-permute-start(f32[24,256]{1,0:T(8,128)S(1)} %get-tuple-element.77), channel_id=1, source_target_pairs={{0,1},{1,0},{2,3},{3,2},{4,5},{5,4},{6,7},{7,6},{8,9},{9,8},{10,11... | collective-permute-start | bytes 73736 | tf_op jit(solution)/shard_map/ppermute | solution.py:477
  47.9 5.6 %collective-permute-start.13 = (f32[24,256]{1,0:T(8,128)S(1)}, f32[24,256]{1,0:T(8,128)S(1)}, u32[]{:S(2)}, u32[]{:S(2)}) collective-permute-start(f32[24,256]{1,0:T(8,128)S(1)} %get-tuple-element.78), channel_id=1, source_target_pairs={{0,3},{1,2},{2,1},{3,0},{4,7},{5,6},{6,5},{7,4},{8,11},{9,10},{10,... | collective-permute-start | bytes 73736 | tf_op jit(solution)/shard_map/ppermute | solution.py:476
  57.3 8.2 %collective-permute-start.14 = (f32[120,256]{1,0:T(8,128)S(1)}, f32[120,256]{1,0:T(8,128)S(1)}, u32[]{:S(2)}, u32[]{:S(2)}) collective-permute-start(f32[120,256]{1,0:T(8,128)S(1)} %get-tuple-element.83), channel_id=1, source_target_pairs={{0,4},{4,0},{8,12},{12,8},{16,20},{20,16},{24,28},{28,24},{1,5},{5... | collective-permute-start | bytes 368648 | tf_op jit(solution)/shard_map/ppermute | solution.py:479
  57.4 8.1 %collective-permute-start.15 = (f32[120,256]{1,0:T(8,128)S(1)}, f32[120,256]{1,0:T(8,128)S(1)}, u32[]{:S(2)}, u32[]{:S(2)}) collective-permute-start(f32[120,256]{1,0:T(8,128)S(1)} %get-tuple-element.84), channel_id=1, source_target_pairs={{0,28},{4,8},{8,4},{12,16},{16,12},{20,24},{24,20},{28,0},{1,29},{... | collective-permute-start | bytes 368648 | tf_op jit(solution)/shard_map/ppermute | solution.py:478
  58.8 6.6 %collective-permute-start.16 = (f32[48,256]{1,0:T(8,128)S(1)}, f32[48,256]{1,0:T(8,128)S(1)}, u32[]{:S(2)}, u32[]{:S(2)}) collective-permute-start(f32[48,256]{1,0:T(8,128)S(1)} %get-tuple-element.85), channel_id=1, source_target_pairs={{0,1},{1,0},{2,3},{3,2},{4,5},{5,4},{6,7},{7,6},{8,9},{9,8},{10,11... | collective-permute-start | bytes 147464 | tf_op jit(solution)/shard_map/ppermute | solution.py:477
  58.8 6.6 %collective-permute-start.17 = (f32[48,256]{1,0:T(8,128)S(1)}, f32[48,256]{1,0:T(8,128)S(1)}, u32[]{:S(2)}, u32[]{:S(2)}) collective-permute-start(f32[48,256]{1,0:T(8,128)S(1)} %get-tuple-element.86), channel_id=1, source_target_pairs={{0,3},{1,2},{2,1},{3,0},{4,7},{5,6},{6,5},{7,4},{8,11},{9,10},{10,... | collective-permute-start | bytes 147464 | tf_op jit(solution)/shard_map/ppermute | solution.py:476
  60.8 4.7 %collective-permute-start.18 = (f32[24,256]{1,0:T(8,128)S(1)}, f32[24,256]{1,0:T(8,128)S(1)}, u32[]{:S(2)}, u32[]{:S(2)}) collective-permute-start(f32[24,256]{1,0:T(8,128)S(1)} %get-tuple-element.87.refs_8_.refs_5_), channel_id=1, source_target_pairs={{0,2},{1,3},{2,0},{3,1},{4,6},{5,7},{6,4},{7,5},{8,10},{9,11},{10,... | collective-permute-start | bytes 73736 | tf_op jit(solution)/shard_map/ppermute | solution.py:485
  69.2 8.2 %collective-permute-start.19 = (f32[120,256]{1,0:T(8,128)S(1)}, f32[120,256]{1,0:T(8,128)S(1)}, u32[]{:S(2)}, u32[]{:S(2)}) collective-permute-start(f32[120,256]{1,0:T(8,128)S(1)} %get-tuple-element.89), channel_id=1, source_target_pairs={{0,4},{4,0},{8,12},{12,8},{16,20},{20,16},{24,28},{28,24},{1,5},{5... | collective-permute-start | bytes 368648 | tf_op jit(solution)/shard_map/ppermute | solution.py:479
  69.2 8.1 %collective-permute-start.20 = (f32[120,256]{1,0:T(8,128)S(1)}, f32[120,256]{1,0:T(8,128)S(1)}, u32[]{:S(2)}, u32[]{:S(2)}) collective-permute-start(f32[120,256]{1,0:T(8,128)S(1)} %get-tuple-element.90), channel_id=1, source_target_pairs={{0,28},{4,8},{8,4},{12,16},{16,12},{20,24},{24,20},{28,0},{1,29},{... | collective-permute-start | bytes 368648 | tf_op jit(solution)/shard_map/ppermute | solution.py:478
  71.4 3.8 %collective-permute-start.21 = (f32[24,256]{1,0:T(8,128)S(1)}, f32[24,256]{1,0:T(8,128)S(1)}, u32[]{:S(2)}, u32[]{:S(2)}) collective-permute-start(f32[24,256]{1,0:T(8,128)S(1)} %get-tuple-element.91), channel_id=1, source_target_pairs={{0,1},{1,0},{2,3},{3,2},{4,5},{5,4},{6,7},{7,6},{8,9},{9,8},{10,11... | collective-permute-start | bytes 73736 | tf_op jit(solution)/shard_map/ppermute | solution.py:477
  71.7 5.6 %collective-permute-start.22 = (f32[24,256]{1,0:T(8,128)S(1)}, f32[24,256]{1,0:T(8,128)S(1)}, u32[]{:S(2)}, u32[]{:S(2)}) collective-permute-start(f32[24,256]{1,0:T(8,128)S(1)} %get-tuple-element.92), channel_id=1, source_target_pairs={{0,3},{1,2},{2,1},{3,0},{4,7},{5,6},{6,5},{7,4},{8,11},{9,10},{10,... | collective-permute-start | bytes 73736 | tf_op jit(solution)/shard_map/ppermute | solution.py:476
  80.7 6.4 %collective-permute-start.23 = (f32[48,256]{1,0:T(8,128)S(1)}, f32[48,256]{1,0:T(8,128)S(1)}, u32[]{:S(2)}, u32[]{:S(2)}) collective-permute-start(f32[48,256]{1,0:T(8,128)S(1)} %get-tuple-element.96), channel_id=1, source_target_pairs={{0,4},{4,0},{8,12},{12,8},{16,20},{20,16},{24,28},{28,24},{1,5},{5... | collective-permute-start | bytes 147464 | tf_op jit(solution)/shard_map/ppermute | solution.py:479
  80.7 6.4 %collective-permute-start.24 = (f32[48,256]{1,0:T(8,128)S(1)}, f32[48,256]{1,0:T(8,128)S(1)}, u32[]{:S(2)}, u32[]{:S(2)}) collective-permute-start(f32[48,256]{1,0:T(8,128)S(1)} %get-tuple-element.97), channel_id=1, source_target_pairs={{0,28},{4,8},{8,4},{12,16},{16,12},{20,24},{24,20},{28,0},{1,29},{... | collective-permute-start | bytes 147464 | tf_op jit(solution)/shard_map/ppermute | solution.py:478
  81.4 3.8 %collective-permute-start.25 = (f32[24,256]{1,0:T(8,128)S(1)}, f32[24,256]{1,0:T(8,128)S(1)}, u32[]{:S(2)}, u32[]{:S(2)}) collective-permute-start(f32[24,256]{1,0:T(8,128)S(1)} %get-tuple-element.98), channel_id=1, source_target_pairs={{0,1},{1,0},{2,3},{3,2},{4,5},{5,4},{6,7},{7,6},{8,9},{9,8},{10,11... | collective-permute-start | bytes 73736 | tf_op jit(solution)/shard_map/ppermute | solution.py:477
  81.5 5.6 %collective-permute-start.26 = (f32[24,256]{1,0:T(8,128)S(1)}, f32[24,256]{1,0:T(8,128)S(1)}, u32[]{:S(2)}, u32[]{:S(2)}) collective-permute-start(f32[24,256]{1,0:T(8,128)S(1)} %get-tuple-element.99), channel_id=1, source_target_pairs={{0,3},{1,2},{2,1},{3,0},{4,7},{5,6},{6,5},{7,4},{8,11},{9,10},{10,... | collective-permute-start | bytes 73736 | tf_op jit(solution)/shard_map/ppermute | solution.py:476
  87.1 1.0 %copy-start.2 = (f32[3,128,256]{2,1,0:T(8,128)S(1)}, f32[3,128,256]{2,1,0:T(8,128)}, u32[]{:S(2)}) copy-start(f32[3,128,256]{2,1,0:T(8,128)} %get-tuple-element.95.refs_1_) | copy-start | bytes 1179652
  (5 other events, 3.9 us)

commit v3 on v2

--- a/solution.py
+++ b/solution.py
@@ -288,7 +288,8 @@
 
 
 def stress_update(
-    sz, depth, plan, stress, velocity, flags, from_da, from_db, from_pa, from_pb, out
+    sz, depth, plan, stress, velocity, flags, from_da, from_db, from_pa, from_pb, out,
+    plane_done=None,
 ):
     cx, cz = sz.cx, sz.cz
     plane = lambda c, z: velocity[c, z * cx : (z + 1) * cx, :]
@@ -326,6 +327,8 @@
         for c in range(3):
             out[c, here, :] = jnp.where(elastic, trial[c], dev[c] * factor + pressure)
             out[3 + c, here, :] = jnp.where(elastic, sheared[c], sheared[c] * factor)
+        if plane_done is not None:
+            plane_done(z)
 
 
 def window_from(sz, depth, pile, from_da, from_db, offset):
@@ -407,10 +410,27 @@
     stress, velocity, flags, from_da, from_db, from_pa, from_pb = take(7)
     head_d, head_p, pr3 = 3 * sz.cx, 3 * sz.cz, 3 * sz.pr
     if step == STEPS - 1:
-        (out,) = take(1)
+        pile, stress_out, velocity_out, pile_out, out, sems = take(6)
+        copies = [
+            pltpu.make_async_copy(velocity, velocity_out, sems.at[sz.cz]),
+            pltpu.make_async_copy(pile, pile_out, sems.at[sz.cz + 1]),
+        ]
+        for copy in copies:
+            copy.start()
+
+        def plane_done(z):
+            part = (slice(None), pl.ds(z * sz.cx, sz.cx), slice(None))
+            copies.append(
+                pltpu.make_async_copy(out.at[part], stress_out.at[part], sems.at[z])
+            )
+            copies[-1].start()
+
         stress_update(
-            sz, depth, plan, stress, velocity, flags, from_da, from_db, from_pa, from_pb, out
+            sz, depth, plan, stress, velocity, flags, from_da, from_db, from_pa, from_pb, out,
+            plane_done,
         )
+        for copy in copies:
+            copy.wait()
         return
     from_others = take(max(sz.np - 3, 0))
     own, set_ids = take(2)
@@ -442,18 +462,18 @@
     send_edges(sz, depth, plan, DEPTH_PART, PLAN_PART, plane, (to_da, to_db, to_pa, to_pb))
 
 
-def call(body, name, ins, outs, scratch=(), copies=0):
-    vmem = pl.BlockSpec(memory_space=pltpu.VMEM)
+def call(body, name, ins, outs, scratch=(), copies=0, far_ins=False, far_outs=False):
+    vmem, far = pl.BlockSpec(memory_space=pltpu.VMEM), pl.BlockSpec(memory_space=pl.ANY)
     sems = [pltpu.SemaphoreType.DMA((copies,))] if copies else []
     return pl.pallas_call(
         body,
         out_shape=[jax.ShapeDtypeStruct(shape, dtype) for shape, dtype in outs],
-        in_specs=[pl.BlockSpec(memory_space=pl.ANY) if copies else vmem] * len(ins),
-        out_specs=[vmem] * len(outs),
+        in_specs=[far if far_ins else vmem] * len(ins),
+        out_specs=[far if far_outs else vmem] * len(outs),
         scratch_shapes=[pltpu.VMEM(shape, dtype) for shape, dtype in scratch] + sems,
         compiler_params=pltpu.CompilerParams(vmem_limit_bytes=48 * 2**20),
         name=name,
-    )(*ins)
+    )(*[pltpu.with_memory_space_constraint(x, pltpu.HBM) if far_ins else x for x in ins])
 
 
 def matchings(count):
@@ -515,6 +535,7 @@
         + [(pile_velocity.shape, F32), ((1, sz.pile), F32), (jack_force.shape, F32)]
         + [(pair_elem.shape, I32), (pair_cell.shape, I32)],
         copies=9,
+        far_ins=True,
     )
     at_cells, cell_ids, elem_ids, pile, mass, jack = to[4:10]
     stress, velocity, density, flags = to[10:]
@@ -583,13 +604,16 @@
         [((3, rows, cy), F32)] + edges(0, 0) + [(pile_velocity.shape, F32)],
         tables + cells + [((pr3, COLS), F32)],
     )
-    velocity, pile_velocity = first[0], first[5]
+    velocity, pile_out = first[0], first[5]
     got = swap(*first[1:5])
-    (stress,) = call(
+    stress, velocity, pile_velocity = call(
         functools.partial(stress_kernel, sz, 2),
         "stress_2",
-        [stress, velocity, flags, *got],
-        [((6, rows, cy), F32)],
+        [stress, velocity, flags, *got, pile_out],
+        [(stress.shape, F32), (velocity.shape, F32), (pile_velocity.shape, F32)],
+        [(stress.shape, F32)],
+        copies=cz + 2,
+        far_outs=True,
     )
     return stress.reshape(full_shape[0]), velocity.reshape(full_shape[1]), pile_velocity
 

time: 90 us -> 80.3 us (0.89)
  local copies, waits for them, and re-layouts: 8.84 us -> 0 us
    unnamed x20 -> x0, local copies, waits for them, and re-layouts: 8.84 us -> none
    pallas_call x7, Pallas kernels: 26.9 us -> 26 us  [call(): pl.pallas_call(body, out_shape=[jax.ShapeDtypeStruct(shape, dtype) for sh...]
where the time goes in v3:
time: 80.3 us; the launch traced here: 80.1 us
  starting transfers between devices  29.6 us (37%)
  Pallas kernels  26 us (32%)
  waiting for transfers between devices  23.6 us (29%)
  between operations  0.93 us (1%)
    pallas_call x7, Pallas kernels, call(): pl.pallas_call(body, out_shape=[jax.ShapeDtypeStruct(shape, dtype) for sh...  26 us
    ppermute x6, starting transfers between devices, swap(): pb = lax.ppermute(pb, 'plan', p_second)  12.4 us
    ppermute x3, waiting for transfers between devices, to_others(): lax.ppermute(x, 'plan', [(i, (i + s) % sz.np) for i in range(sz.np)])  12.2 us
    ppermute x6, starting transfers between devices, swap(): db = lax.ppermute(db, 'depth', d_second)  10.6 us
    ppermute x6, waiting for transfers between devices, swap(): pb = lax.ppermute(pb, 'plan', p_second)  6.63 us
    ppermute x6, waiting for transfers between devices, swap(): pa = lax.ppermute(pa, 'plan', p_first)  4.75 us
    ppermute x6, starting transfers between devices, swap(): pa = lax.ppermute(pa, 'plan', p_first)  2.86 us
    ppermute x3, starting transfers between devices, to_others(): lax.ppermute(x, 'plan', [(i, (i + s) % sz.np) for i in range(sz.np)])  2.6 us
  transfers between devices with their start and end apart: 27, of which 9 were waited for; matrix products, arithmetic and copies ran while one was open for 0% of the time, Pallas kernels for 0%

profile of v3, /device:TPU:0, one launch (start us, length us, event | category | flops | bytes accessed | tf_op | source)
XLA Modules:
  0.0 80.1 jit_solution(17907681323045714402)
XLA Ops:
  0.6 2.5 %first.1 = (f32[120,256]{1,0:T(8,128)S(1)}, f32[120,256]{1,0:T(8,128)S(1)}, f32[64,256]{1,0:T(8,128)S(1)}, f32[64,256]{1,0:T(8,128)S(1)}, f32[40,256]{1,0:T(8,12...) custom-call(s32[1,2048]{1,0:T(1,128)} %refs_0_.1, ...), custom_call_target="tpu_custom_call" | custom-call | tf_op jit(solution)/shard_map/first/pallas_call | solution.py:468
  3.7 3.6 %collective-permute-start.1 = (f32[120,256]{1,0:T(8,128)S(1)}, f32[120,256]{1,0:T(8,128)S(1)}, u32[]{:S(2)}, u32[]{:S(2)}) collective-permute-start(f32[120,256]{1,0:T(8,128)S(1)} %get-tuple-element.62), channel_id=1, source_target_pairs={{0,28},{4,8},{8,4},{12,16},{16,12},{20,24},{24,20},{28,0},{1,29},{... | collective-permute-start | bytes 368648 | tf_op jit(solution)/shard_map/ppermute | solution.py:498
  7.3 1.6 %collective-permute-start.2 = (f32[64,256]{1,0:T(8,128)S(1)}, f32[64,256]{1,0:T(8,128)S(1)}, u32[]{:S(2)}, u32[]{:S(2)}) collective-permute-start(f32[64,256]{1,0:T(8,128)S(1)} %get-tuple-element.63), channel_id=1, source_target_pairs={{0,1},{1,0},{2,3},{3,2},{4,5},{5,4},{6,7},{7,6},{8,9},{9,8},{10,11... | collective-permute-start | bytes 196616 | tf_op jit(solution)/shard_map/ppermute | solution.py:497
  8.8 2.5 %collective-permute-start.3 = (f32[64,256]{1,0:T(8,128)S(1)}, f32[64,256]{1,0:T(8,128)S(1)}, u32[]{:S(2)}, u32[]{:S(2)}) collective-permute-start(f32[64,256]{1,0:T(8,128)S(1)} %get-tuple-element.64), channel_id=1, source_target_pairs={{0,3},{1,2},{2,1},{3,0},{4,7},{5,6},{6,5},{7,4},{8,11},{9,10},{10,... | collective-permute-start | bytes 196616 | tf_op jit(solution)/shard_map/ppermute | solution.py:496
  11.4 5.2 %collective-permute-done.4.refs_10_ = f32[40,256]{1,0:T(8,128)S(1)} collective-permute-done((f32[40,256]{1,0:T(8,128)S(1)}, f32[40,256]{1,0:T(8,128)S(1)}, u32[]{:S(2)}, u32[]{:S(2)}) %collective-permute-start.4) | collective-permute-done | bytes 40992 | tf_op jit(solution)/shard_map/ppermute | solution.py:505
  16.7 8.6 %velocity_0.1 = (f32[3,128,256]{2,1,0:T(8,128)S(1)}, f32[144,256]{1,0:T(8,128)S(1)}, f32[144,256]{1,0:T(8,128)S(1)}, f32[48,256]{1,0:T(8,128)S(1)}, f32[48,256]{...) custom-call(f32[6,128,256]{2,1,0:T(8,128)S(1)} %get-tuple-element.55.refs_0_, ...), custom_call_target="tpu_custom_call" | custom-call | tf_op jit(solution)/shard_map/velocity_0/pallas_call | solution.py:468
  25.3 0.8 %collective-permute-start.6 = (f32[144,256]{1,0:T(8,128)S(1)}, f32[144,256]{1,0:T(8,128)S(1)}, u32[]{:S(2)}, u32[]{:S(2)}) collective-permute-start(f32[144,256]{1,0:T(8,128)S(1)} %get-tuple-element.69), channel_id=1, source_target_pairs={{0,28},{4,8},{8,4},{12,16},{16,12},{20,24},{24,20},{28,0},{1,29},{... | collective-permute-start | bytes 442376 | tf_op jit(solution)/shard_map/ppermute | solution.py:498
  26.2 2.5 %collective-permute-start.8 = (f32[48,256]{1,0:T(8,128)S(1)}, f32[48,256]{1,0:T(8,128)S(1)}, u32[]{:S(2)}, u32[]{:S(2)}) collective-permute-start(f32[48,256]{1,0:T(8,128)S(1)} %get-tuple-element.71), channel_id=1, source_target_pairs={{0,3},{1,2},{2,1},{3,0},{4,7},{5,6},{6,5},{7,4},{8,11},{9,10},{10,... | collective-permute-start | bytes 147464 | tf_op jit(solution)/shard_map/ppermute | solution.py:496
  28.7 0.9 %collective-permute-start.9 = (f32[24,256]{1,0:T(8,128)S(1)}, f32[24,256]{1,0:T(8,128)S(1)}, u32[]{:S(2)}, u32[]{:S(2)}) collective-permute-start(f32[24,256]{1,0:T(8,128)S(1)} %get-tuple-element.72.refs_8_.refs_5_), channel_id=1, source_target_pairs={{0,2},{1,3},{2,0},{3,1},{4,6},{5,7},{6,4},{7,5},{8,10},{9,11},{10,... | collective-permute-start | bytes 73736 | tf_op jit(solution)/shard_map/ppermute | solution.py:505
  29.6 3.8 %collective-permute-done.9.refs_7_ = f32[24,256]{1,0:T(8,128)S(1)} collective-permute-done((f32[24,256]{1,0:T(8,128)S(1)}, f32[24,256]{1,0:T(8,128)S(1)}, u32[]{:S(2)}, u32[]{:S(2)}) %collective-permute-start.9) | collective-permute-done | bytes 24608 | tf_op jit(solution)/shard_map/ppermute | solution.py:505
  33.5 3.6 %stress_0.1 = (f32[6,128,256]{2,1,0:T(8,128)S(1)}, f32[192,256]{1,0:T(8,128)S(1)}, f32[192,256]{1,0:T(8,128)S(1)}, f32[24,256]{1,0:T(8,128)S(1)}, f32[24,256]{1,...) custom-call(f32[6,128,256]{2,1,0:T(8,128)S(1)} %get-tuple-element.55.refs_0_, ...), custom_call_target="tpu_custom_call" | custom-call | tf_op jit(solution)/shard_map/stress_0/pallas_call | solution.py:468
  37.3 1.8 %collective-permute-start.11 = (f32[192,256]{1,0:T(8,128)S(1)}, f32[192,256]{1,0:T(8,128)S(1)}, u32[]{:S(2)}, u32[]{:S(2)}) collective-permute-start(f32[192,256]{1,0:T(8,128)S(1)} %get-tuple-element.79), channel_id=1, source_target_pairs={{0,28},{4,8},{8,4},{12,16},{16,12},{20,24},{24,20},{28,0},{1,29},{... | collective-permute-start | bytes 589832 | tf_op jit(solution)/shard_map/ppermute | solution.py:498
  39.1 0.9 %collective-permute-start.12 = (f32[24,256]{1,0:T(8,128)S(1)}, f32[24,256]{1,0:T(8,128)S(1)}, u32[]{:S(2)}, u32[]{:S(2)}) collective-permute-start(f32[24,256]{1,0:T(8,128)S(1)} %get-tuple-element.80), channel_id=1, source_target_pairs={{0,1},{1,0},{2,3},{3,2},{4,5},{5,4},{6,7},{7,6},{8,9},{9,8},{10,11... | collective-permute-start | bytes 73736 | tf_op jit(solution)/shard_map/ppermute | solution.py:497
  40.0 1.5 %collective-permute-start.13 = (f32[24,256]{1,0:T(8,128)S(1)}, f32[24,256]{1,0:T(8,128)S(1)}, u32[]{:S(2)}, u32[]{:S(2)}) collective-permute-start(f32[24,256]{1,0:T(8,128)S(1)} %get-tuple-element.81), channel_id=1, source_target_pairs={{0,3},{1,2},{2,1},{3,0},{4,7},{5,6},{6,5},{7,4},{8,11},{9,10},{10,... | collective-permute-start | bytes 73736 | tf_op jit(solution)/shard_map/ppermute | solution.py:496
  41.6 1.3 %collective-permute-done.12.refs_8_ = f32[24,256]{1,0:T(8,128)S(1)} collective-permute-done((f32[24,256]{1,0:T(8,128)S(1)}, f32[24,256]{1,0:T(8,128)S(1)}, u32[]{:S(2)}, u32[]{:S(2)}) %collective-permute-start.12) | collective-permute-done | bytes 24608 | tf_op jit(solution)/shard_map/ppermute | solution.py:497
  42.9 2.7 %collective-permute-done.13.refs_9_ = f32[24,256]{1,0:T(8,128)S(1)} collective-permute-done((f32[24,256]{1,0:T(8,128)S(1)}, f32[24,256]{1,0:T(8,128)S(1)}, u32[]{:S(2)}, u32[]{:S(2)}) %collective-permute-start.13) | collective-permute-done | bytes 24608 | tf_op jit(solution)/shard_map/ppermute | solution.py:496
  45.6 3.8 %velocity_1.1 = (f32[3,128,256]{2,1,0:T(8,128)S(1)}, f32[120,256]{1,0:T(8,128)S(1)}, f32[120,256]{1,0:T(8,128)S(1)}, f32[48,256]{1,0:T(8,128)S(1)}, f32[48,256]{...) custom-call(f32[6,128,256]{2,1,0:T(8,128)S(1)} %get-tuple-element.77.refs_0_, ...), custom_call_target="tpu_custom_call" | custom-call | tf_op jit(solution)/shard_map/velocity_1/pallas_call | solution.py:468
  49.5 1.4 %collective-permute-start.15 = (f32[120,256]{1,0:T(8,128)S(1)}, f32[120,256]{1,0:T(8,128)S(1)}, u32[]{:S(2)}, u32[]{:S(2)}) collective-permute-start(f32[120,256]{1,0:T(8,128)S(1)} %get-tuple-element.87), channel_id=1, source_target_pairs={{0,28},{4,8},{8,4},{12,16},{16,12},{20,24},{24,20},{28,0},{1,29},{... | collective-permute-start | bytes 368648 | tf_op jit(solution)/shard_map/ppermute | solution.py:498
  51.0 1.9 %collective-permute-start.17 = (f32[48,256]{1,0:T(8,128)S(1)}, f32[48,256]{1,0:T(8,128)S(1)}, u32[]{:S(2)}, u32[]{:S(2)}) collective-permute-start(f32[48,256]{1,0:T(8,128)S(1)} %get-tuple-element.89), channel_id=1, source_target_pairs={{0,3},{1,2},{2,1},{3,0},{4,7},{5,6},{6,5},{7,4},{8,11},{9,10},{10,... | collective-permute-start | bytes 147464 | tf_op jit(solution)/shard_map/ppermute | solution.py:496
  52.9 1.6 %collective-permute-start.18 = (f32[24,256]{1,0:T(8,128)S(1)}, f32[24,256]{1,0:T(8,128)S(1)}, u32[]{:S(2)}, u32[]{:S(2)}) collective-permute-start(f32[24,256]{1,0:T(8,128)S(1)} %get-tuple-element.90.refs_8_.refs_5_), channel_id=1, source_target_pairs={{0,2},{1,3},{2,0},{3,1},{4,6},{5,7},{6,4},{7,5},{8,10},{9,11},{10,... | collective-permute-start | bytes 73736 | tf_op jit(solution)/shard_map/ppermute | solution.py:505
  54.5 3.1 %collective-permute-done.18.refs_7_ = f32[24,256]{1,0:T(8,128)S(1)} collective-permute-done((f32[24,256]{1,0:T(8,128)S(1)}, f32[24,256]{1,0:T(8,128)S(1)}, u32[]{:S(2)}, u32[]{:S(2)}) %collective-permute-start.18) | collective-permute-done | bytes 24608 | tf_op jit(solution)/shard_map/ppermute | solution.py:505
  57.6 3.6 %stress_1.1 = (f32[6,128,256]{2,1,0:T(8,128)S(1)}, f32[120,256]{1,0:T(8,128)S(1)}, f32[120,256]{1,0:T(8,128)S(1)}, f32[24,256]{1,0:T(8,128)S(1)}, f32[24,256]{1,0:T(8,128)S(1)}, /*index=5*/f32[72,256]{1,0:T(8,128)S(1)}) custom-call(f32[6,128,256]{2,1,0:T(8,128)S(1)} %get-tuple-element.77.refs_0_, f32[3,128,256]{2,1,0:T(8,128)S(1)} %get-tuple-element.85.refs_1_, ...), custom_call_target="tpu_custom_call" | custom-call | tf_op jit(solution)/shard_map/stress_1/pallas_call | solution.py:468
  61.3 2.2 %collective-permute-start.20 = (f32[120,256]{1,0:T(8,128)S(1)}, f32[120,256]{1,0:T(8,128)S(1)}, u32[]{:S(2)}, u32[]{:S(2)}) collective-permute-start(f32[120,256]{1,0:T(8,128)S(1)} %get-tuple-element.93), channel_id=1, source_target_pairs={{0,28},{4,8},{8,4},{12,16},{16,12},{20,24},{24,20},{28,0},{1,29},{... | collective-permute-start | bytes 368648 | tf_op jit(solution)/shard_map/ppermute | solution.py:498
  63.8 1.9 %collective-permute-start.22 = (f32[24,256]{1,0:T(8,128)S(1)}, f32[24,256]{1,0:T(8,128)S(1)}, u32[]{:S(2)}, u32[]{:S(2)}) collective-permute-start(f32[24,256]{1,0:T(8,128)S(1)} %get-tuple-element.95), channel_id=1, source_target_pairs={{0,3},{1,2},{2,1},{3,0},{4,7},{5,6},{6,5},{7,4},{8,11},{9,10},{10,... | collective-permute-start | bytes 73736 | tf_op jit(solution)/shard_map/ppermute | solution.py:496
  65.7 1.6 %collective-permute-done.21.refs_8_ = f32[24,256]{1,0:T(8,128)S(1)} collective-permute-done((f32[24,256]{1,0:T(8,128)S(1)}, f32[24,256]{1,0:T(8,128)S(1)}, u32[]{:S(2)}, u32[]{:S(2)}) %collective-permute-start.21) | collective-permute-done | bytes 24608 | tf_op jit(solution)/shard_map/ppermute | solution.py:497
  67.3 2.1 %collective-permute-done.22.refs_9_ = f32[24,256]{1,0:T(8,128)S(1)} collective-permute-done((f32[24,256]{1,0:T(8,128)S(1)}, f32[24,256]{1,0:T(8,128)S(1)}, u32[]{:S(2)}, u32[]{:S(2)}) %collective-permute-start.22) | collective-permute-done | bytes 24608 | tf_op jit(solution)/shard_map/ppermute | solution.py:496
  69.4 2.6 %velocity_2.1 = (f32[3,128,256]{2,1,0:T(8,128)S(1)}, f32[48,256]{1,0:T(8,128)S(1)}, f32[48,256]{1,0:T(8,128)S(1)}, f32[24,256]{1,0:T(8,128)S(1)}, f32[24,256]{1,0:T(8,128)S(1)}, /*index=5*/f32[3,6144]{1,0:T(4,128)S(1)}) custom-call(f32[6,128,256]{2,1,0:T(8,128)S(1)} %get-tuple-element.91.refs_0_, f32[3,128,256]{2,1,0:T(8,128)S(1)} %get-tuple-element.85.refs_1_, ...), custom_call_target="tpu_custom_call" | custom-call | tf_op jit(solution)/shard_map/velocity_2/pallas_call | solution.py:468
  72.1 0.9 %collective-permute-start.24 = (f32[48,256]{1,0:T(8,128)S(1)}, f32[48,256]{1,0:T(8,128)S(1)}, u32[]{:S(2)}, u32[]{:S(2)}) collective-permute-start(f32[48,256]{1,0:T(8,128)S(1)} %get-tuple-element.100), channel_id=1, source_target_pairs={{0,28},{4,8},{8,4},{12,16},{16,12},{20,24},{24,20},{28,0},{1,29},{... | collective-permute-start | bytes 147464 | tf_op jit(solution)/shard_map/ppermute | solution.py:498
  73.0 2.1 %collective-permute-start.26 = (f32[24,256]{1,0:T(8,128)S(1)}, f32[24,256]{1,0:T(8,128)S(1)}, u32[]{:S(2)}, u32[]{:S(2)}) collective-permute-start(f32[24,256]{1,0:T(8,128)S(1)} %get-tuple-element.102), channel_id=1, source_target_pairs={{0,3},{1,2},{2,1},{3,0},{4,7},{5,6},{6,5},{7,4},{8,11},{9,10},{10,... | collective-permute-start | bytes 73736 | tf_op jit(solution)/shard_map/ppermute | solution.py:496
  75.1 1.8 %collective-permute-done.25.refs_5_ = f32[24,256]{1,0:T(8,128)S(1)} collective-permute-done((f32[24,256]{1,0:T(8,128)S(1)}, f32[24,256]{1,0:T(8,128)S(1)}, u32[]{:S(2)}, u32[]{:S(2)}) %collective-permute-start.25) | collective-permute-done | bytes 24608 | tf_op jit(solution)/shard_map/ppermute | solution.py:497
  76.8 1.8 %collective-permute-done.26.refs_6_ = f32[24,256]{1,0:T(8,128)S(1)} collective-permute-done((f32[24,256]{1,0:T(8,128)S(1)}, f32[24,256]{1,0:T(8,128)S(1)}, u32[]{:S(2)}, u32[]{:S(2)}) %collective-permute-start.26) | collective-permute-done | bytes 24608 | tf_op jit(solution)/shard_map/ppermute | solution.py:496
  78.6 1.3 %stress_2.1 = (f32[6,128,256]{2,1,0:T(8,128)}, f32[3,128,256]{2,1,0:T(8,128)}, f32[3,6144]{1,0:T(4,128)}) custom-call(f32[6,128,256]{2,1,0:T(8,128)S(1)} %get-tuple-element.91.refs_0_, f32[3,128,256]{2,1,0:T(8,128)S(1)} %get-tuple-element.98.refs_1_, s32[128,256]{1,0:T(8,128)S(1)} %get-tuple-element.67.refs_2_, ...), custom_call_target="tpu_custom_call" | custom-call | tf_op jit(solution)/shard_map/stress_2/pallas_call | solution.py:468
  (29 shorter events, 1.6 us)
Async XLA Ops:
  3.1 13.5 %collective-permute-start = (f32[120,256]{1,0:T(8,128)S(1)}, f32[120,256]{1,0:T(8,128)S(1)}, u32[]{:S(2)}, u32[]{:S(2)}) collective-permute-start(f32[120,256]{1,0:T(8,128)S(1)} %get-tuple-element.61), channel_id=1, source_target_pairs={{0,4},{4,0},{8,12},{12,8},{16,20},{20,16},{24,28},{28,24},{1,5},{5... | collective-permute-start | bytes 368648 | tf_op jit(solution)/shard_map/ppermute | solution.py:499
  3.7 13.0 %collective-permute-start.1 = (f32[120,256]{1,0:T(8,128)S(1)}, f32[120,256]{1,0:T(8,128)S(1)}, u32[]{:S(2)}, u32[]{:S(2)}) collective-permute-start(f32[120,256]{1,0:T(8,128)S(1)} %get-tuple-element.62), channel_id=1, source_target_pairs={{0,28},{4,8},{8,4},{12,16},{16,12},{20,24},{24,20},{28,0},{1,29},{... | collective-permute-start | bytes 368648 | tf_op jit(solution)/shard_map/ppermute | solution.py:498
  7.3 9.4 %collective-permute-start.2 = (f32[64,256]{1,0:T(8,128)S(1)}, f32[64,256]{1,0:T(8,128)S(1)}, u32[]{:S(2)}, u32[]{:S(2)}) collective-permute-start(f32[64,256]{1,0:T(8,128)S(1)} %get-tuple-element.63), channel_id=1, source_target_pairs={{0,1},{1,0},{2,3},{3,2},{4,5},{5,4},{6,7},{7,6},{8,9},{9,8},{10,11... | collective-permute-start | bytes 196616 | tf_op jit(solution)/shard_map/ppermute | solution.py:497
  8.8 7.8 %collective-permute-start.3 = (f32[64,256]{1,0:T(8,128)S(1)}, f32[64,256]{1,0:T(8,128)S(1)}, u32[]{:S(2)}, u32[]{:S(2)}) collective-permute-start(f32[64,256]{1,0:T(8,128)S(1)} %get-tuple-element.64), channel_id=1, source_target_pairs={{0,3},{1,2},{2,1},{3,0},{4,7},{5,6},{6,5},{7,4},{8,11},{9,10},{10,... | collective-permute-start | bytes 196616 | tf_op jit(solution)/shard_map/ppermute | solution.py:496
  11.3 5.3 %collective-permute-start.4 = (f32[40,256]{1,0:T(8,128)S(1)}, f32[40,256]{1,0:T(8,128)S(1)}, u32[]{:S(2)}, u32[]{:S(2)}) collective-permute-start(f32[40,256]{1,0:T(8,128)S(1)} %get-tuple-element.60.refs_5_), channel_id=1, source_target_pairs={{0,2},{1,3},{2,0},{3,1},{4,6},{5,7},{6,4},{7,5},{8,10},{9,11},{10,... | collective-permute-start | bytes 122888 | tf_op jit(solution)/shard_map/ppermute | solution.py:505
  25.2 8.2 %collective-permute-start.5 = (f32[144,256]{1,0:T(8,128)S(1)}, f32[144,256]{1,0:T(8,128)S(1)}, u32[]{:S(2)}, u32[]{:S(2)}) collective-permute-start(f32[144,256]{1,0:T(8,128)S(1)} %get-tuple-element.68), channel_id=1, source_target_pairs={{0,4},{4,0},{8,12},{12,8},{16,20},{20,16},{24,28},{28,24},{1,5},{5... | collective-permute-start | bytes 442376 | tf_op jit(solution)/shard_map/ppermute | solution.py:499
  25.3 8.1 %collective-permute-start.6 = (f32[144,256]{1,0:T(8,128)S(1)}, f32[144,256]{1,0:T(8,128)S(1)}, u32[]{:S(2)}, u32[]{:S(2)}) collective-permute-start(f32[144,256]{1,0:T(8,128)S(1)} %get-tuple-element.69), channel_id=1, source_target_pairs={{0,28},{4,8},{8,4},{12,16},{16,12},{20,24},{24,20},{28,0},{1,29},{... | collective-permute-start | bytes 442376 | tf_op jit(solution)/shard_map/ppermute | solution.py:498
  26.1 7.3 %collective-permute-start.7 = (f32[48,256]{1,0:T(8,128)S(1)}, f32[48,256]{1,0:T(8,128)S(1)}, u32[]{:S(2)}, u32[]{:S(2)}) collective-permute-start(f32[48,256]{1,0:T(8,128)S(1)} %get-tuple-element.70), channel_id=1, source_target_pairs={{0,1},{1,0},{2,3},{3,2},{4,5},{5,4},{6,7},{7,6},{8,9},{9,8},{10,11... | collective-permute-start | bytes 147464 | tf_op jit(solution)/shard_map/ppermute | solution.py:497
  26.2 7.3 %collective-permute-start.8 = (f32[48,256]{1,0:T(8,128)S(1)}, f32[48,256]{1,0:T(8,128)S(1)}, u32[]{:S(2)}, u32[]{:S(2)}) collective-permute-start(f32[48,256]{1,0:T(8,128)S(1)} %get-tuple-element.71), channel_id=1, source_target_pairs={{0,3},{1,2},{2,1},{3,0},{4,7},{5,6},{6,5},{7,4},{8,11},{9,10},{10,... | collective-permute-start | bytes 147464 | tf_op jit(solution)/shard_map/ppermute | solution.py:496
  28.7 4.7 %collective-permute-start.9 = (f32[24,256]{1,0:T(8,128)S(1)}, f32[24,256]{1,0:T(8,128)S(1)}, u32[]{:S(2)}, u32[]{:S(2)}) collective-permute-start(f32[24,256]{1,0:T(8,128)S(1)} %get-tuple-element.72.refs_8_.refs_5_), channel_id=1, source_target_pairs={{0,2},{1,3},{2,0},{3,1},{4,6},{5,7},{6,4},{7,5},{8,10},{9,11},{10,... | collective-permute-start | bytes 73736 | tf_op jit(solution)/shard_map/ppermute | solution.py:505
  37.1 8.6 %collective-permute-start.10 = (f32[192,256]{1,0:T(8,128)S(1)}, f32[192,256]{1,0:T(8,128)S(1)}, u32[]{:S(2)}, u32[]{:S(2)}) collective-permute-start(f32[192,256]{1,0:T(8,128)S(1)} %get-tuple-element.78), channel_id=1, source_target_pairs={{0,4},{4,0},{8,12},{12,8},{16,20},{20,16},{24,28},{28,24},{1,5},{5... | collective-permute-start | bytes 589832 | tf_op jit(solution)/shard_map/ppermute | solution.py:499
  37.3 8.3 %collective-permute-start.11 = (f32[192,256]{1,0:T(8,128)S(1)}, f32[192,256]{1,0:T(8,128)S(1)}, u32[]{:S(2)}, u32[]{:S(2)}) collective-permute-start(f32[192,256]{1,0:T(8,128)S(1)} %get-tuple-element.79), channel_id=1, source_target_pairs={{0,28},{4,8},{8,4},{12,16},{16,12},{20,24},{24,20},{28,0},{1,29},{... | collective-permute-start | bytes 589832 | tf_op jit(solution)/shard_map/ppermute | solution.py:498
  39.1 3.8 %collective-permute-start.12 = (f32[24,256]{1,0:T(8,128)S(1)}, f32[24,256]{1,0:T(8,128)S(1)}, u32[]{:S(2)}, u32[]{:S(2)}) collective-permute-start(f32[24,256]{1,0:T(8,128)S(1)} %get-tuple-element.80), channel_id=1, source_target_pairs={{0,1},{1,0},{2,3},{3,2},{4,5},{5,4},{6,7},{7,6},{8,9},{9,8},{10,11... | collective-permute-start | bytes 73736 | tf_op jit(solution)/shard_map/ppermute | solution.py:497
  40.0 5.6 %collective-permute-start.13 = (f32[24,256]{1,0:T(8,128)S(1)}, f32[24,256]{1,0:T(8,128)S(1)}, u32[]{:S(2)}, u32[]{:S(2)}) collective-permute-start(f32[24,256]{1,0:T(8,128)S(1)} %get-tuple-element.81), channel_id=1, source_target_pairs={{0,3},{1,2},{2,1},{3,0},{4,7},{5,6},{6,5},{7,4},{8,11},{9,10},{10,... | collective-permute-start | bytes 73736 | tf_op jit(solution)/shard_map/ppermute | solution.py:496
  49.4 8.2 %collective-permute-start.14 = (f32[120,256]{1,0:T(8,128)S(1)}, f32[120,256]{1,0:T(8,128)S(1)}, u32[]{:S(2)}, u32[]{:S(2)}) collective-permute-start(f32[120,256]{1,0:T(8,128)S(1)} %get-tuple-element.86), channel_id=1, source_target_pairs={{0,4},{4,0},{8,12},{12,8},{16,20},{20,16},{24,28},{28,24},{1,5},{5... | collective-permute-start | bytes 368648 | tf_op jit(solution)/shard_map/ppermute | solution.py:499
  49.5 8.1 %collective-permute-start.15 = (f32[120,256]{1,0:T(8,128)S(1)}, f32[120,256]{1,0:T(8,128)S(1)}, u32[]{:S(2)}, u32[]{:S(2)}) collective-permute-start(f32[120,256]{1,0:T(8,128)S(1)} %get-tuple-element.87), channel_id=1, source_target_pairs={{0,28},{4,8},{8,4},{12,16},{16,12},{20,24},{24,20},{28,0},{1,29},{... | collective-permute-start | bytes 368648 | tf_op jit(solution)/shard_map/ppermute | solution.py:498
  51.0 6.6 %collective-permute-start.16 = (f32[48,256]{1,0:T(8,128)S(1)}, f32[48,256]{1,0:T(8,128)S(1)}, u32[]{:S(2)}, u32[]{:S(2)}) collective-permute-start(f32[48,256]{1,0:T(8,128)S(1)} %get-tuple-element.88), channel_id=1, source_target_pairs={{0,1},{1,0},{2,3},{3,2},{4,5},{5,4},{6,7},{7,6},{8,9},{9,8},{10,11... | collective-permute-start | bytes 147464 | tf_op jit(solution)/shard_map/ppermute | solution.py:497
  51.0 6.6 %collective-permute-start.17 = (f32[48,256]{1,0:T(8,128)S(1)}, f32[48,256]{1,0:T(8,128)S(1)}, u32[]{:S(2)}, u32[]{:S(2)}) collective-permute-start(f32[48,256]{1,0:T(8,128)S(1)} %get-tuple-element.89), channel_id=1, source_target_pairs={{0,3},{1,2},{2,1},{3,0},{4,7},{5,6},{6,5},{7,4},{8,11},{9,10},{10,... | collective-permute-start | bytes 147464 | tf_op jit(solution)/shard_map/ppermute | solution.py:496
  52.9 4.7 %collective-permute-start.18 = (f32[24,256]{1,0:T(8,128)S(1)}, f32[24,256]{1,0:T(8,128)S(1)}, u32[]{:S(2)}, u32[]{:S(2)}) collective-permute-start(f32[24,256]{1,0:T(8,128)S(1)} %get-tuple-element.90.refs_8_.refs_5_), channel_id=1, source_target_pairs={{0,2},{1,3},{2,0},{3,1},{4,6},{5,7},{6,4},{7,5},{8,10},{9,11},{10,... | collective-permute-start | bytes 73736 | tf_op jit(solution)/shard_map/ppermute | solution.py:505
  61.2 8.2 %collective-permute-start.19 = (f32[120,256]{1,0:T(8,128)S(1)}, f32[120,256]{1,0:T(8,128)S(1)}, u32[]{:S(2)}, u32[]{:S(2)}) collective-permute-start(f32[120,256]{1,0:T(8,128)S(1)} %get-tuple-element.92), channel_id=1, source_target_pairs={{0,4},{4,0},{8,12},{12,8},{16,20},{20,16},{24,28},{28,24},{1,5},{5... | collective-permute-start | bytes 368648 | tf_op jit(solution)/shard_map/ppermute | solution.py:499
  61.3 8.1 %collective-permute-start.20 = (f32[120,256]{1,0:T(8,128)S(1)}, f32[120,256]{1,0:T(8,128)S(1)}, u32[]{:S(2)}, u32[]{:S(2)}) collective-permute-start(f32[120,256]{1,0:T(8,128)S(1)} %get-tuple-element.93), channel_id=1, source_target_pairs={{0,28},{4,8},{8,4},{12,16},{16,12},{20,24},{24,20},{28,0},{1,29},{... | collective-permute-start | bytes 368648 | tf_op jit(solution)/shard_map/ppermute | solution.py:498
  63.5 3.8 %collective-permute-start.21 = (f32[24,256]{1,0:T(8,128)S(1)}, f32[24,256]{1,0:T(8,128)S(1)}, u32[]{:S(2)}, u32[]{:S(2)}) collective-permute-start(f32[24,256]{1,0:T(8,128)S(1)} %get-tuple-element.94), channel_id=1, source_target_pairs={{0,1},{1,0},{2,3},{3,2},{4,5},{5,4},{6,7},{7,6},{8,9},{9,8},{10,11... | collective-permute-start | bytes 73736 | tf_op jit(solution)/shard_map/ppermute | solution.py:497
  63.8 5.6 %collective-permute-start.22 = (f32[24,256]{1,0:T(8,128)S(1)}, f32[24,256]{1,0:T(8,128)S(1)}, u32[]{:S(2)}, u32[]{:S(2)}) collective-permute-start(f32[24,256]{1,0:T(8,128)S(1)} %get-tuple-element.95), channel_id=1, source_target_pairs={{0,3},{1,2},{2,1},{3,0},{4,7},{5,6},{6,5},{7,4},{8,11},{9,10},{10,... | collective-permute-start | bytes 73736 | tf_op jit(solution)/shard_map/ppermute | solution.py:496
  72.1 6.6 %collective-permute-start.23 = (f32[48,256]{1,0:T(8,128)S(1)}, f32[48,256]{1,0:T(8,128)S(1)}, u32[]{:S(2)}, u32[]{:S(2)}) collective-permute-start(f32[48,256]{1,0:T(8,128)S(1)} %get-tuple-element.99), channel_id=1, source_target_pairs={{0,4},{4,0},{8,12},{12,8},{16,20},{20,16},{24,28},{28,24},{1,5},{5... | collective-permute-start | bytes 147464 | tf_op jit(solution)/shard_map/ppermute | solution.py:499
  72.1 6.5 %collective-permute-start.24 = (f32[48,256]{1,0:T(8,128)S(1)}, f32[48,256]{1,0:T(8,128)S(1)}, u32[]{:S(2)}, u32[]{:S(2)}) collective-permute-start(f32[48,256]{1,0:T(8,128)S(1)} %get-tuple-element.100), channel_id=1, source_target_pairs={{0,28},{4,8},{8,4},{12,16},{16,12},{20,24},{24,20},{28,0},{1,29},{... | collective-permute-start | bytes 147464 | tf_op jit(solution)/shard_map/ppermute | solution.py:498
  73.0 3.8 %collective-permute-start.25 = (f32[24,256]{1,0:T(8,128)S(1)}, f32[24,256]{1,0:T(8,128)S(1)}, u32[]{:S(2)}, u32[]{:S(2)}) collective-permute-start(f32[24,256]{1,0:T(8,128)S(1)} %get-tuple-element.101), channel_id=1, source_target_pairs={{0,1},{1,0},{2,3},{3,2},{4,5},{5,4},{6,7},{7,6},{8,9},{9,8},{10,11... | collective-permute-start | bytes 73736 | tf_op jit(solution)/shard_map/ppermute | solution.py:497
  73.0 5.6 %collective-permute-start.26 = (f32[24,256]{1,0:T(8,128)S(1)}, f32[24,256]{1,0:T(8,128)S(1)}, u32[]{:S(2)}, u32[]{:S(2)}) collective-permute-start(f32[24,256]{1,0:T(8,128)S(1)} %get-tuple-element.102), channel_id=1, source_target_pairs={{0,3},{1,2},{2,1},{3,0},{4,7},{5,6},{6,5},{7,4},{8,11},{9,10},{10,... | collective-permute-start | bytes 73736 | tf_op jit(solution)/shard_map/ppermute | solution.py:496

commit v4 on v2

v4 whole, which is shorter than its diff:
```python
import functools
import math

import jax
import jax.numpy as jnp
from jax import lax
from jax.experimental import pallas as pl
from jax.experimental.pallas import tpu as pltpu
from jax.sharding import PartitionSpec as P

STEPS = 3
time_step = 0.2
cone_rate = 1.5
F32, BF16, I32 = jnp.float32, jnp.bfloat16, jnp.int32
COLS = 256
DEPTH_PART = (0, 3, 4)
PLAN_PART = (3, 1, 5)
LAST_PART = (4, 5, 2)


class Sizes:
    def __init__(self, stress, pile_velocity, pair_cell):
        self.cz, self.cx, self.cy = stress.shape[1:]
        self.rows = self.cz * self.cx
        self.pile = pile_velocity.shape[1]
        self.pr = self.pile // COLS
        self.wp = 3 * self.pr
        self.pairs = pair_cell.shape[1]
        self.kn = self.pairs // COLS
        self.nd = lax.axis_size("depth")
        self.np = lax.axis_size("plan")


def partner_b(index, count):
    return jnp.where(
        index % 2 == 0, lax.rem(index + count - 1, count), lax.rem(index + 1, count)
    )


def low_high(index, count, ref_a, ref_b, where):
    a, b = ref_a[where], ref_b[where]
    even = index % 2 == 0
    zero = jnp.zeros_like(a)
    low = jnp.where(index > 0, jnp.where(even, b, a), zero)
    high = jnp.where(index < count - 1, jnp.where(even, a, b), zero)
    return low, high


def split(x):
    high = x.astype(BF16)
    return high, (x - high.astype(F32)).astype(BF16)


def hits(ids, count):
    return lax.broadcasted_iota(I32, (count, ids.shape[1]), 0) == ids


def one_hot(ids, count):
    return jnp.where(hits(ids, count), 1.0, 0.0).astype(BF16)


def gather_chunk(table, row_ids, col_ids, parts, rows):
    pick = one_hot(col_ids, COLS)
    got = jnp.dot(table[0][...], pick, preferred_element_type=F32)
    got = got + jnp.dot(table[1][...], pick, preferred_element_type=F32)
    mask = hits(row_ids, rows)
    return [
        jnp.sum(jnp.where(mask, got[c * rows : (c + 1) * rows], 0.0), axis=0, keepdims=True)
        for c in range(parts)
    ]


def scatter_chunk(values, row_ids, col_ids, rows, exact=0):
    put = one_hot(col_ids, COLS)
    mask = hits(row_ids, rows)
    pairs = [split(v) for v in values]
    pieces = [v[0] for v in pairs], [v[1] for v in pairs[: len(values) - exact]]
    terms = []
    for piece in pieces:
        spread = jnp.concatenate(
            [jnp.where(mask, v.astype(F32), 0.0) for v in piece], axis=0
        ).astype(BF16)
        terms.append(
            lax.dot_general(spread, put, (((1,), (1,)), ((), ())), preferred_element_type=F32)
        )
    return terms


def added(total, terms):
    return terms if total is None else [a + b for a, b in zip(total, terms)]


def row_of(ref, row):
    return ref[row : row + 1, :]


def shifted_rows(a, low, high):
    count = a.shape[0]
    row = lax.broadcasted_iota(I32, a.shape, 0)
    up = jnp.where(row == count - 1, high, pltpu.roll(a, count - 1, 0))
    down = jnp.where(row == 0, low, pltpu.roll(a, 1, 0))
    return up - down


def shifted_lanes(a):
    count = a.shape[1]
    lane = lax.broadcasted_iota(I32, a.shape, 1)
    up = jnp.where(lane == count - 1, 0.0, pltpu.roll(a, count - 1, 1))
    down = jnp.where(lane == 0, 0.0, pltpu.roll(a, 1, 1))
    return up - down


def send_layers(sz, depth, parts, plane, to_da, to_db):
    even, cx = depth % 2 == 0, sz.cx
    for i, c in enumerate(parts):
        first, last = plane(c, 0), plane(c, sz.cz - 1)
        to_da[i * cx : (i + 1) * cx, :] = jnp.where(even, last, first)
        to_db[i * cx : (i + 1) * cx, :] = jnp.where(even, first, last)


def column(sz, ref, c, x):
    rows = [z * sz.cx + x for z in range(sz.cz)]
    return jnp.concatenate([ref[c, r : r + 1, :] for r in rows], axis=0)


def send_columns(sz, plan, columns, to_pa, to_pb):
    even, cz = plan % 2 == 0, sz.cz
    for i, (first, last) in enumerate(columns):
        to_pa[i * cz : (i + 1) * cz, :] = jnp.where(even, last, first)
        to_pb[i * cz : (i + 1) * cz, :] = jnp.where(even, first, last)


def store_split(sz, source, parts, rows, refs):
    for c in range(parts):
        high, low = split(source(c))
        refs[0][c * rows : (c + 1) * rows, :] = high
        refs[1][c * rows : (c + 1) * rows, :] = low


def gather_cells(sz, table, ids, out):
    for j in range(sz.kn):
        got = gather_chunk(table, row_of(ids, j), row_of(ids, sz.kn + j), 3, sz.rows)
        for c in range(3):
            out[c * sz.kn + j : c * sz.kn + j + 1, :] = got[c]


def scatter_sets(sz, parts, sets, ids, acc):
    group = math.gcd(sz.np, 4)
    low_rows = 3 * sz.wp

    def some(t):
        total = None
        for s in range(group):
            one, index = sets.at[t * group + s], ids.at[t * group + s]
            for j in range(sz.kn):
                values = [row_of(one, c * sz.kn + j) for c in range(parts)]
                terms = scatter_chunk(
                    values, row_of(index, j), row_of(index, sz.kn + j), sz.wp, parts - 3
                )
                total = added(total, terms)
        return total

    if group == sz.np:
        high, low = some(0)
        acc[...] = high
        acc[0:low_rows, :] += low
    else:
        acc[...] = jnp.zeros_like(acc)

        def body(t, carry):
            high, low = some(t)
            acc[...] += high
            acc[0:low_rows, :] += low
            return carry

        lax.fori_loop(0, sz.np // group, body, 0)


def sort_sets(sz, plan, own, got, sets, rows, offset):
    a, b, others = got
    index = [plan, lax.rem(plan + 1 - 2 * (plan % 2) + sz.np, sz.np), partner_b(plan, sz.np)]
    sets[index[1]] = a[offset : offset + rows, :]
    sets[index[2]] = b[offset : offset + rows, :]
    for shift, ref in zip(range(2, sz.np - 1), others):
        sets[lax.rem(plan + sz.np - shift, sz.np)] = ref[...]
    sets[index[0]] = own[...]


def send_sums(sz, depth, parts, acc, to_da, to_db, offset):
    even = depth % 2 == 0
    pr = sz.pr
    for c in range(parts):
        first = acc[c * sz.wp : c * sz.wp + pr, :]
        last = acc[c * sz.wp + 2 * pr : c * sz.wp + 3 * pr, :]
        to_da[offset + c * pr : offset + (c + 1) * pr, :] = jnp.where(even, last, first)
        to_db[offset + c * pr : offset + (c + 1) * pr, :] = jnp.where(even, first, last)


def total_sum(sz, depth, c, acc, from_da, from_db, offset):
    rows = slice(offset + c * sz.pr, offset + (c + 1) * sz.pr)
    low, high = low_high(depth, sz.nd, from_da, from_db, (rows, slice(None)))
    return low + acc[c * sz.wp + sz.pr : c * sz.wp + 2 * sz.pr, :] + high


def move_pile(sz, depth, pile, jack, mass, count, acc, from_da, from_db, offset, out):
    for c in range(3):
        rows = slice(c * sz.pr, (c + 1) * sz.pr)
        summed = total_sum(sz, depth, c, acc, from_da, from_db, offset)
        p = pile[rows, :]
        out[rows, :] = p + time_step * (jack[rows, :] - (count[...] * p - summed)) / mass[...]


def new_stress(along_z, along_x, along_y, old, flag):
    normal = [along_z[0], along_x[1], along_y[2]]
    shear = [along_x[0] + along_z[1], along_y[0] + along_z[2], along_y[1] + along_x[2]]
    bulk = (0.5 * time_step) * (normal[0] + normal[1] + normal[2])
    trial = [old[c] + (time_step * normal[c] + bulk) for c in range(3)]
    sheared = [old[3 + c] + (0.5 * time_step) * shear[c] for c in range(3)]
    pressure = (trial[0] + trial[1] + trial[2]) * (1.0 / 3.0)
    dev = [t - pressure for t in trial]
    second = 0.5 * (dev[0] * dev[0] + dev[1] * dev[1] + dev[2] * dev[2])
    for t in sheared:
        second = second + t * t
    shrink = 1.0 / (1.0 + cone_rate * jnp.sqrt(second))
    factor = jnp.where(flag == 1, shrink, 0.0)
    elastic = flag == 0
    return [jnp.where(elastic, t, d * factor + pressure) for t, d in zip(trial, dev)] + [
        jnp.where(elastic, t, t * factor) for t in sheared
    ]


def taker(refs):
    refs = list(refs)
    return lambda n: [refs.pop(0) for _ in range(n)]


def first_kernel(sz, *refs):
    take = taker(refs)
    sources = take(9)
    to_da, to_db, to_pa, to_pb, to_all, cell_ids, elem_ids, pile, mass, jack = take(10)
    stress, velocity, density, flags = take(4)
    high, low, pile_in, mass_in, jack_in, elem_in, cell_in, sems = take(8)
    targets = (
        cell_in, velocity, elem_in, pile_in, mass_in, jack_in, stress, flags, density,
    )
    copies = [
        pltpu.make_async_copy(a, b, sems.at[i]) for i, (a, b) in enumerate(zip(sources, targets))
    ]
    for copy in copies:
        copy.start()
    depth, plan = lax.axis_index("depth"), lax.axis_index("plan")
    kn, pr, cx, cz = sz.kn, sz.pr, sz.cx, sz.cz
    for copy in copies[:3]:
        copy.wait()
    for j in range(kn):
        lanes = slice(j * COLS, (j + 1) * COLS)
        cell, elem = cell_in[:, lanes], elem_in[:, lanes]
        cell_ids[j : j + 1, :] = lax.shift_right_arithmetic(cell, 8)
        cell_ids[kn + j : kn + j + 1, :] = lax.bitwise_and(cell, COLS - 1)
        elem_ids[j : j + 1, :] = lax.shift_right_arithmetic(elem, 8)
        elem_ids[kn + j : kn + j + 1, :] = lax.bitwise_and(elem, COLS - 1)
        to_all[3 * kn + j : 3 * kn + j + 1, :] = jnp.where(cell >= 0, elem, -1).astype(F32)
    store_split(sz, lambda c: velocity[c], 3, sz.rows, (high, low))
    gather_cells(sz, (high, low), cell_ids, to_all)
    for copy in copies[3:]:
        copy.wait()
    for r in range(pr):
        lanes = slice(r * COLS, (r + 1) * COLS)
        for c in range(3):
            pile[c * pr + r : c * pr + r + 1, :] = pile_in[c : c + 1, lanes]
            jack[c * pr + r : c * pr + r + 1, :] = jack_in[c : c + 1, lanes]
        mass[r : r + 1, :] = mass_in[:, lanes]
    to_da[3 * cx :, :] = pile[...]
    to_db[3 * cx :, :] = pile[...]
    to_pa[7 * cz :, :] = to_all[...]
    to_pb[7 * cz :, :] = to_all[...]
    plane = lambda c, z: stress[c, z * cx : (z + 1) * cx, :]
    send_layers(sz, depth, DEPTH_PART, plane, to_da, to_db)
    columns = [(column(sz, stress, c, 0), column(sz, stress, c, cx - 1)) for c in range(6)]
    ends = [
        jnp.concatenate([row_of(flags, z * cx + x) for z in range(cz)], axis=0).astype(F32)
        for x in (0, cx - 1)
    ]
    send_columns(sz, plan, columns + [ends], to_pa, to_pb)


def update_velocity(
    sz, depth, stress, velocity, density, from_da, from_db, columns, window_of, at_cells,
    cell_ids, elem_ids, out, high, low, on_cells,
):
    kn, rows, wp, cx, cz = sz.kn, sz.rows, sz.wp, sz.cx, sz.cz
    pile_high, pile_low = high.at[0 : 3 * wp, :], low.at[0 : 3 * wp, :]
    store_split(
        sz, lambda c: jnp.concatenate(list(window_of(c)), axis=0), 3, wp, (pile_high, pile_low)
    )
    total = None
    for j in range(kn):
        at_pile = gather_chunk(
            (pile_high, pile_low), row_of(elem_ids, j), row_of(elem_ids, kn + j), 3, wp
        )
        push = [at_pile[c] - row_of(at_cells, c * kn + j) for c in range(3)]
        total = added(
            total, scatter_chunk(push, row_of(cell_ids, j), row_of(cell_ids, kn + j), rows)
        )
    on_cells[...] = total[0] + total[1]
    plane = lambda c, z: stress[c, z * cx : (z + 1) * cx, :]
    d_low, d_high = low_high(
        depth, sz.nd, from_da, from_db, (slice(0, 3 * cx), slice(None))
    )
    for z in range(cz):
        here = slice(z * cx, (z + 1) * cx)
        scale = time_step / density[here, :]
        for i in range(3):
            ahead = plane(DEPTH_PART[i], z + 1) if z + 1 < cz else d_high[i * cx : (i + 1) * cx]
            behind = plane(DEPTH_PART[i], z - 1) if z > 0 else d_low[i * cx : (i + 1) * cx]
            c = PLAN_PART[i]
            twice = (
                (ahead - behind)
                + shifted_rows(
                    plane(c, z), row_of(columns, c * cz + z), row_of(columns, (6 + c) * cz + z)
                )
                + shifted_lanes(plane(LAST_PART[i], z))
            )
            force = 0.5 * twice + on_cells[i * rows + z * cx : i * rows + (z + 1) * cx, :]
            out[i, here, :] = velocity[i, here, :] + scale * force


def update_columns(
    sz, depth, plan, velocity, from_pa, from_pb, from_da, from_db, offset, old, flags, out
):
    cz, cx = sz.cz, sz.cx
    lines = low_high(depth, sz.nd, from_da, from_db, (slice(offset, offset + 8), slice(None)))
    strips = low_high(plan, sz.np, from_pa, from_pb, (slice(0, 6 * cz), slice(None)))
    inside = plan > 0, plan < sz.np - 1
    for side in range(2):
        along_z, along_x, along_y = [], [], []
        for c in range(3):
            near = strips[side][c * cz : (c + 1) * cz]
            away = strips[side][(3 + c) * cz : (4 + c) * cz]
            mine = column(sz, velocity, c, 0 if side == 0 else cx - 1)
            line = slice(side * 3 + c, side * 3 + c + 1)
            along_z.append(shifted_rows(near, lines[0][line], lines[1][line]))
            along_x.append(mine - away if side == 0 else away - mine)
            along_y.append(shifted_lanes(near))
        where = lambda c: slice((side * 6 + c) * cz, (side * 6 + c + 1) * cz)
        flag = flags[side * cz : (side + 1) * cz, :]
        got = new_stress(along_z, along_x, along_y, [old[where(c), :] for c in range(6)], flag)
        for c in range(6):
            out[where(c), :] = jnp.where(inside[side], got[c], jnp.zeros_like(got[c]))


def update_stress(
    sz, depth, plan, stress, velocity, flags, from_da, from_db, from_pa, from_pb, out,
    plane_done=None,
):
    cx, cz = sz.cx, sz.cz
    plane = lambda c, z: velocity[c, z * cx : (z + 1) * cx, :]
    d_low, d_high = low_high(
        depth, sz.nd, from_da, from_db, (slice(0, 3 * cx), slice(None))
    )
    p_low, p_high = low_high(plan, sz.np, from_pa, from_pb, (slice(0, 3 * cz), slice(None)))
    for z in range(cz):
        here = slice(z * cx, (z + 1) * cx)
        v = [plane(c, z) for c in range(3)]
        along_z, along_x = [], []
        for c in range(3):
            ahead = plane(c, z + 1) if z + 1 < cz else d_high[c * cx : (c + 1) * cx]
            behind = plane(c, z - 1) if z > 0 else d_low[c * cx : (c + 1) * cx]
            along_z.append(ahead - behind)
            row = slice(c * cz + z, c * cz + z + 1)
            along_x.append(shifted_rows(v[c], p_low[row], p_high[row]))
        along_y = [shifted_lanes(v[c]) for c in range(3)]
        got = new_stress(
            along_z, along_x, along_y, [stress[c, here, :] for c in range(6)], flags[here, :]
        )
        for c in range(6):
            out[c, here, :] = got[c]
        if plane_done is not None:
            plane_done(z)
    return p_low, p_high


def window_from(sz, depth, pile, from_da, from_db, offset):
    def of(c):
        rows = slice(offset + c * sz.pr, offset + (c + 1) * sz.pr)
        low, high = low_high(depth, sz.nd, from_da, from_db, (rows, slice(None)))
        return low, pile[c * sz.pr : (c + 1) * sz.pr, :], high

    return of


def velocity_kernel(sz, step, *refs):
    depth, plan = lax.axis_index("depth"), lax.axis_index("plan")
    take = taker(refs)
    cx, cz = sz.cx, sz.cz
    stress, velocity, density, cell_ids, elem_ids, at_cells, pile = take(7)
    from_da, from_db, from_pa, from_pb = take(4)
    if step > 0:
        old_columns, column_flags, acc = take(3)
    out, to_da, to_db, to_pa, to_pb = take(5)
    if step < STEPS - 1:
        to_all, columns = take(2)
    if step == 0:
        (column_flags,) = take(1)
    if step == STEPS - 1:
        (columns,) = take(1)
    high, low, on_cells = take(3)
    head = 3 * cx
    if step == 0:
        offset = head
        strips = low_high(plan, sz.np, from_pa, from_pb, (slice(0, 7 * cz), slice(None)))
        for side in range(2):
            columns[6 * cz * side : 6 * cz * (side + 1), :] = strips[side][0 : 6 * cz]
            column_flags[cz * side : cz * (side + 1), :] = strips[side][6 * cz :].astype(I32)
    else:
        offset = head + 8
        update_columns(
            sz, depth, plan, velocity, from_pa, from_pb, from_da, from_db, head, old_columns,
            column_flags, columns,
        )
    update_velocity(
        sz, depth, stress, velocity, density, from_da, from_db, columns,
        window_from(sz, depth, pile, from_da, from_db, offset), at_cells, cell_ids, elem_ids,
        out, high, low, on_cells,
    )
    plane = lambda c, z: out[c, z * cx : (z + 1) * cx, :]
    send_layers(sz, depth, range(3), plane, to_da, to_db)
    if step > 0:
        send_sums(sz, depth, 3, acc, to_da, to_db, head)
    shifts = range(2 if step < STEPS - 1 else 1)
    ends = [
        (column(sz, out, c, x), column(sz, out, c, cx - 1 - x)) for x in shifts for c in range(3)
    ]
    send_columns(sz, plan, ends, to_pa, to_pb)
    if step < STEPS - 1:
        store_split(sz, lambda c: out[c], 3, sz.rows, (high, low))
        gather_cells(sz, (high, low), cell_ids, to_all)
        to_pa[6 * cz :, :] = to_all[...]
        to_pb[6 * cz :, :] = to_all[...]


def sums_kernel(sz, step, *refs):
    depth, plan = lax.axis_index("depth"), lax.axis_index("plan")
    take = taker(refs)
    own, from_pa, from_pb = take(3)
    from_others = take(max(sz.np - 3, 0))
    kn, head = sz.kn, 3 * sz.cx
    if step == 0:
        layer_a, layer_b, to_da, to_db, acc, set_ids, sets = take(7)
        sort_sets(sz, plan, own, (from_pa, from_pb, from_others), sets, 4 * kn, 7 * sz.cz)
        for s in range(sz.np):
            ids = sets[s, 3 * kn : 4 * kn, :]
            elem = ids.astype(I32)
            set_ids[s, 0:kn, :] = lax.shift_right_arithmetic(elem, 8)
            set_ids[s, kn : 2 * kn, :] = lax.bitwise_and(elem, COLS - 1)
            sets[s, 3 * kn : 4 * kn, :] = jnp.where(ids >= 0, 1.0, 0.0)
        scatter_sets(sz, 4, sets, set_ids, acc)
        to_da[0:head, :] = layer_a[...]
        to_db[0:head, :] = layer_b[...]
        send_sums(sz, depth, 4, acc, to_da, to_db, head)
    else:
        set_ids, acc, sets = take(3)
        sort_sets(sz, plan, own, (from_pa, from_pb, from_others), sets, 3 * kn, 6 * sz.cz)
        scatter_sets(sz, 3, sets, set_ids, acc)


def stress_kernel(sz, step, *refs):
    depth, plan = lax.axis_index("depth"), lax.axis_index("plan")
    take = taker(refs)
    stress, velocity, flags, from_da, from_db, from_pa, from_pb = take(7)
    pile, mass, jack, acc = take(4)
    cx, cz, head = sz.cx, sz.cz, 3 * sz.cx
    froms = from_da, from_db, from_pa, from_pb
    if step == 0:
        out, to_da, to_db, new_pile, count = take(5)
        count[...] = total_sum(sz, depth, 3, acc, from_da, from_db, head)
    elif step < STEPS - 1:
        count, out, to_da, to_db, new_pile = take(5)
    else:
        count, stress_out, velocity_out, pile_out, out, new_pile, flat_pile, sems = take(8)
        copies = [pltpu.make_async_copy(velocity, velocity_out, sems.at[cz])]
        copies[0].start()
    move_pile(sz, depth, pile, jack, mass, count, acc, from_da, from_db, head, new_pile)
    if step < STEPS - 1:
        strips = update_stress(sz, depth, plan, stress, velocity, flags, *froms, out)
        plane = lambda c, z: out[c, z * cx : (z + 1) * cx, :]
        send_layers(sz, depth, DEPTH_PART, plane, to_da, to_db)
        lines = [
            [strips[side][c * cz + z : c * cz + z + 1] for side in range(2) for c in range(3)]
            for z in (0, cz - 1)
        ]
        blank = [jnp.zeros((2, sz.cy), F32)]
        first, last = [jnp.concatenate(one + blank, axis=0) for one in lines]
        even = depth % 2 == 0
        to_da[head : head + 8, :] = jnp.where(even, last, first)
        to_db[head : head + 8, :] = jnp.where(even, first, last)
        to_da[head + 8 :, :] = new_pile[...]
        to_db[head + 8 :, :] = new_pile[...]
        return
    for r in range(sz.pr):
        for c in range(3):
            row = c * sz.pr + r
            flat_pile[c : c + 1, r * COLS : (r + 1) * COLS] = new_pile[row : row + 1, :]
    copies.append(pltpu.make_async_copy(flat_pile, pile_out, sems.at[cz + 1]))
    copies[-1].start()

    def plane_done(z):
        part = (slice(None), pl.ds(z * cx, cx), slice(None))
        copies.append(pltpu.make_async_copy(out.at[part], stress_out.at[part], sems.at[z]))
        copies[-1].start()

    update_stress(sz, depth, plan, stress, velocity, flags, *froms, out, plane_done)
    for copy in copies:
        copy.wait()


def call(body, name, ins, outs, scratch=(), copies=0, far_ins=False, far_outs=False, flops=0):
    vmem, far = pl.BlockSpec(memory_space=pltpu.VMEM), pl.BlockSpec(memory_space=pl.ANY)
    sems = [pltpu.SemaphoreType.DMA((copies,))] if copies else []
    moved = sum(4 * x.size for x in ins) + sum(4 * math.prod(shape) for shape, _ in outs)
    return pl.pallas_call(
        body,
        out_shape=[jax.ShapeDtypeStruct(shape, dtype) for shape, dtype in outs],
        in_specs=[far if far_ins else vmem] * len(ins),
        out_specs=[far if far_outs else vmem] * len(outs),
        scratch_shapes=[pltpu.VMEM(shape, dtype) for shape, dtype in scratch] + sems,
        compiler_params=pltpu.CompilerParams(vmem_limit_bytes=48 * 2**20),
        cost_estimate=pl.CostEstimate(flops=flops, bytes_accessed=moved, transcendentals=0),
        name=name,
    )(*[pltpu.with_memory_space_constraint(x, pltpu.HBM) if far_ins else x for x in ins])


def matchings(count):
    first = [(i, i ^ 1) for i in range(count)]
    second = [(i, (i - 1) % count if i % 2 == 0 else (i + 1) % count) for i in range(count)]
    return first, second


def shards(
    stress, velocity, density, flags, pile_velocity, pile_mass, jack_force, pair_elem, pair_cell
):
    sz = Sizes(stress, pile_velocity, pair_cell)
    cz, cx, cy, rows, kn, pr = sz.cz, sz.cx, sz.cy, sz.rows, sz.kn, sz.pr
    assert cy == COLS and sz.pile % COLS == 0 and sz.pairs % COLS == 0
    assert sz.nd % 2 == 0 and sz.np % 2 == 0
    d_first, d_second = matchings(sz.nd)
    p_first, p_second = matchings(sz.np)

    def swap_plan(pa, pb):
        pb = lax.ppermute(pb, "plan", p_second)
        pa = lax.ppermute(pa, "plan", p_first)
        return [pa, pb]

    def swap_depth(da, db):
        db = lax.ppermute(db, "depth", d_second)
        da = lax.ppermute(da, "depth", d_first)
        return [da, db]

    def to_others(x):
        shifts = range(2, sz.np - 1)
        return [
            lax.ppermute(x, "plan", [(i, (i + s) % sz.np) for i in range(sz.np)]) for s in shifts
        ]

    full_shape = stress.shape, velocity.shape
    stress = stress.reshape(6, rows, cy)
    velocity = velocity.reshape(3, rows, cy)
    density = density.reshape(rows, cy)
    flags = flags.reshape(rows, cy)
    pr3, wp = 3 * pr, sz.wp
    tables = [((max(3 * rows, 3 * wp), COLS), BF16)] * 2
    cells = [((3 * rows, COLS), F32)]
    scatter = 4 * 3 * wp * COLS * sz.pairs * sz.np
    layers = lambda extra: [((3 * cx + extra, COLS), F32)] * 2
    strips = lambda extra: [((extra, COLS), F32)] * 2

    to = call(
        functools.partial(first_kernel, sz),
        "first",
        [
            pair_cell, velocity, pair_elem, pile_velocity, pile_mass.reshape(1, -1), jack_force,
            stress, flags, density,
        ],
        layers(pr3)
        + strips(7 * cz + 4 * kn)
        + [
            ((4 * kn, COLS), F32), ((2 * kn, COLS), I32), ((2 * kn, COLS), I32),
            ((pr3, COLS), F32), ((pr, COLS), F32), ((pr3, COLS), F32),
            (stress.shape, F32), (velocity.shape, F32), (density.shape, F32), (flags.shape, I32),
        ],
        tables
        + [(pile_velocity.shape, F32), ((1, sz.pile), F32), (jack_force.shape, F32)]
        + [(pair_elem.shape, I32), (pair_cell.shape, I32)],
        copies=9,
        far_ins=True,
    )
    at_cells, cell_ids, elem_ids, pile, mass, jack = to[4:10]
    stress, velocity, density, flags = to[10:]
    others = to_others(at_cells)
    by_plan = swap_plan(*to[2:4])
    by_depth = swap_depth(*to[0:2])
    count = acc = set_ids = columns = column_flags = None
    for step in range(STEPS):
        last = step == STEPS - 1
        state = [] if step == 0 else [columns, column_flags, acc]
        moved = call(
            functools.partial(velocity_kernel, sz, step),
            f"velocity_{step}",
            [stress, velocity, density, cell_ids, elem_ids, at_cells, pile]
            + by_depth
            + by_plan
            + state,
            [(velocity.shape, F32)]
            + layers(0 if step == 0 else pr3)
            + strips(3 * cz if last else 6 * cz + 3 * kn)
            + ([] if last else [((3 * kn, COLS), F32), ((12 * cz, COLS), F32)])
            + ([((2 * cz, COLS), I32)] if step == 0 else []),
            ([((12 * cz, COLS), F32)] if last else []) + tables + cells,
        )
        velocity, layer = moved[0], list(moved[1:3])
        sets = [at_cells, *by_plan, *others]
        if not last:
            at_cells, columns = moved[5:7]
            others = to_others(at_cells)
        by_plan = swap_plan(*moved[3:5])
        if step == 0:
            column_flags = moved[7]
            *layer, acc, set_ids = call(
                functools.partial(sums_kernel, sz, 0),
                "sums_0",
                sets + layer,
                layers(4 * pr)
                + [((4 * wp, COLS), F32), ((sz.np, 2 * kn, COLS), I32)],
                [((sz.np, 4 * kn, COLS), F32)],
                flops=scatter,
            )
        by_depth = swap_depth(*layer)
        ins = [stress, velocity, flags, *by_depth, *by_plan, pile, mass, jack, acc]
        ins = ins if step == 0 else ins + [count]
        if last:
            stress, velocity, pile = call(
                functools.partial(stress_kernel, sz, step),
                f"stress_{step}",
                ins,
                [(stress.shape, F32), (velocity.shape, F32), (pile_velocity.shape, F32)],
                [(stress.shape, F32), ((pr3, COLS), F32), (pile_velocity.shape, F32)],
                copies=cz + 2,
                far_outs=True,
            )
            break
        got = call(
            functools.partial(stress_kernel, sz, step),
            f"stress_{step}",
            ins,
            [(stress.shape, F32)]
            + layers(8 + pr3)
            + [((pr3, COLS), F32)]
            + ([((pr, COLS), F32)] if step == 0 else []),
        )
        stress, pile = got[0], got[3]
        count = got[4] if step == 0 else count
        by_depth = swap_depth(*got[1:3])
        (acc,) = call(
            functools.partial(sums_kernel, sz, step + 1),
            f"sums_{step + 1}",
            [at_cells, *by_plan, *others, set_ids],
            [((3 * wp, COLS), F32)],
            [((sz.np, 3 * kn, COLS), F32)],
            flops=scatter,
        )
    return stress.reshape(full_shape[0]), velocity.reshape(full_shape[1]), pile


def solution(mesh):
    cells, field = P("depth", "plan", None), P(None, "depth", "plan", None)
    pile, pairs = P(None, "depth"), P("depth", "plan")
    return jax.shard_map(
        shards,
        mesh=mesh,
        in_specs=(field, field, cells, cells, pile, P("depth"), pile, pairs, pairs),
        out_specs=(field, field, pile),
        check_vma=False,
    )
```

time: 90 us -> 70.8 us (0.79)
  local copies, waits for them, and re-layouts: 8.84 us -> 0 us
  waiting for transfers between devices: 23.5 us -> 18 us
  Pallas kernels: 26.9 us -> 24.4 us
  starting transfers between devices: 29.5 us -> 27.3 us
    ppermute x3, waiting for transfers between devices: 12.2 us -> 0.01 us  [to_others(): lax.ppermute(x, 'plan', [(i, (i + s) % sz.np) for i in range(sz.np)])]
    unnamed x20 -> x0, local copies, waits for them, and re-layouts: 8.84 us -> none
    ppermute x24 -> x20, waiting for transfers between devices: 11.3 us -> 18 us  [the longest x4 12.3 us: swap_plan(): pb = lax.ppermute(pb, 'plan', p_second)]
    pallas_call x7 -> x10, Pallas kernels: 26.9 us -> 24.4 us  [call(): pl.pallas_call(body, out_shape=[jax.ShapeDtypeStruct(shape, dtype) for sh...]
    ppermute x3, starting transfers between devices: 2.59 us -> 1.39 us  [to_others(): lax.ppermute(x, 'plan', [(i, (i + s) % sz.np) for i in range(sz.np)])]
    ppermute x24 -> x20, starting transfers between devices: 26.9 us -> 25.9 us  [the longest x6 10.4 us: swap_depth(): db = lax.ppermute(db, 'depth', d_second)]
  transfers between devices with their start and end apart: 27 -> 23, of which waited for: 9 -> 9; matrix products, arithmetic and copies ran while one was open for 0% -> 0% of each run, Pallas kernels for 0% -> 16%
where the time goes in v4:
time: 70.8 us; the launch traced here: 70.6 us
  starting transfers between devices  27.3 us (39%)
  Pallas kernels  24.4 us (34%)
  waiting for transfers between devices  18 us (25%)
  between operations  0.93 us (1%)
    pallas_call x10, Pallas kernels, call(): pl.pallas_call(body, out_shape=[jax.ShapeDtypeStruct(shape, dtype) for sh...  24.4 us
    ppermute x4, waiting for transfers between devices, swap_plan(): pb = lax.ppermute(pb, 'plan', p_second)  12.3 us
    ppermute x6, starting transfers between devices, swap_depth(): db = lax.ppermute(db, 'depth', d_second)  10.4 us
    ppermute x4, starting transfers between devices, swap_plan(): pb = lax.ppermute(pb, 'plan', p_second)  9.79 us
    ppermute x4, starting transfers between devices, swap_plan(): pa = lax.ppermute(pa, 'plan', p_first)  4.86 us
    ppermute x6, waiting for transfers between devices, swap_depth(): db = lax.ppermute(db, 'depth', d_second)  3.88 us
    ppermute x4, waiting for transfers between devices, swap_plan(): pa = lax.ppermute(pa, 'plan', p_first)  1.83 us
  transfers between devices with their start and end apart: 23, of which 9 were waited for; matrix products, arithmetic and copies ran while one was open for 0% of the time, Pallas kernels for 16%

profile of v4, /device:TPU:0, one launch (start us, length us, event | category | flops | bytes accessed | tf_op | source)
XLA Modules:
  0.0 70.6 jit_solution(9200832694469122999)
XLA Ops:
  0.6 2.5 %first.1 = (f32[120,256]{1,0:T(8,128)S(1)}, f32[120,256]{1,0:T(8,128)S(1)}, f32[88,256]{1,0:T(8,128)S(1)}, f32[88,256]{1,0:T(8,128)S(1)}, f32[32,256]{1,0:T(8,12...) custom-call(s32[1,2048]{1,0:T(1,128)} %refs_0_.1, ...), custom_call_target="tpu_custom_call" | custom-call | bytes 3735552 | tf_op jit(solution)/shard_map/first/pallas_call | solution.py:521
  3.1 0.6 collective-permute-start
  3.7 3.5 %collective-permute-start.1 = (f32[120,256]{1,0:T(8,128)S(1)}, f32[120,256]{1,0:T(8,128)S(1)}, u32[]{:S(2)}, u32[]{:S(2)}) collective-permute-start(f32[120,256]{1,0:T(8,128)S(1)} %get-tuple-element.61), channel_id=1, source_target_pairs={{0,28},{4,8},{8,4},{12,16},{16,12},{20,24},{24,20},{28,0},{1,29},{... | collective-permute-start | bytes 368648 | tf_op jit(solution)/shard_map/ppermute | solution.py:555
  7.2 1.6 %collective-permute-start.2 = (f32[88,256]{1,0:T(8,128)S(1)}, f32[88,256]{1,0:T(8,128)S(1)}, u32[]{:S(2)}, u32[]{:S(2)}) collective-permute-start(f32[88,256]{1,0:T(8,128)S(1)} %get-tuple-element.62), channel_id=1, source_target_pairs={{0,1},{1,0},{2,3},{3,2},{4,5},{5,4},{6,7},{7,6},{8,9},{9,8},{10,11... | collective-permute-start | bytes 270344 | tf_op jit(solution)/shard_map/ppermute | solution.py:551
  8.8 2.5 %collective-permute-start.3 = (f32[88,256]{1,0:T(8,128)S(1)}, f32[88,256]{1,0:T(8,128)S(1)}, u32[]{:S(2)}, u32[]{:S(2)}) collective-permute-start(f32[88,256]{1,0:T(8,128)S(1)} %get-tuple-element.63), channel_id=1, source_target_pairs={{0,3},{1,2},{2,1},{3,0},{4,7},{5,6},{6,5},{7,4},{8,11},{9,10},{10,... | collective-permute-start | bytes 270344 | tf_op jit(solution)/shard_map/ppermute | solution.py:550
  11.7 3.5 %collective-permute-done.3.refs_10_.refs_2_ = f32[88,256]{1,0:T(8,128)S(1)} collective-permute-done((f32[88,256]{1,0:T(8,128)S(1)}, f32[88,256]{1,0:T(8,128)S(1)}, u32[]{:S(2)}, u32[]{:S(2)}) %collective-permute-start.3) | collective-permute-done | bytes 90144 | tf_op jit(solution)/shard_map/ppermute | solution.py:550
  15.3 3.9 %velocity_0.1 = (f32[3,128,256]{2,1,0:T(8,128)S(1)}, f32[48,256]{1,0:T(8,128)S(1)}, f32[48,256]{1,0:T(8,128)S(1)}, f32[72,256]{1,0:T(8,128)S(1)}, f32[72,256]{1,...) custom-call(f32[6,128,256]{2,1,0:T(8,128)S(1)} %get-tuple-element.53.refs_0_, ...), custom_call_target="tpu_custom_call" | custom-call | bytes 2654208 | tf_op jit(solution)/shard_map/velocity_0/pallas_call | solution.py:521
  19.2 3.0 %sums_0.1 = (f32[144,256]{1,0:T(8,128)S(1)}, f32[144,256]{1,0:T(8,128)S(1)}, f32[288,256]{1,0:T(8,128)S(1)}, s32[4,16,256]{2,1,0:T(8,128)S(1)}) custom-call(f32[32,256]{1,0:T(8,128)S(1)} %get-tuple-element.58.refs_5_.refs_0_, f32[88,256]{1,0:T(8,128)S(1)} %collective-permute-done.2.refs_9_.refs_1_, f32[88,256]{1,0:T(8,128)S(1)} %collective-permute-done.3.refs_10_.refs_2_, ...), custom_call_target="tpu_custom_call" | custom-call | flops 1811939328 | bytes 999424 | tf_op jit(solution)/shard_map/sums_0/pallas_call | solution.py:521
  22.3 1.5 %collective-permute-start.6 = (f32[144,256]{1,0:T(8,128)S(1)}, f32[144,256]{1,0:T(8,128)S(1)}, u32[]{:S(2)}, u32[]{:S(2)}) collective-permute-start(f32[144,256]{1,0:T(8,128)S(1)} %get-tuple-element.69), channel_id=1, source_target_pairs={{0,28},{4,8},{8,4},{12,16},{16,12},{20,24},{24,20},{28,0},{1,29},{... | collective-permute-start | bytes 442376 | tf_op jit(solution)/shard_map/ppermute | solution.py:555
  23.8 1.2 %collective-permute-start.7 = (f32[72,256]{1,0:T(8,128)S(1)}, f32[72,256]{1,0:T(8,128)S(1)}, u32[]{:S(2)}, u32[]{:S(2)}) collective-permute-start(f32[72,256]{1,0:T(8,128)S(1)} %get-tuple-element.70), channel_id=1, source_target_pairs={{0,1},{1,0},{2,3},{3,2},{4,5},{5,4},{6,7},{7,6},{8,9},{9,8},{10,11... | collective-permute-start | bytes 221192 | tf_op jit(solution)/shard_map/ppermute | solution.py:551
  25.0 2.7 %collective-permute-start.8 = (f32[72,256]{1,0:T(8,128)S(1)}, f32[72,256]{1,0:T(8,128)S(1)}, u32[]{:S(2)}, u32[]{:S(2)}) collective-permute-start(f32[72,256]{1,0:T(8,128)S(1)} %get-tuple-element.71), channel_id=1, source_target_pairs={{0,3},{1,2},{2,1},{3,0},{4,7},{5,6},{6,5},{7,4},{8,11},{9,10},{10,... | collective-permute-start | bytes 221192 | tf_op jit(solution)/shard_map/ppermute | solution.py:550
  28.1 3.6 %collective-permute-done.8.refs_6_.refs_2_.refs_10_ = f32[72,256]{1,0:T(8,128)S(1)} collective-permute-done((f32[72,256]{1,0:T(8,128)S(1)}, f32[72,256]{1,0:T(8,128)S(1)}, u32[]{:S(2)}, u32[]{:S(2)}) %collective-permute-start.8) | collective-permute-done | bytes 73760 | tf_op jit(solution)/shard_map/ppermute | solution.py:550
  31.7 0.6 stress_0.1
  32.4 1.8 %collective-permute-start.10 = (f32[128,256]{1,0:T(8,128)S(1)}, f32[128,256]{1,0:T(8,128)S(1)}, u32[]{:S(2)}, u32[]{:S(2)}) collective-permute-start(f32[128,256]{1,0:T(8,128)S(1)} %get-tuple-element.79), channel_id=1, source_target_pairs={{0,28},{4,8},{8,4},{12,16},{16,12},{20,24},{24,20},{28,0},{1,29},{... | collective-permute-start | bytes 393224 | tf_op jit(solution)/shard_map/ppermute | solution.py:555
  34.2 3.0 %sums_1.1.refs_13_.refs_10_ = f32[216,256]{1,0:T(8,128)S(1)} custom-call(f32[24,256]{1,0:T(8,128)S(1)} %get-tuple-element.76.refs_0_.refs_5_, f32[72,256]{1,0:T(8,128)S(1)} %collective-permute-done.7.refs_5_.refs_1_.refs_9_, f32[72,256]{1,0:T(8,128)S(1)} %collective-permute-done.8.refs_6_.refs_2_.refs_10_, f32[24,256]{1,0:T(8,128)S(1)} %collective-permute-done.11.refs_3_, ...), custom_call_target="tpu_custom_call" | custom-call | flops 1811939328 | bytes 483328 | tf_op jit(solution)/shard_map/sums_1/pallas_call | solution.py:521
  37.1 2.0 %collective-permute-done.10.refs_8_ = f32[128,256]{1,0:T(8,128)S(1)} collective-permute-done((f32[128,256]{1,0:T(8,128)S(1)}, f32[128,256]{1,0:T(8,128)S(1)}, u32[]{:S(2)}, u32[]{:S(2)}) %collective-permute-start.10) | collective-permute-done | bytes 131104 | tf_op jit(solution)/shard_map/ppermute | solution.py:555
  39.1 4.1 %velocity_1.1 = (f32[3,128,256]{2,1,0:T(8,128)S(1)}, f32[120,256]{1,0:T(8,128)S(1)}, f32[120,256]{1,0:T(8,128)S(1)}, f32[72,256]{1,0:T(8,128)S(1)}, f32[72,256]{...) custom-call(f32[6,128,256]{2,1,0:T(8,128)S(1)} %get-tuple-element.75.refs_0_, ...), custom_call_target="tpu_custom_call" | custom-call | bytes 3096576 | tf_op jit(solution)/shard_map/velocity_1/pallas_call | solution.py:521
  43.3 1.0 %collective-permute-start.13 = (f32[120,256]{1,0:T(8,128)S(1)}, f32[120,256]{1,0:T(8,128)S(1)}, u32[]{:S(2)}, u32[]{:S(2)}) collective-permute-start(f32[120,256]{1,0:T(8,128)S(1)} %get-tuple-element.85), channel_id=1, source_target_pairs={{0,28},{4,8},{8,4},{12,16},{16,12},{20,24},{24,20},{28,0},{1,29},{... | collective-permute-start | bytes 368648 | tf_op jit(solution)/shard_map/ppermute | solution.py:555
  44.3 2.2 %collective-permute-start.15 = (f32[72,256]{1,0:T(8,128)S(1)}, f32[72,256]{1,0:T(8,128)S(1)}, u32[]{:S(2)}, u32[]{:S(2)}) collective-permute-start(f32[72,256]{1,0:T(8,128)S(1)} %get-tuple-element.87), channel_id=1, source_target_pairs={{0,3},{1,2},{2,1},{3,0},{4,7},{5,6},{6,5},{7,4},{8,11},{9,10},{10,... | collective-permute-start | bytes 221192 | tf_op jit(solution)/shard_map/ppermute | solution.py:550
  46.5 1.3 %collective-permute-start.18 = (f32[24,256]{1,0:T(8,128)S(1)}, f32[24,256]{1,0:T(8,128)S(1)}, u32[]{:S(2)}, u32[]{:S(2)}) collective-permute-start(f32[24,256]{1,0:T(8,128)S(1)} %get-tuple-element.90.refs_0_.refs_5_), channel_id=1, source_target_pairs={{0,2},{1,3},{2,0},{3,1},{4,6},{5,7},{6,4},{7,5},{8,10},{9,11},{10,... | collective-permute-start | bytes 73736 | tf_op jit(solution)/shard_map/ppermute | solution.py:562
  47.8 1.0 %collective-permute-done.14.refs_5_.refs_1_.refs_9_ = f32[72,256]{1,0:T(8,128)S(1)} collective-permute-done((f32[72,256]{1,0:T(8,128)S(1)}, f32[72,256]{1,0:T(8,128)S(1)}, u32[]{:S(2)}, u32[]{:S(2)}) %collective-permute-start.14) | collective-permute-done | bytes 73760 | tf_op jit(solution)/shard_map/ppermute | solution.py:551
  48.8 2.0 %collective-permute-done.15.refs_6_.refs_2_.refs_10_ = f32[72,256]{1,0:T(8,128)S(1)} collective-permute-done((f32[72,256]{1,0:T(8,128)S(1)}, f32[72,256]{1,0:T(8,128)S(1)}, u32[]{:S(2)}, u32[]{:S(2)}) %collective-permute-start.15) | collective-permute-done | bytes 73760 | tf_op jit(solution)/shard_map/ppermute | solution.py:550
  50.8 0.6 stress_1.1
  51.4 1.6 %collective-permute-start.17 = (f32[128,256]{1,0:T(8,128)S(1)}, f32[128,256]{1,0:T(8,128)S(1)}, u32[]{:S(2)}, u32[]{:S(2)}) collective-permute-start(f32[128,256]{1,0:T(8,128)S(1)} %get-tuple-element.93), channel_id=1, source_target_pairs={{0,28},{4,8},{8,4},{12,16},{16,12},{20,24},{24,20},{28,0},{1,29},{... | collective-permute-start | bytes 393224 | tf_op jit(solution)/shard_map/ppermute | solution.py:555
  53.1 3.0 %sums_2.1.refs_13_.refs_10_ = f32[216,256]{1,0:T(8,128)S(1)} custom-call(f32[24,256]{1,0:T(8,128)S(1)} %get-tuple-element.90.refs_0_.refs_5_, f32[72,256]{1,0:T(8,128)S(1)} %collective-permute-done.14.refs_5_.refs_1_.refs_9_, f32[72,256]{1,0:T(8,128)S(1)} %collective-permute-done.15.refs_6_.refs_2_.refs_10_, f32[24,256]{1,0:T(8,128)S(1)} %collective-permute-done.18.refs_3_, ...), custom_call_target="tpu_custom_call" | custom-call | flops 1811939328 | bytes 483328 | tf_op jit(solution)/shard_map/sums_2/pallas_call | solution.py:521
  56.1 1.9 %collective-permute-done.17.refs_8_ = f32[128,256]{1,0:T(8,128)S(1)} collective-permute-done((f32[128,256]{1,0:T(8,128)S(1)}, f32[128,256]{1,0:T(8,128)S(1)}, u32[]{:S(2)}, u32[]{:S(2)}) %collective-permute-start.17) | collective-permute-done | bytes 131104 | tf_op jit(solution)/shard_map/ppermute | solution.py:555
  57.9 2.5 %velocity_2.1 = (f32[3,128,256]{2,1,0:T(8,128)S(1)}, f32[120,256]{1,0:T(8,128)S(1)}, f32[120,256]{1,0:T(8,128)S(1)}, f32[24,256]{1,0:T(8,128)S(1)}, f32[24,256]{1,0:T(8,128)S(1)}) custom-call(f32[6,128,256]{2,1,0:T(8,128)S(1)} %get-tuple-element.89.refs_0_, f32[3,128,256]{2,1,0:T(8,128)S(1)} %get-tuple-element.83.refs_1_, ...), custom_call_target="tpu_custom_call" | custom-call | bytes 2875392 | tf_op jit(solution)/shard_map/velocity_2/pallas_call | solution.py:521
  60.5 0.9 %collective-permute-start.20 = (f32[120,256]{1,0:T(8,128)S(1)}, f32[120,256]{1,0:T(8,128)S(1)}, u32[]{:S(2)}, u32[]{:S(2)}) collective-permute-start(f32[120,256]{1,0:T(8,128)S(1)} %get-tuple-element.97), channel_id=1, source_target_pairs={{0,28},{4,8},{8,4},{12,16},{16,12},{20,24},{24,20},{28,0},{1,29},{... | collective-permute-start | bytes 368648 | tf_op jit(solution)/shard_map/ppermute | solution.py:555
  61.4 2.0 %collective-permute-start.21 = (f32[24,256]{1,0:T(8,128)S(1)}, f32[24,256]{1,0:T(8,128)S(1)}, u32[]{:S(2)}, u32[]{:S(2)}) collective-permute-start(f32[24,256]{1,0:T(8,128)S(1)} %get-tuple-element.98), channel_id=1, source_target_pairs={{0,1},{1,0},{2,3},{3,2},{4,5},{5,4},{6,7},{7,6},{8,9},{9,8},{10,11... | collective-permute-start | bytes 73736 | tf_op jit(solution)/shard_map/ppermute | solution.py:551
  63.5 2.4 %collective-permute-start.22 = (f32[24,256]{1,0:T(8,128)S(1)}, f32[24,256]{1,0:T(8,128)S(1)}, u32[]{:S(2)}, u32[]{:S(2)}) collective-permute-start(f32[24,256]{1,0:T(8,128)S(1)} %get-tuple-element.99), channel_id=1, source_target_pairs={{0,3},{1,2},{2,1},{3,0},{4,7},{5,6},{6,5},{7,4},{8,11},{9,10},{10,... | collective-permute-start | bytes 73736 | tf_op jit(solution)/shard_map/ppermute | solution.py:550
  65.9 3.2 %collective-permute-done.22.refs_6_ = f32[24,256]{1,0:T(8,128)S(1)} collective-permute-done((f32[24,256]{1,0:T(8,128)S(1)}, f32[24,256]{1,0:T(8,128)S(1)}, u32[]{:S(2)}, u32[]{:S(2)}) %collective-permute-start.22) | collective-permute-done | bytes 24608 | tf_op jit(solution)/shard_map/ppermute | solution.py:550
  69.1 1.4 %stress_2.1 = (f32[6,128,256]{2,1,0:T(8,128)}, f32[3,128,256]{2,1,0:T(8,128)}, f32[3,6144]{1,0:T(4,128)}) custom-call(f32[6,128,256]{2,1,0:T(8,128)S(1)} %get-tuple-element.89.refs_0_, f32[3,128,256]{2,1,0:T(8,128)S(1)} %get-tuple-element.95.refs_1_, s32[128,256]{1,0:T(8,128)S(1)} %get-tuple-element.65.refs_2_, ...), custom_call_target="tpu_custom_call" | custom-call | bytes 3276800 | tf_op jit(solution)/shard_map/stress_2/pallas_call | solution.py:521
  (24 shorter events, 1.3 us)
Async XLA Ops:
  3.1 12.2 %collective-permute-start = (f32[120,256]{1,0:T(8,128)S(1)}, f32[120,256]{1,0:T(8,128)S(1)}, u32[]{:S(2)}, u32[]{:S(2)}) collective-permute-start(f32[120,256]{1,0:T(8,128)S(1)} %get-tuple-element.60), channel_id=1, source_target_pairs={{0,4},{4,0},{8,12},{12,8},{16,20},{20,16},{24,28},{28,24},{1,5},{5... | collective-permute-start | bytes 368648 | tf_op jit(solution)/shard_map/ppermute | solution.py:556
  3.7 11.6 %collective-permute-start.1 = (f32[120,256]{1,0:T(8,128)S(1)}, f32[120,256]{1,0:T(8,128)S(1)}, u32[]{:S(2)}, u32[]{:S(2)}) collective-permute-start(f32[120,256]{1,0:T(8,128)S(1)} %get-tuple-element.61), channel_id=1, source_target_pairs={{0,28},{4,8},{8,4},{12,16},{16,12},{20,24},{24,20},{28,0},{1,29},{... | collective-permute-start | bytes 368648 | tf_op jit(solution)/shard_map/ppermute | solution.py:555
  7.2 4.5 %collective-permute-start.2 = (f32[88,256]{1,0:T(8,128)S(1)}, f32[88,256]{1,0:T(8,128)S(1)}, u32[]{:S(2)}, u32[]{:S(2)}) collective-permute-start(f32[88,256]{1,0:T(8,128)S(1)} %get-tuple-element.62), channel_id=1, source_target_pairs={{0,1},{1,0},{2,3},{3,2},{4,5},{5,4},{6,7},{7,6},{8,9},{9,8},{10,11... | collective-permute-start | bytes 270344 | tf_op jit(solution)/shard_map/ppermute | solution.py:551
  8.8 6.5 %collective-permute-start.3 = (f32[88,256]{1,0:T(8,128)S(1)}, f32[88,256]{1,0:T(8,128)S(1)}, u32[]{:S(2)}, u32[]{:S(2)}) collective-permute-start(f32[88,256]{1,0:T(8,128)S(1)} %get-tuple-element.63), channel_id=1, source_target_pairs={{0,3},{1,2},{2,1},{3,0},{4,7},{5,6},{6,5},{7,4},{8,11},{9,10},{10,... | collective-permute-start | bytes 270344 | tf_op jit(solution)/shard_map/ppermute | solution.py:550
  11.3 7.9 %collective-permute-start.4 = (f32[32,256]{1,0:T(8,128)S(1)}, f32[32,256]{1,0:T(8,128)S(1)}, u32[]{:S(2)}, u32[]{:S(2)}) collective-permute-start(f32[32,256]{1,0:T(8,128)S(1)} %get-tuple-element.58.refs_5_.refs_0_), channel_id=1, source_target_pairs={{0,2},{1,3},{2,0},{3,1},{4,6},{5,7},{6,4},{7,5},{8,10},{9,11},{10,... | collective-permute-start | bytes 98312 | tf_op jit(solution)/shard_map/ppermute | solution.py:562
  22.2 9.5 %collective-permute-start.5 = (f32[144,256]{1,0:T(8,128)S(1)}, f32[144,256]{1,0:T(8,128)S(1)}, u32[]{:S(2)}, u32[]{:S(2)}) collective-permute-start(f32[144,256]{1,0:T(8,128)S(1)} %get-tuple-element.68), channel_id=1, source_target_pairs={{0,4},{4,0},{8,12},{12,8},{16,20},{20,16},{24,28},{28,24},{1,5},{5... | collective-permute-start | bytes 442376 | tf_op jit(solution)/shard_map/ppermute | solution.py:556
  22.3 9.4 %collective-permute-start.6 = (f32[144,256]{1,0:T(8,128)S(1)}, f32[144,256]{1,0:T(8,128)S(1)}, u32[]{:S(2)}, u32[]{:S(2)}) collective-permute-start(f32[144,256]{1,0:T(8,128)S(1)} %get-tuple-element.69), channel_id=1, source_target_pairs={{0,28},{4,8},{8,4},{12,16},{16,12},{20,24},{24,20},{28,0},{1,29},{... | collective-permute-start | bytes 442376 | tf_op jit(solution)/shard_map/ppermute | solution.py:555
  23.8 4.4 %collective-permute-start.7 = (f32[72,256]{1,0:T(8,128)S(1)}, f32[72,256]{1,0:T(8,128)S(1)}, u32[]{:S(2)}, u32[]{:S(2)}) collective-permute-start(f32[72,256]{1,0:T(8,128)S(1)} %get-tuple-element.70), channel_id=1, source_target_pairs={{0,1},{1,0},{2,3},{3,2},{4,5},{5,4},{6,7},{7,6},{8,9},{9,8},{10,11... | collective-permute-start | bytes 221192 | tf_op jit(solution)/shard_map/ppermute | solution.py:551
  25.0 6.7 %collective-permute-start.8 = (f32[72,256]{1,0:T(8,128)S(1)}, f32[72,256]{1,0:T(8,128)S(1)}, u32[]{:S(2)}, u32[]{:S(2)}) collective-permute-start(f32[72,256]{1,0:T(8,128)S(1)} %get-tuple-element.71), channel_id=1, source_target_pairs={{0,3},{1,2},{2,1},{3,0},{4,7},{5,6},{6,5},{7,4},{8,11},{9,10},{10,... | collective-permute-start | bytes 221192 | tf_op jit(solution)/shard_map/ppermute | solution.py:550
  27.7 6.5 %collective-permute-start.11 = (f32[24,256]{1,0:T(8,128)S(1)}, f32[24,256]{1,0:T(8,128)S(1)}, u32[]{:S(2)}, u32[]{:S(2)}) collective-permute-start(f32[24,256]{1,0:T(8,128)S(1)} %get-tuple-element.76.refs_0_.refs_5_), channel_id=1, source_target_pairs={{0,2},{1,3},{2,0},{3,1},{4,6},{5,7},{6,4},{7,5},{8,10},{9,11},{10,... | collective-permute-start | bytes 73736 | tf_op jit(solution)/shard_map/ppermute | solution.py:562
  32.3 4.8 %collective-permute-start.9 = (f32[128,256]{1,0:T(8,128)S(1)}, f32[128,256]{1,0:T(8,128)S(1)}, u32[]{:S(2)}, u32[]{:S(2)}) collective-permute-start(f32[128,256]{1,0:T(8,128)S(1)} %get-tuple-element.78), channel_id=1, source_target_pairs={{0,4},{4,0},{8,12},{12,8},{16,20},{20,16},{24,28},{28,24},{1,5},{5... | collective-permute-start | bytes 393224 | tf_op jit(solution)/shard_map/ppermute | solution.py:556
  32.4 6.7 %collective-permute-start.10 = (f32[128,256]{1,0:T(8,128)S(1)}, f32[128,256]{1,0:T(8,128)S(1)}, u32[]{:S(2)}, u32[]{:S(2)}) collective-permute-start(f32[128,256]{1,0:T(8,128)S(1)} %get-tuple-element.79), channel_id=1, source_target_pairs={{0,28},{4,8},{8,4},{12,16},{16,12},{20,24},{24,20},{28,0},{1,29},{... | collective-permute-start | bytes 393224 | tf_op jit(solution)/shard_map/ppermute | solution.py:555
  43.2 7.6 %collective-permute-start.12 = (f32[120,256]{1,0:T(8,128)S(1)}, f32[120,256]{1,0:T(8,128)S(1)}, u32[]{:S(2)}, u32[]{:S(2)}) collective-permute-start(f32[120,256]{1,0:T(8,128)S(1)} %get-tuple-element.84), channel_id=1, source_target_pairs={{0,4},{4,0},{8,12},{12,8},{16,20},{20,16},{24,28},{28,24},{1,5},{5... | collective-permute-start | bytes 368648 | tf_op jit(solution)/shard_map/ppermute | solution.py:556
  43.3 7.5 %collective-permute-start.13 = (f32[120,256]{1,0:T(8,128)S(1)}, f32[120,256]{1,0:T(8,128)S(1)}, u32[]{:S(2)}, u32[]{:S(2)}) collective-permute-start(f32[120,256]{1,0:T(8,128)S(1)} %get-tuple-element.85), channel_id=1, source_target_pairs={{0,28},{4,8},{8,4},{12,16},{16,12},{20,24},{24,20},{28,0},{1,29},{... | collective-permute-start | bytes 368648 | tf_op jit(solution)/shard_map/ppermute | solution.py:555
  44.3 4.5 %collective-permute-start.14 = (f32[72,256]{1,0:T(8,128)S(1)}, f32[72,256]{1,0:T(8,128)S(1)}, u32[]{:S(2)}, u32[]{:S(2)}) collective-permute-start(f32[72,256]{1,0:T(8,128)S(1)} %get-tuple-element.86), channel_id=1, source_target_pairs={{0,1},{1,0},{2,3},{3,2},{4,5},{5,4},{6,7},{7,6},{8,9},{9,8},{10,11... | collective-permute-start | bytes 221192 | tf_op jit(solution)/shard_map/ppermute | solution.py:551
  44.3 6.5 %collective-permute-start.15 = (f32[72,256]{1,0:T(8,128)S(1)}, f32[72,256]{1,0:T(8,128)S(1)}, u32[]{:S(2)}, u32[]{:S(2)}) collective-permute-start(f32[72,256]{1,0:T(8,128)S(1)} %get-tuple-element.87), channel_id=1, source_target_pairs={{0,3},{1,2},{2,1},{3,0},{4,7},{5,6},{6,5},{7,4},{8,11},{9,10},{10,... | collective-permute-start | bytes 221192 | tf_op jit(solution)/shard_map/ppermute | solution.py:550
  46.5 6.6 %collective-permute-start.18 = (f32[24,256]{1,0:T(8,128)S(1)}, f32[24,256]{1,0:T(8,128)S(1)}, u32[]{:S(2)}, u32[]{:S(2)}) collective-permute-start(f32[24,256]{1,0:T(8,128)S(1)} %get-tuple-element.90.refs_0_.refs_5_), channel_id=1, source_target_pairs={{0,2},{1,3},{2,0},{3,1},{4,6},{5,7},{6,4},{7,5},{8,10},{9,11},{10,... | collective-permute-start | bytes 73736 | tf_op jit(solution)/shard_map/ppermute | solution.py:562
  51.4 4.7 %collective-permute-start.16 = (f32[128,256]{1,0:T(8,128)S(1)}, f32[128,256]{1,0:T(8,128)S(1)}, u32[]{:S(2)}, u32[]{:S(2)}) collective-permute-start(f32[128,256]{1,0:T(8,128)S(1)} %get-tuple-element.92), channel_id=1, source_target_pairs={{0,4},{4,0},{8,12},{12,8},{16,20},{20,16},{24,28},{28,24},{1,5},{5... | collective-permute-start | bytes 393224 | tf_op jit(solution)/shard_map/ppermute | solution.py:556
  51.4 6.5 %collective-permute-start.17 = (f32[128,256]{1,0:T(8,128)S(1)}, f32[128,256]{1,0:T(8,128)S(1)}, u32[]{:S(2)}, u32[]{:S(2)}) collective-permute-start(f32[128,256]{1,0:T(8,128)S(1)} %get-tuple-element.93), channel_id=1, source_target_pairs={{0,28},{4,8},{8,4},{12,16},{16,12},{20,24},{24,20},{28,0},{1,29},{... | collective-permute-start | bytes 393224 | tf_op jit(solution)/shard_map/ppermute | solution.py:555
  60.4 8.7 %collective-permute-start.19 = (f32[120,256]{1,0:T(8,128)S(1)}, f32[120,256]{1,0:T(8,128)S(1)}, u32[]{:S(2)}, u32[]{:S(2)}) collective-permute-start(f32[120,256]{1,0:T(8,128)S(1)} %get-tuple-element.96), channel_id=1, source_target_pairs={{0,4},{4,0},{8,12},{12,8},{16,20},{20,16},{24,28},{28,24},{1,5},{5... | collective-permute-start | bytes 368648 | tf_op jit(solution)/shard_map/ppermute | solution.py:556
  60.5 8.6 %collective-permute-start.20 = (f32[120,256]{1,0:T(8,128)S(1)}, f32[120,256]{1,0:T(8,128)S(1)}, u32[]{:S(2)}, u32[]{:S(2)}) collective-permute-start(f32[120,256]{1,0:T(8,128)S(1)} %get-tuple-element.97), channel_id=1, source_target_pairs={{0,28},{4,8},{8,4},{12,16},{16,12},{20,24},{24,20},{28,0},{1,29},{... | collective-permute-start | bytes 368648 | tf_op jit(solution)/shard_map/ppermute | solution.py:555
  61.4 4.5 %collective-permute-start.21 = (f32[24,256]{1,0:T(8,128)S(1)}, f32[24,256]{1,0:T(8,128)S(1)}, u32[]{:S(2)}, u32[]{:S(2)}) collective-permute-start(f32[24,256]{1,0:T(8,128)S(1)} %get-tuple-element.98), channel_id=1, source_target_pairs={{0,1},{1,0},{2,3},{3,2},{4,5},{5,4},{6,7},{7,6},{8,9},{9,8},{10,11... | collective-permute-start | bytes 73736 | tf_op jit(solution)/shard_map/ppermute | solution.py:551
  63.5 5.6 %collective-permute-start.22 = (f32[24,256]{1,0:T(8,128)S(1)}, f32[24,256]{1,0:T(8,128)S(1)}, u32[]{:S(2)}, u32[]{:S(2)}) collective-permute-start(f32[24,256]{1,0:T(8,128)S(1)} %get-tuple-element.99), channel_id=1, source_target_pairs={{0,3},{1,2},{2,1},{3,0},{4,7},{5,6},{6,5},{7,4},{8,11},{9,10},{10,... | collective-permute-start | bytes 73736 | tf_op jit(solution)/shard_map/ppermute | solution.py:550

commit v5 on v4

--- a/solution.py
+++ b/solution.py
@@ -7,6 +7,7 @@
 from jax.experimental import pallas as pl
 from jax.experimental.pallas import tpu as pltpu
 from jax.sharding import PartitionSpec as P
+
 
 STEPS = 3
 time_step = 0.2
@@ -130,7 +131,7 @@
         to_pb[i * cz : (i + 1) * cz, :] = jnp.where(even, first, last)
 
 
-def store_split(sz, source, parts, rows, refs):
+def store_split(source, parts, rows, refs):
     for c in range(parts):
         high, low = split(source(c))
         refs[0][c * rows : (c + 1) * rows, :] = high
@@ -260,7 +261,7 @@
         elem_ids[j : j + 1, :] = lax.shift_right_arithmetic(elem, 8)
         elem_ids[kn + j : kn + j + 1, :] = lax.bitwise_and(elem, COLS - 1)
         to_all[3 * kn + j : 3 * kn + j + 1, :] = jnp.where(cell >= 0, elem, -1).astype(F32)
-    store_split(sz, lambda c: velocity[c], 3, sz.rows, (high, low))
+    store_split(lambda c: velocity[c], 3, sz.rows, (high, low))
     gather_cells(sz, (high, low), cell_ids, to_all)
     for copy in copies[3:]:
         copy.wait()
@@ -290,9 +291,7 @@
 ):
     kn, rows, wp, cx, cz = sz.kn, sz.rows, sz.wp, sz.cx, sz.cz
     pile_high, pile_low = high.at[0 : 3 * wp, :], low.at[0 : 3 * wp, :]
-    store_split(
-        sz, lambda c: jnp.concatenate(list(window_of(c)), axis=0), 3, wp, (pile_high, pile_low)
-    )
+    store_split(lambda c: jnp.concatenate(list(window_of(c)), axis=0), 3, wp, (pile_high, pile_low))
     total = None
     for j in range(kn):
         at_pile = gather_chunk(
@@ -433,7 +432,7 @@
     ]
     send_columns(sz, plan, ends, to_pa, to_pb)
     if step < STEPS - 1:
-        store_split(sz, lambda c: out[c], 3, sz.rows, (high, low))
+        store_split(lambda c: out[c], 3, sz.rows, (high, low))
         gather_cells(sz, (high, low), cell_ids, to_all)
         to_pa[6 * cz :, :] = to_all[...]
         to_pb[6 * cz :, :] = to_all[...]
@@ -514,7 +513,7 @@
         copy.wait()
 
 
-def call(body, name, ins, outs, scratch=(), copies=0, far_ins=False, far_outs=False, flops=0):
+def call(body, ins, outs, scratch=(), copies=0, far_ins=False, far_outs=False, flops=0):
     vmem, far = pl.BlockSpec(memory_space=pltpu.VMEM), pl.BlockSpec(memory_space=pl.ANY)
     sems = [pltpu.SemaphoreType.DMA((copies,))] if copies else []
     moved = sum(4 * x.size for x in ins) + sum(4 * math.prod(shape) for shape, _ in outs)
@@ -526,7 +525,6 @@
         scratch_shapes=[pltpu.VMEM(shape, dtype) for shape, dtype in scratch] + sems,
         compiler_params=pltpu.CompilerParams(vmem_limit_bytes=48 * 2**20),
         cost_estimate=pl.CostEstimate(flops=flops, bytes_accessed=moved, transcendentals=0),
-        name=name,
     )(*[pltpu.with_memory_space_constraint(x, pltpu.HBM) if far_ins else x for x in ins])
 
 
@@ -557,10 +555,12 @@
         return [da, db]
 
     def to_others(x):
-        shifts = range(2, sz.np - 1)
-        return [
-            lax.ppermute(x, "plan", [(i, (i + s) % sz.np) for i in range(sz.np)]) for s in shifts
-        ]
+        found = []
+        for s in range(2, sz.np - 1):
+            found.append(
+                lax.ppermute(x, "plan", [(i, (i + s) % sz.np) for i in range(sz.np)])
+            )
+        return found
 
     full_shape = stress.shape, velocity.shape
     stress = stress.reshape(6, rows, cy)
@@ -576,7 +576,6 @@
 
     to = call(
         functools.partial(first_kernel, sz),
-        "first",
         [
             pair_cell, velocity, pair_elem, pile_velocity, pile_mass.reshape(1, -1), jack_force,
             stress, flags, density,
@@ -605,7 +604,6 @@
         state = [] if step == 0 else [columns, column_flags, acc]
         moved = call(
             functools.partial(velocity_kernel, sz, step),
-            f"velocity_{step}",
             [stress, velocity, density, cell_ids, elem_ids, at_cells, pile]
             + by_depth
             + by_plan
@@ -627,7 +625,6 @@
             column_flags = moved[7]
             *layer, acc, set_ids = call(
                 functools.partial(sums_kernel, sz, 0),
-                "sums_0",
                 sets + layer,
                 layers(4 * pr)
                 + [((4 * wp, COLS), F32), ((sz.np, 2 * kn, COLS), I32)],
@@ -640,7 +637,6 @@
         if last:
             stress, velocity, pile = call(
                 functools.partial(stress_kernel, sz, step),
-                f"stress_{step}",
                 ins,
                 [(stress.shape, F32), (velocity.shape, F32), (pile_velocity.shape, F32)],
                 [(stress.shape, F32), ((pr3, COLS), F32), (pile_velocity.shape, F32)],
@@ -650,7 +646,6 @@
             break
         got = call(
             functools.partial(stress_kernel, sz, step),
-            f"stress_{step}",
             ins,
             [(stress.shape, F32)]
             + layers(8 + pr3)
@@ -662,7 +657,6 @@
         by_depth = swap_depth(*got[1:3])
         (acc,) = call(
             functools.partial(sums_kernel, sz, step + 1),
-            f"sums_{step + 1}",
             [at_cells, *by_plan, *others, set_ids],
             [((3 * wp, COLS), F32)],
             [((sz.np, 3 * kn, COLS), F32)],

time: 70.8 us -> 70.8 us (level)
  no operation moved by 1% of the time
where the time goes in v5:
time: 70.8 us; the launch traced here: 70.6 us
  starting transfers between devices  27.3 us (39%)
  Pallas kernels  24.4 us (34%)
  waiting for transfers between devices  18 us (25%)
  between operations  0.93 us (1%)
    pallas_call x10, Pallas kernels, call(): pl.pallas_call(body, out_shape=[jax.ShapeDtypeStruct(shape, dtype) for sh...  24.4 us
    ppermute x4, waiting for transfers between devices, swap_plan(): pb = lax.ppermute(pb, 'plan', p_second)  12.3 us
    ppermute x6, starting transfers between devices, swap_depth(): db = lax.ppermute(db, 'depth', d_second)  10.4 us
    ppermute x4, starting transfers between devices, swap_plan(): pb = lax.ppermute(pb, 'plan', p_second)  9.79 us
    ppermute x4, starting transfers between devices, swap_plan(): pa = lax.ppermute(pa, 'plan', p_first)  4.86 us
    ppermute x6, waiting for transfers between devices, swap_depth(): db = lax.ppermute(db, 'depth', d_second)  3.88 us
    ppermute x4, waiting for transfers between devices, swap_plan(): pa = lax.ppermute(pa, 'plan', p_first)  1.83 us
  transfers between devices with their start and end apart: 23, of which 9 were waited for; matrix products, arithmetic and copies ran while one was open for 0% of the time, Pallas kernels for 16%

profile of v5, /device:TPU:0, one launch (start us, length us, event | category | flops | bytes accessed | tf_op | source)
XLA Modules:
  0.0 70.6 jit_solution(9200832694469122999)
XLA Ops:
  0.6 2.5 %shard_map.112 = (f32[120,256]{1,0:T(8,128)S(1)}, f32[120,256]{1,0:T(8,128)S(1)}, f32[88,256]{1,0:T(8,128)S(1)}, f32[88,256]{1,0:T(8,128)S(1)}, f32[32,256]{1,0:...) custom-call(s32[1,2048]{1,0:T(1,128)} %refs_0_.1, ...), custom_call_target="tpu_custom_call" | custom-call | bytes 3735552 | tf_op jit(solution)/shard_map/pallas_call | solution.py:520
  3.1 0.6 collective-permute-start
  3.7 3.5 %collective-permute-start.1 = (f32[120,256]{1,0:T(8,128)S(1)}, f32[120,256]{1,0:T(8,128)S(1)}, u32[]{:S(2)}, u32[]{:S(2)}) collective-permute-start(f32[120,256]{1,0:T(8,128)S(1)} %get-tuple-element.61), channel_id=1, source_target_pairs={{0,28},{4,8},{8,4},{12,16},{16,12},{20,24},{24,20},{28,0},{1,29},{... | collective-permute-start | bytes 368648 | tf_op jit(solution)/shard_map/ppermute | solution.py:553
  7.2 1.6 %collective-permute-start.2 = (f32[88,256]{1,0:T(8,128)S(1)}, f32[88,256]{1,0:T(8,128)S(1)}, u32[]{:S(2)}, u32[]{:S(2)}) collective-permute-start(f32[88,256]{1,0:T(8,128)S(1)} %get-tuple-element.62), channel_id=1, source_target_pairs={{0,1},{1,0},{2,3},{3,2},{4,5},{5,4},{6,7},{7,6},{8,9},{9,8},{10,11... | collective-permute-start | bytes 270344 | tf_op jit(solution)/shard_map/ppermute | solution.py:549
  8.8 2.5 %collective-permute-start.3 = (f32[88,256]{1,0:T(8,128)S(1)}, f32[88,256]{1,0:T(8,128)S(1)}, u32[]{:S(2)}, u32[]{:S(2)}) collective-permute-start(f32[88,256]{1,0:T(8,128)S(1)} %get-tuple-element.63), channel_id=1, source_target_pairs={{0,3},{1,2},{2,1},{3,0},{4,7},{5,6},{6,5},{7,4},{8,11},{9,10},{10,... | collective-permute-start | bytes 270344 | tf_op jit(solution)/shard_map/ppermute | solution.py:548
  11.7 3.5 %collective-permute-done.3.refs_10_.refs_2_ = f32[88,256]{1,0:T(8,128)S(1)} collective-permute-done((f32[88,256]{1,0:T(8,128)S(1)}, f32[88,256]{1,0:T(8,128)S(1)}, u32[]{:S(2)}, u32[]{:S(2)}) %collective-permute-start.3) | collective-permute-done | bytes 90144 | tf_op jit(solution)/shard_map/ppermute | solution.py:548
  15.3 3.9 %shard_map.113 = (f32[3,128,256]{2,1,0:T(8,128)S(1)}, f32[48,256]{1,0:T(8,128)S(1)}, f32[48,256]{1,0:T(8,128)S(1)}, f32[72,256]{1,0:T(8,128)S(1)}, f32[72,256]{1...) custom-call(f32[6,128,256]{2,1,0:T(8,128)S(1)} %get-tuple-element.53.refs_0_, ...), custom_call_target="tpu_custom_call" | custom-call | bytes 2654208 | tf_op jit(solution)/shard_map/pallas_call | solution.py:520
  19.2 3.0 %shard_map.114 = (f32[144,256]{1,0:T(8,128)S(1)}, f32[144,256]{1,0:T(8,128)S(1)}, f32[288,256]{1,0:T(8,128)S(1)}, s32[4,16,256]{2,1,0:T(8,128)S(1)}) custom-call(f32[32,256]{1,0:T(8,128)S(1)} %get-tuple-element.58.refs_5_.refs_0_, f32[88,256]{1,0:T(8,128)S(1)} %collective-permute-done.2.refs_9_.refs_1_, ...), custom_call_target="tpu_custom_call" | custom-call | flops 1811939328 | bytes 999424 | tf_op jit(solution)/shard_map/pallas_call | solution.py:520
  22.3 1.5 %collective-permute-start.6 = (f32[144,256]{1,0:T(8,128)S(1)}, f32[144,256]{1,0:T(8,128)S(1)}, u32[]{:S(2)}, u32[]{:S(2)}) collective-permute-start(f32[144,256]{1,0:T(8,128)S(1)} %get-tuple-element.69), channel_id=1, source_target_pairs={{0,28},{4,8},{8,4},{12,16},{16,12},{20,24},{24,20},{28,0},{1,29},{... | collective-permute-start | bytes 442376 | tf_op jit(solution)/shard_map/ppermute | solution.py:553
  23.8 1.2 %collective-permute-start.7 = (f32[72,256]{1,0:T(8,128)S(1)}, f32[72,256]{1,0:T(8,128)S(1)}, u32[]{:S(2)}, u32[]{:S(2)}) collective-permute-start(f32[72,256]{1,0:T(8,128)S(1)} %get-tuple-element.70), channel_id=1, source_target_pairs={{0,1},{1,0},{2,3},{3,2},{4,5},{5,4},{6,7},{7,6},{8,9},{9,8},{10,11... | collective-permute-start | bytes 221192 | tf_op jit(solution)/shard_map/ppermute | solution.py:549
  25.0 2.7 %collective-permute-start.8 = (f32[72,256]{1,0:T(8,128)S(1)}, f32[72,256]{1,0:T(8,128)S(1)}, u32[]{:S(2)}, u32[]{:S(2)}) collective-permute-start(f32[72,256]{1,0:T(8,128)S(1)} %get-tuple-element.71), channel_id=1, source_target_pairs={{0,3},{1,2},{2,1},{3,0},{4,7},{5,6},{6,5},{7,4},{8,11},{9,10},{10,... | collective-permute-start | bytes 221192 | tf_op jit(solution)/shard_map/ppermute | solution.py:548
  28.1 3.6 %collective-permute-done.8.refs_6_.refs_2_.refs_10_ = f32[72,256]{1,0:T(8,128)S(1)} collective-permute-done((f32[72,256]{1,0:T(8,128)S(1)}, f32[72,256]{1,0:T(8,128)S(1)}, u32[]{:S(2)}, u32[]{:S(2)}) %collective-permute-start.8) | collective-permute-done | bytes 73760 | tf_op jit(solution)/shard_map/ppermute | solution.py:548
  31.7 0.6 shard_map.115
  32.4 1.8 %collective-permute-start.10 = (f32[128,256]{1,0:T(8,128)S(1)}, f32[128,256]{1,0:T(8,128)S(1)}, u32[]{:S(2)}, u32[]{:S(2)}) collective-permute-start(f32[128,256]{1,0:T(8,128)S(1)} %get-tuple-element.79), channel_id=1, source_target_pairs={{0,28},{4,8},{8,4},{12,16},{16,12},{20,24},{24,20},{28,0},{1,29},{... | collective-permute-start | bytes 393224 | tf_op jit(solution)/shard_map/ppermute | solution.py:553
  34.2 3.0 %shard_map.116.refs_13_.refs_10_ = f32[216,256]{1,0:T(8,128)S(1)} custom-call(f32[24,256]{1,0:T(8,128)S(1)} %get-tuple-element.76.refs_0_.refs_5_, f32[72,256]{1,0:T(8,128)S(1)} %collective-permute-done.7.refs_5_.refs_1_.refs_9_, f32[72,256]{1,0:T(8,128)S(1)} %collective-permute-done.8.refs_6_.refs_2_.refs_10_, ...), custom_call_target="tpu_custom_call" | custom-call | flops 1811939328 | bytes 483328 | tf_op jit(solution)/shard_map/pallas_call | solution.py:520
  37.1 2.0 %collective-permute-done.10.refs_8_ = f32[128,256]{1,0:T(8,128)S(1)} collective-permute-done((f32[128,256]{1,0:T(8,128)S(1)}, f32[128,256]{1,0:T(8,128)S(1)}, u32[]{:S(2)}, u32[]{:S(2)}) %collective-permute-start.10) | collective-permute-done | bytes 131104 | tf_op jit(solution)/shard_map/ppermute | solution.py:553
  39.1 4.1 %shard_map.117 = (f32[3,128,256]{2,1,0:T(8,128)S(1)}, f32[120,256]{1,0:T(8,128)S(1)}, f32[120,256]{1,0:T(8,128)S(1)}, f32[72,256]{1,0:T(8,128)S(1)}, f32[72,256]...) custom-call(f32[6,128,256]{2,1,0:T(8,128)S(1)} %get-tuple-element.75.refs_0_, ...), custom_call_target="tpu_custom_call" | custom-call | bytes 3096576 | tf_op jit(solution)/shard_map/pallas_call | solution.py:520
  43.3 1.0 %collective-permute-start.13 = (f32[120,256]{1,0:T(8,128)S(1)}, f32[120,256]{1,0:T(8,128)S(1)}, u32[]{:S(2)}, u32[]{:S(2)}) collective-permute-start(f32[120,256]{1,0:T(8,128)S(1)} %get-tuple-element.85), channel_id=1, source_target_pairs={{0,28},{4,8},{8,4},{12,16},{16,12},{20,24},{24,20},{28,0},{1,29},{... | collective-permute-start | bytes 368648 | tf_op jit(solution)/shard_map/ppermute | solution.py:553
  44.3 2.2 %collective-permute-start.15 = (f32[72,256]{1,0:T(8,128)S(1)}, f32[72,256]{1,0:T(8,128)S(1)}, u32[]{:S(2)}, u32[]{:S(2)}) collective-permute-start(f32[72,256]{1,0:T(8,128)S(1)} %get-tuple-element.87), channel_id=1, source_target_pairs={{0,3},{1,2},{2,1},{3,0},{4,7},{5,6},{6,5},{7,4},{8,11},{9,10},{10,... | collective-permute-start | bytes 221192 | tf_op jit(solution)/shard_map/ppermute | solution.py:548
  46.5 1.3 %collective-permute-start.18 = (f32[24,256]{1,0:T(8,128)S(1)}, f32[24,256]{1,0:T(8,128)S(1)}, u32[]{:S(2)}, u32[]{:S(2)}) collective-permute-start(f32[24,256]{1,0:T(8,128)S(1)} %get-tuple-element.90.refs_0_.refs_5_), channel_id=1, source_target_pairs={{0,2},{1,3},{2,0},{3,1},{4,6},{5,7},{6,4},{7,5},{8,10},{9,11},{10,... | collective-permute-start | bytes 73736 | tf_op jit(solution)/shard_map/ppermute | solution.py:561
  47.8 1.0 %collective-permute-done.14.refs_5_.refs_1_.refs_9_ = f32[72,256]{1,0:T(8,128)S(1)} collective-permute-done((f32[72,256]{1,0:T(8,128)S(1)}, f32[72,256]{1,0:T(8,128)S(1)}, u32[]{:S(2)}, u32[]{:S(2)}) %collective-permute-start.14) | collective-permute-done | bytes 73760 | tf_op jit(solution)/shard_map/ppermute | solution.py:549
  48.8 2.0 %collective-permute-done.15.refs_6_.refs_2_.refs_10_ = f32[72,256]{1,0:T(8,128)S(1)} collective-permute-done((f32[72,256]{1,0:T(8,128)S(1)}, f32[72,256]{1,0:T(8,128)S(1)}, u32[]{:S(2)}, u32[]{:S(2)}) %collective-permute-start.15) | collective-permute-done | bytes 73760 | tf_op jit(solution)/shard_map/ppermute | solution.py:548
  50.8 0.6 shard_map.118
  51.4 1.6 %collective-permute-start.17 = (f32[128,256]{1,0:T(8,128)S(1)}, f32[128,256]{1,0:T(8,128)S(1)}, u32[]{:S(2)}, u32[]{:S(2)}) collective-permute-start(f32[128,256]{1,0:T(8,128)S(1)} %get-tuple-element.93), channel_id=1, source_target_pairs={{0,28},{4,8},{8,4},{12,16},{16,12},{20,24},{24,20},{28,0},{1,29},{... | collective-permute-start | bytes 393224 | tf_op jit(solution)/shard_map/ppermute | solution.py:553
  53.1 3.0 %shard_map.119.refs_13_.refs_10_ = f32[216,256]{1,0:T(8,128)S(1)} custom-call(f32[24,256]{1,0:T(8,128)S(1)} %get-tuple-element.90.refs_0_.refs_5_, f32[72,256]{1,0:T(8,128)S(1)} %collective-permute-done.14.refs_5_.refs_1_.refs_9_, f32[72,256]{1,0:T(8,128)S(1)} %collective-permute-done.15.refs_6_.refs_2_.refs_10_, ...), custom_call_target="tpu_custom_call" | custom-call | flops 1811939328 | bytes 483328 | tf_op jit(solution)/shard_map/pallas_call | solution.py:520
  56.1 1.9 %collective-permute-done.17.refs_8_ = f32[128,256]{1,0:T(8,128)S(1)} collective-permute-done((f32[128,256]{1,0:T(8,128)S(1)}, f32[128,256]{1,0:T(8,128)S(1)}, u32[]{:S(2)}, u32[]{:S(2)}) %collective-permute-start.17) | collective-permute-done | bytes 131104 | tf_op jit(solution)/shard_map/ppermute | solution.py:553
  57.9 2.5 %shard_map.120 = (f32[3,128,256]{2,1,0:T(8,128)S(1)}, f32[120,256]{1,0:T(8,128)S(1)}, f32[120,256]{1,0:T(8,128)S(1)}, f32[24,256]{1,0:T(8,128)S(1)}, f32[24,256]{1,0:T(8,128)S(1)}) custom-call(f32[6,128,256]{2,1,0:T(8,128)S(1)} %get-tuple-element.89.refs_0_, f32[3,128,256]{2,1,0:T(8,128)S(1)} %get-tuple-element.83.refs_1_, ...), custom_call_target="tpu_custom_call" | custom-call | bytes 2875392 | tf_op jit(solution)/shard_map/pallas_call | solution.py:520
  60.5 0.9 %collective-permute-start.20 = (f32[120,256]{1,0:T(8,128)S(1)}, f32[120,256]{1,0:T(8,128)S(1)}, u32[]{:S(2)}, u32[]{:S(2)}) collective-permute-start(f32[120,256]{1,0:T(8,128)S(1)} %get-tuple-element.97), channel_id=1, source_target_pairs={{0,28},{4,8},{8,4},{12,16},{16,12},{20,24},{24,20},{28,0},{1,29},{... | collective-permute-start | bytes 368648 | tf_op jit(solution)/shard_map/ppermute | solution.py:553
  61.4 2.0 %collective-permute-start.21 = (f32[24,256]{1,0:T(8,128)S(1)}, f32[24,256]{1,0:T(8,128)S(1)}, u32[]{:S(2)}, u32[]{:S(2)}) collective-permute-start(f32[24,256]{1,0:T(8,128)S(1)} %get-tuple-element.98), channel_id=1, source_target_pairs={{0,1},{1,0},{2,3},{3,2},{4,5},{5,4},{6,7},{7,6},{8,9},{9,8},{10,11... | collective-permute-start | bytes 73736 | tf_op jit(solution)/shard_map/ppermute | solution.py:549
  63.5 2.4 %collective-permute-start.22 = (f32[24,256]{1,0:T(8,128)S(1)}, f32[24,256]{1,0:T(8,128)S(1)}, u32[]{:S(2)}, u32[]{:S(2)}) collective-permute-start(f32[24,256]{1,0:T(8,128)S(1)} %get-tuple-element.99), channel_id=1, source_target_pairs={{0,3},{1,2},{2,1},{3,0},{4,7},{5,6},{6,5},{7,4},{8,11},{9,10},{10,... | collective-permute-start | bytes 73736 | tf_op jit(solution)/shard_map/ppermute | solution.py:548
  65.9 3.2 %collective-permute-done.22.refs_6_ = f32[24,256]{1,0:T(8,128)S(1)} collective-permute-done((f32[24,256]{1,0:T(8,128)S(1)}, f32[24,256]{1,0:T(8,128)S(1)}, u32[]{:S(2)}, u32[]{:S(2)}) %collective-permute-start.22) | collective-permute-done | bytes 24608 | tf_op jit(solution)/shard_map/ppermute | solution.py:548
  69.1 1.4 %shard_map.121 = (f32[6,128,256]{2,1,0:T(8,128)}, f32[3,128,256]{2,1,0:T(8,128)}, f32[3,6144]{1,0:T(4,128)}) custom-call(f32[6,128,256]{2,1,0:T(8,128)S(1)} %get-tuple-element.89.refs_0_, f32[3,128,256]{2,1,0:T(8,128)S(1)} %get-tuple-element.95.refs_1_, s32[128,256]{1,0:T(8,128)S(1)} %get-tuple-element.65.refs_2_, ...), custom_call_target="tpu_custom_call" | custom-call | bytes 3276800 | tf_op jit(solution)/shard_map/pallas_call | solution.py:520
  (24 shorter events, 1.3 us)
Async XLA Ops:
  3.1 12.2 %collective-permute-start = (f32[120,256]{1,0:T(8,128)S(1)}, f32[120,256]{1,0:T(8,128)S(1)}, u32[]{:S(2)}, u32[]{:S(2)}) collective-permute-start(f32[120,256]{1,0:T(8,128)S(1)} %get-tuple-element.60), channel_id=1, source_target_pairs={{0,4},{4,0},{8,12},{12,8},{16,20},{20,16},{24,28},{28,24},{1,5},{5... | collective-permute-start | bytes 368648 | tf_op jit(solution)/shard_map/ppermute | solution.py:554
  3.7 11.6 %collective-permute-start.1 = (f32[120,256]{1,0:T(8,128)S(1)}, f32[120,256]{1,0:T(8,128)S(1)}, u32[]{:S(2)}, u32[]{:S(2)}) collective-permute-start(f32[120,256]{1,0:T(8,128)S(1)} %get-tuple-element.61), channel_id=1, source_target_pairs={{0,28},{4,8},{8,4},{12,16},{16,12},{20,24},{24,20},{28,0},{1,29},{... | collective-permute-start | bytes 368648 | tf_op jit(solution)/shard_map/ppermute | solution.py:553
  7.2 4.5 %collective-permute-start.2 = (f32[88,256]{1,0:T(8,128)S(1)}, f32[88,256]{1,0:T(8,128)S(1)}, u32[]{:S(2)}, u32[]{:S(2)}) collective-permute-start(f32[88,256]{1,0:T(8,128)S(1)} %get-tuple-element.62), channel_id=1, source_target_pairs={{0,1},{1,0},{2,3},{3,2},{4,5},{5,4},{6,7},{7,6},{8,9},{9,8},{10,11... | collective-permute-start | bytes 270344 | tf_op jit(solution)/shard_map/ppermute | solution.py:549
  8.8 6.5 %collective-permute-start.3 = (f32[88,256]{1,0:T(8,128)S(1)}, f32[88,256]{1,0:T(8,128)S(1)}, u32[]{:S(2)}, u32[]{:S(2)}) collective-permute-start(f32[88,256]{1,0:T(8,128)S(1)} %get-tuple-element.63), channel_id=1, source_target_pairs={{0,3},{1,2},{2,1},{3,0},{4,7},{5,6},{6,5},{7,4},{8,11},{9,10},{10,... | collective-permute-start | bytes 270344 | tf_op jit(solution)/shard_map/ppermute | solution.py:548
  11.3 7.9 %collective-permute-start.4 = (f32[32,256]{1,0:T(8,128)S(1)}, f32[32,256]{1,0:T(8,128)S(1)}, u32[]{:S(2)}, u32[]{:S(2)}) collective-permute-start(f32[32,256]{1,0:T(8,128)S(1)} %get-tuple-element.58.refs_5_.refs_0_), channel_id=1, source_target_pairs={{0,2},{1,3},{2,0},{3,1},{4,6},{5,7},{6,4},{7,5},{8,10},{9,11},{10,... | collective-permute-start | bytes 98312 | tf_op jit(solution)/shard_map/ppermute | solution.py:561
  22.2 9.5 %collective-permute-start.5 = (f32[144,256]{1,0:T(8,128)S(1)}, f32[144,256]{1,0:T(8,128)S(1)}, u32[]{:S(2)}, u32[]{:S(2)}) collective-permute-start(f32[144,256]{1,0:T(8,128)S(1)} %get-tuple-element.68), channel_id=1, source_target_pairs={{0,4},{4,0},{8,12},{12,8},{16,20},{20,16},{24,28},{28,24},{1,5},{5... | collective-permute-start | bytes 442376 | tf_op jit(solution)/shard_map/ppermute | solution.py:554
  22.3 9.4 %collective-permute-start.6 = (f32[144,256]{1,0:T(8,128)S(1)}, f32[144,256]{1,0:T(8,128)S(1)}, u32[]{:S(2)}, u32[]{:S(2)}) collective-permute-start(f32[144,256]{1,0:T(8,128)S(1)} %get-tuple-element.69), channel_id=1, source_target_pairs={{0,28},{4,8},{8,4},{12,16},{16,12},{20,24},{24,20},{28,0},{1,29},{... | collective-permute-start | bytes 442376 | tf_op jit(solution)/shard_map/ppermute | solution.py:553
  23.8 4.4 %collective-permute-start.7 = (f32[72,256]{1,0:T(8,128)S(1)}, f32[72,256]{1,0:T(8,128)S(1)}, u32[]{:S(2)}, u32[]{:S(2)}) collective-permute-start(f32[72,256]{1,0:T(8,128)S(1)} %get-tuple-element.70), channel_id=1, source_target_pairs={{0,1},{1,0},{2,3},{3,2},{4,5},{5,4},{6,7},{7,6},{8,9},{9,8},{10,11... | collective-permute-start | bytes 221192 | tf_op jit(solution)/shard_map/ppermute | solution.py:549
  25.0 6.7 %collective-permute-start.8 = (f32[72,256]{1,0:T(8,128)S(1)}, f32[72,256]{1,0:T(8,128)S(1)}, u32[]{:S(2)}, u32[]{:S(2)}) collective-permute-start(f32[72,256]{1,0:T(8,128)S(1)} %get-tuple-element.71), channel_id=1, source_target_pairs={{0,3},{1,2},{2,1},{3,0},{4,7},{5,6},{6,5},{7,4},{8,11},{9,10},{10,... | collective-permute-start | bytes 221192 | tf_op jit(solution)/shard_map/ppermute | solution.py:548
  27.7 6.5 %collective-permute-start.11 = (f32[24,256]{1,0:T(8,128)S(1)}, f32[24,256]{1,0:T(8,128)S(1)}, u32[]{:S(2)}, u32[]{:S(2)}) collective-permute-start(f32[24,256]{1,0:T(8,128)S(1)} %get-tuple-element.76.refs_0_.refs_5_), channel_id=1, source_target_pairs={{0,2},{1,3},{2,0},{3,1},{4,6},{5,7},{6,4},{7,5},{8,10},{9,11},{10,... | collective-permute-start | bytes 73736 | tf_op jit(solution)/shard_map/ppermute | solution.py:561
  32.3 4.8 %collective-permute-start.9 = (f32[128,256]{1,0:T(8,128)S(1)}, f32[128,256]{1,0:T(8,128)S(1)}, u32[]{:S(2)}, u32[]{:S(2)}) collective-permute-start(f32[128,256]{1,0:T(8,128)S(1)} %get-tuple-element.78), channel_id=1, source_target_pairs={{0,4},{4,0},{8,12},{12,8},{16,20},{20,16},{24,28},{28,24},{1,5},{5... | collective-permute-start | bytes 393224 | tf_op jit(solution)/shard_map/ppermute | solution.py:554
  32.4 6.7 %collective-permute-start.10 = (f32[128,256]{1,0:T(8,128)S(1)}, f32[128,256]{1,0:T(8,128)S(1)}, u32[]{:S(2)}, u32[]{:S(2)}) collective-permute-start(f32[128,256]{1,0:T(8,128)S(1)} %get-tuple-element.79), channel_id=1, source_target_pairs={{0,28},{4,8},{8,4},{12,16},{16,12},{20,24},{24,20},{28,0},{1,29},{... | collective-permute-start | bytes 393224 | tf_op jit(solution)/shard_map/ppermute | solution.py:553
  43.2 7.6 %collective-permute-start.12 = (f32[120,256]{1,0:T(8,128)S(1)}, f32[120,256]{1,0:T(8,128)S(1)}, u32[]{:S(2)}, u32[]{:S(2)}) collective-permute-start(f32[120,256]{1,0:T(8,128)S(1)} %get-tuple-element.84), channel_id=1, source_target_pairs={{0,4},{4,0},{8,12},{12,8},{16,20},{20,16},{24,28},{28,24},{1,5},{5... | collective-permute-start | bytes 368648 | tf_op jit(solution)/shard_map/ppermute | solution.py:554
  43.3 7.5 %collective-permute-start.13 = (f32[120,256]{1,0:T(8,128)S(1)}, f32[120,256]{1,0:T(8,128)S(1)}, u32[]{:S(2)}, u32[]{:S(2)}) collective-permute-start(f32[120,256]{1,0:T(8,128)S(1)} %get-tuple-element.85), channel_id=1, source_target_pairs={{0,28},{4,8},{8,4},{12,16},{16,12},{20,24},{24,20},{28,0},{1,29},{... | collective-permute-start | bytes 368648 | tf_op jit(solution)/shard_map/ppermute | solution.py:553
  44.3 4.5 %collective-permute-start.14 = (f32[72,256]{1,0:T(8,128)S(1)}, f32[72,256]{1,0:T(8,128)S(1)}, u32[]{:S(2)}, u32[]{:S(2)}) collective-permute-start(f32[72,256]{1,0:T(8,128)S(1)} %get-tuple-element.86), channel_id=1, source_target_pairs={{0,1},{1,0},{2,3},{3,2},{4,5},{5,4},{6,7},{7,6},{8,9},{9,8},{10,11... | collective-permute-start | bytes 221192 | tf_op jit(solution)/shard_map/ppermute | solution.py:549
  44.3 6.5 %collective-permute-start.15 = (f32[72,256]{1,0:T(8,128)S(1)}, f32[72,256]{1,0:T(8,128)S(1)}, u32[]{:S(2)}, u32[]{:S(2)}) collective-permute-start(f32[72,256]{1,0:T(8,128)S(1)} %get-tuple-element.87), channel_id=1, source_target_pairs={{0,3},{1,2},{2,1},{3,0},{4,7},{5,6},{6,5},{7,4},{8,11},{9,10},{10,... | collective-permute-start | bytes 221192 | tf_op jit(solution)/shard_map/ppermute | solution.py:548
  46.5 6.6 %collective-permute-start.18 = (f32[24,256]{1,0:T(8,128)S(1)}, f32[24,256]{1,0:T(8,128)S(1)}, u32[]{:S(2)}, u32[]{:S(2)}) collective-permute-start(f32[24,256]{1,0:T(8,128)S(1)} %get-tuple-element.90.refs_0_.refs_5_), channel_id=1, source_target_pairs={{0,2},{1,3},{2,0},{3,1},{4,6},{5,7},{6,4},{7,5},{8,10},{9,11},{10,... | collective-permute-start | bytes 73736 | tf_op jit(solution)/shard_map/ppermute | solution.py:561
  51.4 4.7 %collective-permute-start.16 = (f32[128,256]{1,0:T(8,128)S(1)}, f32[128,256]{1,0:T(8,128)S(1)}, u32[]{:S(2)}, u32[]{:S(2)}) collective-permute-start(f32[128,256]{1,0:T(8,128)S(1)} %get-tuple-element.92), channel_id=1, source_target_pairs={{0,4},{4,0},{8,12},{12,8},{16,20},{20,16},{24,28},{28,24},{1,5},{5... | collective-permute-start | bytes 393224 | tf_op jit(solution)/shard_map/ppermute | solution.py:554
  51.4 6.5 %collective-permute-start.17 = (f32[128,256]{1,0:T(8,128)S(1)}, f32[128,256]{1,0:T(8,128)S(1)}, u32[]{:S(2)}, u32[]{:S(2)}) collective-permute-start(f32[128,256]{1,0:T(8,128)S(1)} %get-tuple-element.93), channel_id=1, source_target_pairs={{0,28},{4,8},{8,4},{12,16},{16,12},{20,24},{24,20},{28,0},{1,29},{... | collective-permute-start | bytes 393224 | tf_op jit(solution)/shard_map/ppermute | solution.py:553
  60.4 8.7 %collective-permute-start.19 = (f32[120,256]{1,0:T(8,128)S(1)}, f32[120,256]{1,0:T(8,128)S(1)}, u32[]{:S(2)}, u32[]{:S(2)}) collective-permute-start(f32[120,256]{1,0:T(8,128)S(1)} %get-tuple-element.96), channel_id=1, source_target_pairs={{0,4},{4,0},{8,12},{12,8},{16,20},{20,16},{24,28},{28,24},{1,5},{5... | collective-permute-start | bytes 368648 | tf_op jit(solution)/shard_map/ppermute | solution.py:554
  60.5 8.6 %collective-permute-start.20 = (f32[120,256]{1,0:T(8,128)S(1)}, f32[120,256]{1,0:T(8,128)S(1)}, u32[]{:S(2)}, u32[]{:S(2)}) collective-permute-start(f32[120,256]{1,0:T(8,128)S(1)} %get-tuple-element.97), channel_id=1, source_target_pairs={{0,28},{4,8},{8,4},{12,16},{16,12},{20,24},{24,20},{28,0},{1,29},{... | collective-permute-start | bytes 368648 | tf_op jit(solution)/shard_map/ppermute | solution.py:553
  61.4 4.5 %collective-permute-start.21 = (f32[24,256]{1,0:T(8,128)S(1)}, f32[24,256]{1,0:T(8,128)S(1)}, u32[]{:S(2)}, u32[]{:S(2)}) collective-permute-start(f32[24,256]{1,0:T(8,128)S(1)} %get-tuple-element.98), channel_id=1, source_target_pairs={{0,1},{1,0},{2,3},{3,2},{4,5},{5,4},{6,7},{7,6},{8,9},{9,8},{10,11... | collective-permute-start | bytes 73736 | tf_op jit(solution)/shard_map/ppermute | solution.py:549
  63.5 5.6 %collective-permute-start.22 = (f32[24,256]{1,0:T(8,128)S(1)}, f32[24,256]{1,0:T(8,128)S(1)}, u32[]{:S(2)}, u32[]{:S(2)}) collective-permute-start(f32[24,256]{1,0:T(8,128)S(1)} %get-tuple-element.99), channel_id=1, source_target_pairs={{0,3},{1,2},{2,1},{3,0},{4,7},{5,6},{6,5},{7,4},{8,11},{9,10},{10,... | collective-permute-start | bytes 73736 | tf_op jit(solution)/shard_map/ppermute | solution.py:548
